TPU v7x, 32 devices: a whole 2x2x4 slice. The times are simulated.
32 devices in a mesh: dp: 8 (over y, x, core), tensor: 4 (over z).
Axes of the slice: x: 2, y: 2, z: 4, core: 2. Of those that a mesh axis runs over, the one named last changes fastest.
Arguments:
- tokens: bfloat16 [3072, 8192], P('dp', 'tensor'), may hold values from -6 to 6
- up_first: bfloat16 [16, 512, 512], P('tensor'), may hold values from -0.25 to 0.25
- up_second: bfloat16 [16, 512, 2048], P('tensor'), may hold values from -0.25 to 0.25
- down_first: bfloat16 [16, 2048, 512], P('tensor'), may hold values from -0.125 to 0.125
- down_second: bfloat16 [16, 512, 512], P('tensor'), may hold values from -0.25 to 0.25
- cotangent: bfloat16 [3072, 8192], P('dp', 'tensor'), may hold values from -6 to 6
Outputs:
- layer_out: bfloat16 [3072, 8192], P('dp', 'tensor')
- grad_tokens: bfloat16 [3072, 8192], P('dp', 'tensor')
- grad_up_first: float32 [16, 512, 512], P('tensor', 'dp')
- grad_up_second: float32 [16, 512, 2048], P('tensor', 'dp')
- grad_down_first: float32 [16, 2048, 512], P('tensor', 'dp')
- grad_down_second: float32 [16, 512, 512], P('tensor', 'dp')
All inputs are finite; a program needn't handle non-finite values.
Results may differ from a plain program's by a relative error of at most 0.023.
Values may be sent and summed in bfloat16 or wider, within the bound.
No kernel may reach another device: no remote copies, remote signals or barrier semaphores. Data moves between devices by JAX's collectives and lax.ppermute only.
A program may use at most 128 MiB of HBM per device.

v0:
```python
import jax
import jax.numpy as jnp
from jax import lax
from jax.sharding import PartitionSpec as P

NB = 16


gelu_coeff = 0.7978845608028654
cubic_coeff = 0.044715


def gelu_pair(hidden):
    inner_arg = gelu_coeff * (hidden + cubic_coeff * hidden * hidden * hidden)
    tangent = jnp.tanh(inner_arg)
    gelu_value = 0.5 * hidden * (1.0 + tangent)
    gelu_slope = 0.5 * (1.0 + tangent) + 0.5 * hidden * (1.0 - tangent * tangent) * gelu_coeff * (
        1.0 + 3.0 * cubic_coeff * hidden * hidden
    )
    return (gelu_value, gelu_slope)


def regroup(sliced, apply_fn):
    return apply_fn(lax.all_to_all(sliced, "tensor", split_axis=2, concat_axis=0, tiled=True))


def body(tokens, up_first, up_second, down_first, down_second, cotangent):
    token_rows = tokens.shape[0]
    local_blocks = up_first.shape[0]
    block_size = up_first.shape[1]
    hidden_size = up_second.shape[2]
    slice_width = block_size // NB
    data_count = lax.axis_size("dp")
    grad_scale = (token_rows * data_count) ** (-0.5)
    x_three = tokens.reshape(token_rows, local_blocks, block_size)
    up_four = up_first.reshape(local_blocks, block_size, NB, slice_width)
    mixed_up = jnp.einsum(
        "tbi,bijc->bcjt", x_three, up_four, preferred_element_type=jnp.float32
    ).astype(jnp.bfloat16)

    def lift_up(received):
        regrouped = received.reshape(block_size, local_blocks, received.shape[3])
        return (
            regrouped,
            jnp.einsum("mjt,jmo->jot", regrouped, up_second, preferred_element_type=jnp.float32),
        )

    regrouped_up, pre_act = regroup(mixed_up, lift_up)
    gelu_value, gelu_slope = gelu_pair(pre_act)
    activated = gelu_value.astype(jnp.bfloat16)
    down_four = down_first.reshape(local_blocks, hidden_size, NB, slice_width)
    mixed_down = jnp.einsum(
        "jmt,jmkc->jckt", activated, down_four, preferred_element_type=jnp.float32
    ).astype(jnp.bfloat16)

    def settle(received):
        regrouped = received.reshape(block_size, local_blocks, received.shape[3])
        return (
            regrouped,
            jnp.einsum("mkt,kmo->kot", regrouped, down_second, preferred_element_type=jnp.float32),
        )

    regrouped_down, branch = regroup(mixed_down, settle)
    branch_rows = branch.transpose(2, 0, 1).reshape(token_rows, local_blocks * block_size)
    layer_out = (tokens.astype(jnp.float32) + branch_rows).astype(jnp.bfloat16)
    grad_three = cotangent.reshape(token_rows, local_blocks, block_size)
    last_four = down_second.reshape(local_blocks, NB, slice_width, block_size)
    back_down = jnp.einsum(
        "tko,kjco->kcjt", grad_three, last_four, preferred_element_type=jnp.float32
    ).astype(jnp.bfloat16)

    def descend(received):
        regrouped = received.reshape(block_size, local_blocks, received.shape[3])
        return (
            regrouped,
            jnp.einsum("ojt,jmo->jmt", regrouped, down_first, preferred_element_type=jnp.float32),
        )

    grad_mid, grad_act = regroup(back_down, descend)
    grad_pre = (grad_act * gelu_slope).astype(jnp.bfloat16)
    term_fourth = grad_scale * jnp.einsum(
        "mkt,tko->mko", regrouped_down, grad_three, preferred_element_type=jnp.float32
    )
    term_third = grad_scale * jnp.einsum(
        "jmt,ojt->mjo", activated, grad_mid, preferred_element_type=jnp.float32
    )
    up_back = up_second.reshape(local_blocks, NB, slice_width, hidden_size)
    back_up = jnp.einsum(
        "jot,jbco->jcbt", grad_pre, up_back, preferred_element_type=jnp.float32
    ).astype(jnp.bfloat16)

    def arrive(received):
        regrouped = received.reshape(block_size, local_blocks, received.shape[3])
        return (
            regrouped,
            jnp.einsum("obt,bio->bit", regrouped, up_first, preferred_element_type=jnp.float32),
        )

    grad_in, back_branch = regroup(back_up, arrive)
    back_rows = back_branch.transpose(2, 0, 1).reshape(token_rows, local_blocks * block_size)
    grad_tokens = (cotangent.astype(jnp.float32) + back_rows).astype(jnp.bfloat16)
    term_second = grad_scale * jnp.einsum(
        "mjt,jot->mjo", regrouped_up, grad_pre, preferred_element_type=jnp.float32
    )
    term_first = grad_scale * jnp.einsum(
        "tbi,obt->ibo", x_three, grad_in, preferred_element_type=jnp.float32
    )
    sum_first, sum_second, sum_third, sum_fourth = (
        lax.psum_scatter(
            term_first.astype(jnp.bfloat16), "dp", scatter_dimension=0, tiled=True
        ).astype(jnp.float32),
        lax.psum_scatter(
            term_second.astype(jnp.bfloat16), "dp", scatter_dimension=0, tiled=True
        ).astype(jnp.float32),
        lax.psum_scatter(
            term_third.astype(jnp.bfloat16), "dp", scatter_dimension=0, tiled=True
        ).astype(jnp.float32),
        lax.psum_scatter(
            term_fourth.astype(jnp.bfloat16), "dp", scatter_dimension=0, tiled=True
        ).astype(jnp.float32),
    )
    grad_up_first = sum_first.transpose(1, 0, 2)
    grad_up_second = sum_second.transpose(1, 0, 2)
    grad_down_first = sum_third.transpose(1, 0, 2)
    grad_down_second = sum_fourth.transpose(1, 0, 2)
    return (
        layer_out,
        grad_tokens,
        grad_up_first,
        grad_up_second,
        grad_down_first,
        grad_down_second,
    )


def solution(mesh):
    in_specs = (
        P("dp", "tensor"),
        P("tensor", None, None),
        P("tensor", None, None),
        P("tensor", None, None),
        P("tensor", None, None),
        P("dp", "tensor"),
    )
    out_specs = (
        P("dp", "tensor"),
        P("dp", "tensor"),
        P("tensor", "dp", None),
        P("tensor", "dp", None),
        P("tensor", "dp", None),
        P("tensor", "dp", None),
    )
    return jax.shard_map(body, mesh=mesh, in_specs=in_specs, out_specs=out_specs, check_vma=False)
```

profile of v0, /device:TPU:0, one launch (start us, length us, event | category | flops | bytes accessed | tf_op | source)
XLA Modules:
  0.0 466.1 jit_solution(12066908594046687807)
XLA Ops:
  7.2 4.0 reshape.59
  15.3 6.3 %all-to-all-start.2 = ((bf16[4,32,16,384]{3,1,0,2:T(8,128)(2,1)}), bf16[4,32,16,384]{3,1,0,2:T(8,128)(2,1)}, u32[]{:S(2)}, u32[]{:S(2)}) async-start(bf16[4,32,16,384]{3,1,0,2:T(8,128)(2,1)} %copy.105), calls=%async_computation.2 | async-start | bytes 3145728 | tf_op jit(solution)/shard_map/all_to_all | solution.py:24
  21.6 3.8 reshape.53
  25.4 4.1 copy.90
  29.6 3.3 fusion.27
  34.3 24.4 %all-to-all-done.2 = bf16[4,32,16,384]{3,1,0,2:T(8,128)(2,1)} async-done(((bf16[4,32,16,384]{3,1,0,2:T(8,128)(2,1)}), bf16[4,32,16,384]{3,1,0,2:T(8,128)(2,1)}, u32[]{:S(2)}, u32[]{:S(2)}) %all-to-all-start.2) | async-done | bytes 1572896 | tf_op jit(solution)/shard_map/all_to_all | solution.py:24
  58.7 4.4 all-to-all-start
  63.0 2.8 copy.107
  65.8 33.7 %all-to-all-done = bf16[4,32,16,384]{3,1,0,2:T(8,128)(2,1)} async-done(((bf16[4,32,16,384]{3,1,0,2:T(8,128)(2,1)}), bf16[4,32,16,384]{3,1,0,2:T(8,128)(2,1)}, u32[]{:S(2)}, u32[]{:S(2)}) %all-to-all-start) | async-done | bytes 1572896 | tf_op jit(solution)/shard_map/all_to_all | solution.py:24
  102.3 6.0 %fusion.34 = f32[4,384,2048]{2,1,0:T(8,128)S(1)} fusion(bf16[512,4,384]{2,0,1:T(8,128)(2,1)S(1)} %bitcast.120, bf16[4,512,2048]{2,1,0:T(8,128)(2,1)} %param.8), kind=kOutput, calls=%fused_computation.45 | convolution fusion | flops 3221225472 | bytes 22544384 | tf_op jit(solution)/shard_map/mjt,jmo->jot/dot_general | solution.py:45
  108.3 11.5 %fusion.33 = f32[4,384,512]{1,2,0:S(1)} fusion(bf16[4,2048,512]{2,1,0:T(8,128)(2,1)} %param.9, f32[4,384,2048]{2,1,0:T(8,128)S(1)} %fusion.34), kind=kOutput, calls=%fused_computation.44 | convolution fusion | flops 3249537024 | bytes 24117248
  121.4 4.3 all-to-all-start.1
  126.0 16.0 %fusion.6 = bf16[4,2048,384]{1,2,0:T(8,128)(2,1)} fusion(f32[4,384,2048]{2,1,0:T(8,128)} %copy-done.1, bf16[512,4,384]{2,0,1:T(8,128)(2,1)} %bitcast.124, bf16[4,2048,512]{2,1,0:T(8,128)(2,1)} %param.9), kind=kOutput, calls=%fused_computation.10 | convolution fusion | flops 3280994304 | bytes 28835840 | tf_op jit(solution)/shard_map/ojt,jmo->jmt/dot_general | solution.py:76
  142.0 20.3 %all-to-all-done.1 = bf16[4,32,16,384]{3,1,0,2:T(8,128)(2,1)} async-done(((bf16[4,32,16,384]{3,1,0,2:T(8,128)(2,1)}), bf16[4,32,16,384]{3,1,0,2:T(8,128)(2,1)}, u32[]{:S(2)}, u32[]{:S(2)}) %all-to-all-start.1) | async-done | bytes 1572896 | tf_op jit(solution)/shard_map/all_to_all | solution.py:24
  167.7 9.9 %fusion.24 = bf16[4,32,16,384]{3,1,2,0:T(8,128)(2,1)S(1)} fusion(bf16[4,16,32,2048]{3,2,1,0:T(8,128)(2,1)} %bitcast.113, bf16[4,2048,384]{1,2,0:T(8,128)(2,1)} %fusion.6), kind=kOutput, calls=%fused_computation.39 | convolution fusion | flops 3222011904 | bytes 16252928 | tf_op jit(solution)/shard_map/jot,jbco->jcbt/dot_general | solution.py:88
  179.0 4.4 all-to-all-start.3
  183.6 11.6 %fusion.7 = bf16[512,4,2048]{0,2,1:T(8,128)(2,1)} fusion(bf16[4,2048,384]{1,2,0:T(8,128)(2,1)} %fusion.6, bf16[512,4,384]{2,0,1:T(8,128)(2,1)} %bitcast.121), kind=kOutput, calls=%fused_computation.13 | convolution fusion | flops 3229614080 | bytes 16252928 | tf_op jit(solution)/shard_map/mjt,jot->mjo/dot_general | solution.py:102
  195.2 14.9 %copy.118 = bf16[512,4,2048]{2,1,0:T(4,128)(2,1)} copy(bf16[512,4,2048]{0,2,1:T(8,128)(2,1)} %fusion.7) | data formatting | bytes 16777216 | tf_op jit(solution)/shard_map/convert_element_type | solution.py:113
  210.1 9.6 %all-to-all-done.3 = bf16[4,32,16,384]{3,1,0,2:T(8,128)(2,1)} async-done(((bf16[4,32,16,384]{3,1,0,2:T(8,128)(2,1)}), bf16[4,32,16,384]{3,1,0,2:T(8,128)(2,1)}, u32[]{:S(2)}, u32[]{:S(2)}) %all-to-all-start.3) | async-done | bytes 1572896 | tf_op jit(solution)/shard_map/all_to_all | solution.py:24
  225.2 4.5 copy.116
  230.0 11.0 %fusion.8 = bf16[2048,4,512]{0,2,1:T(8,128)(2,1)} fusion(bf16[512,4,384]{2,0,1:T(8,128)(2,1)} %bitcast.125, f32[4,384,2048]{2,1,0:T(8,128)} %copy-done.1), kind=kOutput, calls=%fused_computation.14 | convolution fusion | flops 3257925632 | bytes 22544384 | tf_op jit(solution)/shard_map/jmt,ojt->mjo/dot_general | solution.py:84
  247.4 4.1 convolution_bitcast_fusion.1
  251.5 3.6 copy.102
  255.1 4.1 fusion.12
  259.3 2.7 copy.121
  262.0 4.9 %convolution_bitcast_fusion = f32[384,4,512]{2,0,1:T(8,128)} fusion(bf16[512,4,384]{2,0,1:T(8,128)(2,1)} %bitcast.119, bf16[4,512,512]{2,1,0:T(8,128)(2,1)} %param.7), kind=kOutput, calls=%fused_computation.25 | convolution fusion | flops 805306368 | bytes 6815744 | tf_op jit(solution)/shard_map/obt,bio->bit/dot_general | solution.py:96
  266.9 3.6 copy.114
  270.5 3.9 fusion.11
  278.9 99.8 %all-reduce.5.cloned.1.call-done = (bf16[512,4,512]{2,1,0:T(4,128)(2,1)}, bf16[512,4,2048]{2,1,0:T(4,128)(2,1)}) async-done(((bf16[512,4,512]{2,1,0:T(4,128)(2,1)}, bf16[512,4,2048]{2,1,0:T(4,128)(2,1)}), (bf16[512,4,512]{2,1,0:T(4,128)(2,1)}, bf16[512,4,2048]{2,1,0:T(4,128)(2,1)})) %all-reduce.5.cloned.1.call-update) | async-done | bytes 10485776
  384.6 69.0 %reduce-scatter.3.cloned.1.call-done = bf16[256,4,512]{0,2,1:T(8,128)(2,1)} async-done(((bf16[2048,4,512]{0,2,1:T(8,128)(2,1)}), bf16[256,4,512]{0,2,1:T(8,128)(2,1)}) %reduce-scatter.3.cloned.1.call-update) | async-done | bytes 1048592 | tf_op jit(solution)/shard_map/reduce_scatter | solution.py:115
  453.6 2.7 convert_bitcast_fusion
  456.3 2.9 copy.125
  (43 shorter events, 39.0 us)
Async XLA Ops:
  7.2 4.0 copy-start
  15.3 43.4 %all-to-all-start.2 = ((bf16[4,32,16,384]{3,1,0,2:T(8,128)(2,1)}), bf16[4,32,16,384]{3,1,0,2:T(8,128)(2,1)}, u32[]{:S(2)}, u32[]{:S(2)}) async-start(bf16[4,32,16,384]{3,1,0,2:T(8,128)(2,1)} %copy.105), calls=%async_computation.2 | async-start | bytes 3145728 | tf_op jit(solution)/shard_map/all_to_all | solution.py:24
  58.7 40.9 %all-to-all-start = ((bf16[4,32,16,384]{3,1,0,2:T(8,128)(2,1)}), bf16[4,32,16,384]{3,1,0,2:T(8,128)(2,1)}, u32[]{:S(2)}, u32[]{:S(2)}) async-start(bf16[4,32,16,384]{3,1,0,2:T(8,128)(2,1)} %copy.92), calls=%async_computation | async-start | bytes 3145728 | tf_op jit(solution)/shard_map/all_to_all | solution.py:24
  101.2 1.1 copy-start.6
  108.3 11.5 %copy-start.1 = (f32[4,384,2048]{2,1,0:T(8,128)}, f32[4,384,2048]{2,1,0:T(8,128)S(1)}, u32[]{:S(2)}) copy-start(f32[4,384,2048]{2,1,0:T(8,128)S(1)} %fusion.34) | copy-start | bytes 37748740
  121.4 40.9 %all-to-all-start.1 = ((bf16[4,32,16,384]{3,1,0,2:T(8,128)(2,1)}), bf16[4,32,16,384]{3,1,0,2:T(8,128)(2,1)}, u32[]{:S(2)}, u32[]{:S(2)}) async-start(bf16[4,32,16,384]{3,1,0,2:T(8,128)(2,1)} %copy.98), calls=%async_computation.1 | async-start | bytes 3145728 | tf_op jit(solution)/shard_map/all_to_all | solution.py:24
  125.8 151.3 %reduce-scatter.5.cloned.1.call-start = ((), (), s32[]{:S(2)}) async-start(), calls=%async_computation.7 | async-start | bytes 2359296 | tf_op jit(solution)/shard_map/reduce_scatter | solution.py:118
  162.3 2.8 copy-start.3
  164.0 1.1 copy-start.4
  179.0 40.7 %all-to-all-start.3 = ((bf16[4,32,16,384]{3,1,0,2:T(8,128)(2,1)}), bf16[4,32,16,384]{3,1,0,2:T(8,128)(2,1)}, u32[]{:S(2)}, u32[]{:S(2)}) async-start(bf16[4,32,16,384]{3,1,0,2:T(8,128)(2,1)} %copy.110), calls=%async_computation.3 | async-start | bytes 3145728 | tf_op jit(solution)/shard_map/all_to_all | solution.py:24
  183.4 195.3 %all-reduce.5.cloned.1.call-start = ((), (), s32[]{:S(2)}) async-start(), calls=%async_computation.8 | async-start | bytes 20971520
  219.7 2.9 copy-start.2
  221.4 1.2 copy-start.5
  229.7 223.9 %reduce-scatter.3.cloned.1.call-start = ((), (), s32[]{:S(2)}) async-start(), calls=%async_computation.6 | async-start | bytes 9437184 | tf_op jit(solution)/shard_map/reduce_scatter | solution.py:115
  241.0 5.2 %copy-start.7 = (u32[32]{0:T(128)S(1)}, u32[32]{0:T(128)}, u32[]{:S(2)}) copy-start(u32[32]{0:T(128)} %constant.16) | copy-start | bytes 388
Sparse Core Ops, SparseCore 0:
  167.8 40.3 reduce-scatter.4
  229.8 148.8 all-reduce.4
  382.1 71.3 reduce-scatter.2
where the time goes:
time: 475 us; the launch traced here: 466 us
  waiting for transfers between devices  257 us (54%)
  matrix products  86 us (18%)
  local copies, waits for them, and re-layouts  72.9 us (15%)
  starting transfers between devices  20.1 us (4%)
  other arithmetic  15.2 us (3%)
  between operations  15 us (3%)
    unnamed x4, waiting for transfers between devices  99.8 us
    all_to_all x4, waiting for transfers between devices, regroup(): lax.all_to_all(sliced, 'tensor', split_axis=2, concat_axis=0, tiled=True)  88 us
    reduce_scatter x1, waiting for transfers between devices, body(): lax.psum_scatter(term_third.astype(jnp.bfloat16), 'dp', scatter_dimension...  69 us
    unnamed x25, local copies, waits for them, and re-layouts  25.1 us
    all_to_all x4, starting transfers between devices, regroup(): lax.all_to_all(sliced, 'tensor', split_axis=2, concat_axis=0, tiled=True)  19.4 us
    dot_general x1, matrix products, descend(): jnp.einsum('ojt,jmo->jmt', regrouped, down_first, preferred_element_type=...  16 us
    convert_element_type x1, local copies, waits for them, and re-layouts, body(): term_second.astype(jnp.bfloat16)  14.9 us
    dot_general x1, matrix products, body(): jnp.einsum('mjt,jot->mjo', regrouped_up, grad_pre, preferred_element_type...  11.6 us
  transfers between devices with their start and end apart: 7, of which 6 were waited for; matrix products, arithmetic and copies ran while one was open for 28% of the time, Pallas kernels for 0%

commit v1 on v0

v1 whole, which is shorter than its diff:
```python
import functools

import jax
import jax.numpy as jnp
from jax import lax
from jax.experimental import pallas as pl
from jax.experimental.pallas import tpu as pltpu
from jax.sharding import PartitionSpec as P

NB = 16
N_CHUNK = 2

gelu_coeff = 0.7978845608028654
cubic_coeff = 0.044715

BF16 = jnp.bfloat16
F32 = jnp.float32


def gelu_pair(hidden):
    inner_arg = gelu_coeff * (hidden + cubic_coeff * hidden * hidden * hidden)
    tangent = jnp.tanh(inner_arg)
    gelu_value = 0.5 * hidden * (1.0 + tangent)
    gelu_slope = 0.5 * (1.0 + tangent) + 0.5 * hidden * (1.0 - tangent * tangent) * gelu_coeff * (
        1.0 + 3.0 * cubic_coeff * hidden * hidden
    )
    return gelu_value, gelu_slope


def dot(a, b, ca, cb):
    return lax.dot_general(a, b, (((ca,), (cb,)), ((), ())), preferred_element_type=F32)


def params():
    return pltpu.CompilerParams(vmem_limit_bytes=52 * 1024 * 1024)


def spec(block, index_map):
    return pl.BlockSpec(block, index_map)


def enter(where, tokens, up_first, cotangent, down_second, sizes):
    T, L, BS, NT, G, SW, Q, _ = sizes
    rows = BS // (2 * Q)

    def kernel(where_ref, x_ref, w_ref, g_ref, d_ref, xt_ref, *rest):
        outs, (up_scr, back_scr) = rest[:-2], rest[-2:]
        turned = x_ref[...].T
        xt_ref[0] = turned.reshape(Q, 2, rows, T)
        up_scr[...] = dot(w_ref[0], turned, 0, 0).astype(BF16).reshape(NT, L, SW, T)
        back_scr[...] = dot(d_ref[0], g_ref[...], 1, 1).astype(BF16).reshape(NT, L, SW, T)
        for shift in range(NT):
            target = lax.rem(where_ref[0] + shift, NT)
            for chunk in range(N_CHUNK):
                out = outs[chunk * NT + shift]
                out[0, :, 0] = up_scr[target, chunk * G : (chunk + 1) * G]
                out[1, :, 0] = back_scr[target, chunk * G : (chunk + 1) * G]

    cols = spec((T, BS), lambda b, s: (0, b))
    square = spec((1, BS, BS), lambda b, s: (b, 0, 0))
    piece = jax.ShapeDtypeStruct((2, G, L, SW, T), BF16)
    outs = pl.pallas_call(
        kernel,
        name="enter",
        grid_spec=pltpu.PrefetchScalarGridSpec(
            num_scalar_prefetch=1,
            grid=(L,),
            in_specs=[cols, square, cols, square],
            out_specs=[spec((1, Q, 2, rows, T), lambda b, s: (b, 0, 0, 0, 0))]
            + [spec((2, G, 1, SW, T), lambda b, s: (0, 0, b, 0, 0))] * (N_CHUNK * NT),
            scratch_shapes=[pltpu.VMEM((NT, L, SW, T), BF16)] * 2,
        ),
        out_shape=[jax.ShapeDtypeStruct((L, Q, 2, rows, T), BF16)] + [piece] * (N_CHUNK * NT),
        compiler_params=params(),
    )(where, tokens, up_first, cotangent, down_second)
    return outs[0], [outs[1 + c * NT : 1 + (c + 1) * NT] for c in range(N_CHUNK)]


def middle(where, received, up_second, down_first, chunk, scale, sizes):
    T, L, BS, NT, G, SW, Q, HB = sizes
    rows_up, rows_down = BS // (2 * Q), HB // (2 * Q)
    tile = min(512, HB)

    def kernel(where_ref, *refs):
        ins, up_ref, down_ref = refs[:NT], refs[NT], refs[NT + 1]
        downs, backs = refs[NT + 2 : 2 * NT + 2], refs[2 * NT + 2 : 3 * NT + 2]
        up_send, up_keep, down_send, down_keep = refs[3 * NT + 2 : 3 * NT + 6]
        r_scr, g_scr, rs_scr, act_scr, gp_scr, out_scr = refs[3 * NT + 6 :]
        me, core = where_ref[0], where_ref[1]
        for shift in range(NT):
            source = lax.rem(me + NT - shift, NT)
            r_scr[source] = ins[shift][0, 0].reshape(L * SW, T)
            g_scr[source] = ins[shift][1, 0].reshape(L * SW, T)
        regrouped = r_scr[...].reshape(BS, T)
        grad_mid = g_scr[...].reshape(BS, T)
        rs_scr[...] = regrouped.reshape(Q, 2, rows_up, T)
        for start in range(0, HB, tile):
            pre = dot(up_ref[0, :, start : start + tile], regrouped, 0, 0)
            value, slope = gelu_pair(pre)
            act_scr[start : start + tile] = value.astype(BF16)
            grad_act = dot(down_ref[0, start : start + tile], grad_mid, 1, 0)
            gp_scr[start : start + tile] = (grad_act * slope).astype(BF16)
        activated = act_scr[...]
        grad_pre = gp_scr[...]
        out_scr[0] = dot(down_ref[0], activated, 0, 0).astype(BF16).reshape(NT, L, SW, T)
        out_scr[1] = dot(up_ref[0], grad_pre, 1, 0).astype(BF16).reshape(NT, L, SW, T)
        for shift in range(NT):
            target = lax.rem(me + shift, NT)
            downs[shift][0] = out_scr[0, target]
            backs[shift][0] = out_scr[1, target]
        for send, ref in ((True, up_send), (False, up_keep)):
            half = rs_scr[:, 1 - core if send else core].reshape(Q * rows_up, T)
            part = scale * dot(half, grad_pre, 1, 1)
            ref[0] = part.astype(BF16).reshape(Q, rows_up, HB)
        for send, ref in ((True, down_send), (False, down_keep)):
            for q in range(Q):
                first = (2 * q + (1 - core if send else core)) * rows_down
                half = act_scr[pl.ds(pl.multiple_of(first, rows_down), rows_down)]
                ref[0, q] = (scale * dot(half, grad_mid, 1, 1)).astype(BF16)

    base = chunk * G
    piece = jax.ShapeDtypeStruct((G, L, SW, T), BF16)
    piece_spec = spec((1, L, SW, T), lambda g, s: (g, 0, 0, 0))
    up_part = jax.ShapeDtypeStruct((G, Q, rows_up, HB), BF16)
    down_part = jax.ShapeDtypeStruct((G, Q, rows_down, BS), BF16)
    outs = pl.pallas_call(
        kernel,
        name="middle",
        grid_spec=pltpu.PrefetchScalarGridSpec(
            num_scalar_prefetch=1,
            grid=(G,),
            in_specs=[spec((2, 1, L, SW, T), lambda g, s: (0, g, 0, 0, 0))] * NT
            + [
                spec((1, BS, HB), lambda g, s: (base + g, 0, 0)),
                spec((1, HB, BS), lambda g, s: (base + g, 0, 0)),
            ],
            out_specs=[piece_spec] * (2 * NT)
            + [spec((1, Q, rows_up, HB), lambda g, s: (g, 0, 0, 0))] * 2
            + [spec((1, Q, rows_down, BS), lambda g, s: (g, 0, 0, 0))] * 2,
            scratch_shapes=[
                pltpu.VMEM((NT, L * SW, T), BF16),
                pltpu.VMEM((NT, L * SW, T), BF16),
                pltpu.VMEM((Q, 2, rows_up, T), BF16),
                pltpu.VMEM((HB, T), BF16),
                pltpu.VMEM((HB, T), BF16),
                pltpu.VMEM((2, NT, L, SW, T), BF16),
            ],
        ),
        out_shape=[piece] * (2 * NT) + [up_part] * 2 + [down_part] * 2,
        compiler_params=params(),
    )(where, *received, up_second, down_first)
    return outs[:NT], outs[NT : 2 * NT], outs[2 * NT : 2 * NT + 2], outs[2 * NT + 2 :]


def leave(where, received, weight, base_rows, left, scale, sizes, backward):
    T, L, BS, NT, G, SW, Q, _ = sizes
    rows = BS // (2 * Q)
    n_in = N_CHUNK * NT

    def kernel(where_ref, *refs):
        ins, w_ref, base_ref, left_ref = refs[:n_in], refs[n_in], refs[n_in + 1], refs[n_in + 2]
        out_ref, send_ref, keep_ref, scr, slab_scr = refs[n_in + 3 :]
        me, core = where_ref[0], where_ref[1]
        for shift in range(NT):
            source = lax.rem(me + NT - shift, NT)
            for chunk in range(N_CHUNK):
                scr[source, chunk] = ins[chunk * NT + shift][:, 0]
        regrouped = scr[...].reshape(BS, T)
        if backward:
            branch = dot(regrouped.T, w_ref[0], 1, 1)
        else:
            branch = dot(regrouped, w_ref[0], 0, 0)
            slab_scr[...] = regrouped.reshape(Q, 2, rows, T)
        out_ref[...] = (base_ref[...].astype(F32) + branch).astype(BF16)
        for send, ref in ((True, send_ref), (False, keep_ref)):
            which = 1 - core if send else core
            if backward:
                half = left_ref[0, :, which].reshape(Q * rows, T)
                part = dot(half, regrouped, 1, 1)
            else:
                half = slab_scr[:, which].reshape(Q * rows, T)
                part = dot(half, left_ref[...], 1, 0)
            ref[0] = (scale * part).astype(BF16).reshape(Q, rows, BS)

    cols = spec((T, BS), lambda b, s: (0, b))
    part = jax.ShapeDtypeStruct((L, Q, rows, BS), BF16)
    part_spec = spec((1, Q, rows, BS), lambda b, s: (b, 0, 0, 0))
    left_spec = spec((1, Q, 2, rows, T), lambda b, s: (b, 0, 0, 0, 0)) if backward else cols
    return pl.pallas_call(
        kernel,
        name="leave_back" if backward else "leave_out",
        grid_spec=pltpu.PrefetchScalarGridSpec(
            num_scalar_prefetch=1,
            grid=(L,),
            in_specs=[spec((G, 1, SW, T), lambda b, s: (0, b, 0, 0))] * n_in
            + [spec((1, BS, BS), lambda b, s: (b, 0, 0)), cols, left_spec],
            out_specs=[cols, part_spec, part_spec],
            scratch_shapes=[
                pltpu.VMEM((NT, N_CHUNK, G, SW, T), BF16),
                pltpu.VMEM((Q, 2, rows, T), BF16),
            ],
        ),
        out_shape=[jax.ShapeDtypeStruct((T, L * BS), BF16), part, part],
        compiler_params=params(),
    )(where, *received, weight, base_rows, left)


def shifted(pieces):
    count = len(pieces)
    order = sorted(range(1, count), key=lambda k: -min(k, count - k))
    moved = {k: lax.ppermute(pieces[k], "tensor", [(s, (s + k) % count) for s in range(count)]) for k in order}
    return [pieces[0]] + [moved[k] for k in range(1, count)]


def swap(value, bit):
    count = lax.axis_size("dp")
    return lax.ppermute(value, "dp", [(s, s ^ (1 << bit)) for s in range(count)])


def reduce_parts(send, keep, rising):
    bits = (lax.axis_size("dp") // 2).bit_length() - 1
    order = list(range(bits)) if rising else list(range(bits))[::-1]
    index = lax.axis_index("dp")
    got = swap(send, 0)
    lead, rows, width = keep.shape[0], keep.shape[2], keep.shape[3]
    held = list(range(bits))[::-1]
    keep = keep.reshape((lead,) + (2,) * bits + (rows, width))
    got = got.reshape(keep.shape)
    for bit in order:
        axis = 1 + held.index(bit)
        held.remove(bit)
        mine = (index >> (bit + 1)) & 1

        def pick(which):
            a = lax.dynamic_index_in_dim(keep, which, axis, False).astype(F32)
            b = lax.dynamic_index_in_dim(got, which, axis, False).astype(F32)
            return (a + b).astype(BF16)

        outgoing, staying = pick(1 - mine), pick(mine)
        got = swap(outgoing, bit + 1)
        keep = staying
    return keep.astype(F32) + got.astype(F32)


def body(tokens, up_first, up_second, down_first, down_second, cotangent):
    T = tokens.shape[0]
    L, BS = up_first.shape[0], up_first.shape[1]
    HB = up_second.shape[2]
    NT = lax.axis_size("tensor")
    n_dp = lax.axis_size("dp")
    scale = (T * n_dp) ** (-0.5)
    sizes = (T, L, BS, NT, L // N_CHUNK, BS // NB, n_dp // 2, HB)
    where = jnp.stack([lax.axis_index("tensor"), lax.axis_index("dp") % 2]).astype(jnp.int32)

    x_turned, first = enter(where, tokens, up_first, cotangent, down_second, sizes)
    arrived = [shifted(first[c]) for c in range(N_CHUNK)]
    downs, backs, second, third = [], [], [], []
    for c in range(N_CHUNK):
        down, back, up_parts, down_parts = middle(where, arrived[c], up_second, down_first, c, scale, sizes)
        backs += shifted(back)
        downs += shifted(down)
        second.append(reduce_parts(*up_parts, True))
        third.append(reduce_parts(*down_parts, False))
    grad_tokens, *first_parts = leave(where, backs, up_first, cotangent, x_turned, scale, sizes, True)
    layer_out, *fourth_parts = leave(where, downs, down_second, tokens, cotangent, scale, sizes, False)

    def halves(parts):
        cut = L // 2
        return jnp.concatenate(
            [
                reduce_parts(parts[0][:cut], parts[1][:cut], True),
                reduce_parts(parts[0][cut:], parts[1][cut:], False),
            ]
        )

    return (
        layer_out,
        grad_tokens,
        halves(first_parts),
        jnp.concatenate(second),
        jnp.concatenate(third),
        halves(fourth_parts),
    )


def solution(mesh):
    in_specs = (
        P("dp", "tensor"),
        P("tensor", None, None),
        P("tensor", None, None),
        P("tensor", None, None),
        P("tensor", None, None),
        P("dp", "tensor"),
    )
    out_specs = (
        P("dp", "tensor"),
        P("dp", "tensor"),
        P("tensor", "dp", None),
        P("tensor", "dp", None),
        P("tensor", "dp", None),
        P("tensor", "dp", None),
    )
    return jax.shard_map(body, mesh=mesh, in_specs=in_specs, out_specs=out_specs, check_vma=False)
```

time: 475 us -> 285 us (0.60); the launches traced: 466 us -> 285 us
  waiting for transfers between devices: 257 us -> 113 us
  matrix products: 86 us -> 0 us
  starting transfers between devices: 20.1 us -> 86.8 us
  Pallas kernels: 0 us -> 62.1 us
  local copies, waits for them, and re-layouts: 72.9 us -> 12.4 us
  between operations: 15 us -> 1.12 us
  other arithmetic: 15.2 us -> 9.66 us
    ppermute x0 -> x42, waiting for transfers between devices: none -> 113 us  [the longest x24 77.6 us: swap(): return lax.ppermute(value, 'dp', [(s, s ^ 1 << bit) for s in range(count)])]
    unnamed x4 -> x0, waiting for transfers between devices: 99.8 us -> none
    all_to_all x4 -> x0, waiting for transfers between devices: 88 us -> none  [regroup(): lax.all_to_all(sliced, 'tensor', split_axis=2, concat_axis=0, tiled=True)]
    ppermute x0 -> x42, starting transfers between devices: none -> 86.8 us  [the longest x18 62.5 us: shifted(): lax.ppermute(pieces[k], 'tensor', [(s, (s + k) % count) for s in range(co...]
    dot_general x11 -> x0, matrix products: 74.5 us -> none  [the longest x1 16 us: descend(): jnp.einsum('ojt,jmo->jmt', regrouped, down_first, preferred_element_type=...]
    reduce_scatter x2 -> x0, waiting for transfers between devices: 69 us -> none  [the longest x1 69 us: body(): lax.psum_scatter(term_third.astype(jnp.bfloat16), 'dp', scatter_dimension...]
    pallas_call x0 -> x5, Pallas kernels: none -> 62.1 us  [the longest x2 42.2 us: middle(): pl.pallas_call(kernel, name='middle', grid_spec=pltpu.PrefetchScalarGridS...]
    convert_element_type x6 -> x0, local copies, waits for them, and re-layouts: 25 us -> none  [the longest x1 14.9 us: body(): term_second.astype(jnp.bfloat16)]
  transfers between devices with their start and end apart: 7 -> 42, of which waited for: 6 -> 18; matrix products, arithmetic and copies ran while one was open for 28% -> 6% of each run, Pallas kernels for 0% -> 19%
where the time goes in v1:
time: 285 us
  waiting for transfers between devices  113 us (40%)
  starting transfers between devices  86.8 us (30%)
  Pallas kernels  62.1 us (22%)
  local copies, waits for them, and re-layouts  12.4 us (4%)
  other arithmetic  9.66 us (3%)
    ppermute x24, waiting for transfers between devices, swap(): return lax.ppermute(value, 'dp', [(s, s ^ 1 << bit) for s in range(count)])  77.6 us
    ppermute x18, starting transfers between devices, shifted(): lax.ppermute(pieces[k], 'tensor', [(s, (s + k) % count) for s in range(co...  62.5 us
    pallas_call x2, Pallas kernels, middle(): pl.pallas_call(kernel, name='middle', grid_spec=pltpu.PrefetchScalarGridS...  42.2 us
    ppermute x18, waiting for transfers between devices, shifted(): lax.ppermute(pieces[k], 'tensor', [(s, (s + k) % count) for s in range(co...  34.9 us
    ppermute x24, starting transfers between devices, swap(): return lax.ppermute(value, 'dp', [(s, s ^ 1 << bit) for s in range(count)])  24.3 us
    pallas_call x2, Pallas kernels, leave(): pl.pallas_call(kernel, name='leave_back' if backward else 'leave_out', gr...  12.7 us
    pallas_call x1, Pallas kernels, enter(): pl.pallas_call(kernel, name='enter', grid_spec=pltpu.PrefetchScalarGridSp...  7.17 us
  transfers between devices with their start and end apart: 42, of which 18 were waited for; matrix products, arithmetic and copies ran while one was open for 6% of the time, Pallas kernels for 19%

profile of v1, /device:TPU:0, one launch (start us, length us, event | category | flops | bytes accessed | tf_op | source)
XLA Modules:
  0.0 284.5 jit_solution(15263317919706810546)
XLA Ops:
  0.7 7.2 %enter.1 = (bf16[4,4,2,64,384]{4,3,2,1,0:T(8,128)(2,1)}, bf16[2,2,4,32,384]{4,3,2,1,0:T(8,128)(2,1)S(1)}, bf16[2,2,4,32,384]{4,3,2,1,0:T(8,128)(2,1)S(1)}, bf16[...) custom-call(s32[2]{0:T(128)S(1)} %pad_add_fusion.where_ref, ...), custom_call_target="tpu_custom_call" | custom-call | tf_op jit(solution)/shard_map/enter/pallas_call | solution.py:62
  7.9 3.0 %collective-permute-start.6 = (bf16[2,2,4,32,384]{4,3,2,1,0:T(8,128)(2,1)}, bf16[2,2,4,32,384]{4,3,2,1,0:T(8,128)(2,1)S(1)}, u32[]{:S(2)}, u32[]{:S(2)}) collective-permute-start(bf16[2,2,4,32,384]{4,3,2,1,0:T(8,128)(2,1)} %get-tuple-element.54), channel_id=1, source_target_pairs={{0,1},{1,2},{2,3},{3,0},{4,5},{5,6},{6,7},{7,4},{8,9},{9,10},{10,1... | collective-permute-start | bytes 1179656 | tf_op jit(solution)/shard_map/ppermute | solution.py:211
  10.9 2.6 collective-permute-start.7
  15.9 7.4 %collective-permute-done.6.refs_1_ = bf16[2,2,4,32,384]{4,3,2,1,0:T(8,128)(2,1)S(1)} collective-permute-done((bf16[2,2,4,32,384]{4,3,2,1,0:T(8,128)(2,1)}, bf16[2,2,4,32,384]{4,3,2,1,0:T(8,128)(2,1)S(1)}, u32[]{:S(2)}, u32[]{:S(2)}) %collective-permute-start.6) | collective-permute-done | bytes 393248 | tf_op jit(solution)/shard_map/ppermute | solution.py:211
  23.2 2.5 collective-permute-start.2
  25.7 14.5 %collective-permute-done.7.refs_2_ = bf16[2,2,4,32,384]{4,3,2,1,0:T(8,128)(2,1)} collective-permute-done((bf16[2,2,4,32,384]{4,3,2,1,0:T(8,128)(2,1)}, bf16[2,2,4,32,384]{4,3,2,1,0:T(8,128)(2,1)}, u32[]{:S(2)}, u32[]{:S(2)}) %collective-permute-start.7) | collective-permute-done | bytes 393248 | tf_op jit(solution)/shard_map/ppermute | solution.py:211
  40.3 21.1 %middle.3 = (bf16[2,4,32,384]{3,2,1,0:T(8,128)(2,1)S(1)}, bf16[2,4,32,384]{3,2,1,0:T(8,128)(2,1)S(1)}, bf16[2,4,32,384]{3,2,1,0:T(8,128)(2,1)S(1)}, bf16[2,4,32,...) custom-call(s32[2]{0:T(128)S(1)} %pad_add_fusion.where_ref, ...), custom_call_target="tpu_custom_call" | custom-call | tf_op jit(solution)/shard_map/middle/pallas_call | solution.py:126
  61.3 25.0 %collective-permute-start.15 = (bf16[2,4,32,384]{3,2,1,0:T(8,128)(2,1)S(1)}, bf16[2,4,32,384]{3,2,1,0:T(8,128)(2,1)S(1)}, u32[]{:S(2)}, u32[]{:S(2)}) collective-permute-start(bf16[2,4,32,384]{3,2,1,0:T(8,128)(2,1)S(1)} %get-tuple-element.67), channel_id=1, source_target_pairs={{0,1},{1,2},{2,3},{3,0},{4,5},{5,6},{6,7},{7,4},{8,9},{9,10},{10,1... | collective-permute-start | bytes 589832 | tf_op jit(solution)/shard_map/ppermute | solution.py:211
  86.3 2.6 collective-permute-start.16
  90.0 21.1 %middle.2 = (bf16[2,4,32,384]{3,2,1,0:T(8,128)(2,1)S(1)}, bf16[2,4,32,384]{3,2,1,0:T(8,128)(2,1)S(1)}, bf16[2,4,32,384]{3,2,1,0:T(8,128)(2,1)S(1)}, bf16[2,4,32,...) custom-call(s32[2]{0:T(128)S(1)} %pad_add_fusion.where_ref, ...), custom_call_target="tpu_custom_call" | custom-call | tf_op jit(solution)/shard_map/middle/pallas_call | solution.py:126
  116.4 2.1 collective-permute-start.14
  122.9 1.9 collective-permute-start.11
  124.8 9.0 %collective-permute-done.13.refs_2_ = bf16[2,4,32,384]{3,2,1,0:T(8,128)(2,1)S(1)} collective-permute-done((bf16[2,4,32,384]{3,2,1,0:T(8,128)(2,1)S(1)}, bf16[2,4,32,384]{3,2,1,0:T(8,128)(2,1)S(1)}, u32[]{:S(2)}, u32[]{:S(2)}) %collective-permute-start.13) | collective-permute-done | bytes 196640 | tf_op jit(solution)/shard_map/ppermute | solution.py:211
  133.8 5.0 %collective-permute-start.3 = (bf16[2,4,32,384]{3,2,1,0:T(8,128)(2,1)S(1)}, bf16[2,4,32,384]{3,2,1,0:T(8,128)(2,1)S(1)}, u32[]{:S(2)}, u32[]{:S(2)}) collective-permute-start(bf16[2,4,32,384]{3,2,1,0:T(8,128)(2,1)S(1)} %get-tuple-element.50), channel_id=1, source_target_pairs={{0,1},{1,2},{2,3},{3,0},{4,5},{5,6},{6,7},{7,4},{8,9},{9,10},{10,1... | collective-permute-start | bytes 589832 | tf_op jit(solution)/shard_map/ppermute | solution.py:211
  138.9 3.8 %collective-permute-start.4 = (bf16[2,4,32,384]{3,2,1,0:T(8,128)(2,1)S(1)}, bf16[2,4,32,384]{3,2,1,0:T(8,128)(2,1)S(1)}, u32[]{:S(2)}, u32[]{:S(2)}) collective-permute-start(bf16[2,4,32,384]{3,2,1,0:T(8,128)(2,1)S(1)} %get-tuple-element.51), channel_id=1, source_target_pairs={{0,2},{1,3},{2,0},{3,1},{4,6},{5,7},{6,4},{7,5},{8,10},{9,11},{10,... | collective-permute-start | bytes 589832 | tf_op jit(solution)/shard_map/ppermute | solution.py:211
  142.7 6.3 %leave_back.1 = (bf16[384,2048]{1,0:T(8,128)(2,1)}, bf16[4,4,64,512]{3,2,1,0:T(8,128)(2,1)}, bf16[4,4,64,512]{3,2,1,0:T(8,128)(2,1)}) custom-call(s32[2]{0:T(128)S(1)} %pad_add_fusion.where_ref, bf16[2,4,32,384]{3,2,1,0:T(8,128)(2,1)S(1)} %get-tuple-element.62.refs_0_, bf16[2,4,32,384]{3,2,1,0:T(8,128)(2,1)S(1)} %collective-permute-done.12.refs_1_, ...), custom_call_target="tpu_custom_call" | custom-call | tf_op jit(solution)/shard_map/leave_back/pallas_call | solution.py:189
  150.5 6.7 %collective-permute-start.5 = (bf16[2,4,32,384]{3,2,1,0:T(8,128)(2,1)S(1)}, bf16[2,4,32,384]{3,2,1,0:T(8,128)(2,1)S(1)}, u32[]{:S(2)}, u32[]{:S(2)}) collective-permute-start(bf16[2,4,32,384]{3,2,1,0:T(8,128)(2,1)S(1)} %get-tuple-element.52), channel_id=1, source_target_pairs={{0,3},{1,0},{2,1},{3,2},{4,7},{5,4},{6,5},{7,6},{8,11},{9,8},{10,9... | collective-permute-start | bytes 589832 | tf_op jit(solution)/shard_map/ppermute | solution.py:211
  158.0 3.0 %collective-permute-done.4.refs_2_ = bf16[2,4,32,384]{3,2,1,0:T(8,128)(2,1)S(1)} collective-permute-done((bf16[2,4,32,384]{3,2,1,0:T(8,128)(2,1)S(1)}, bf16[2,4,32,384]{3,2,1,0:T(8,128)(2,1)S(1)}, u32[]{:S(2)}, u32[]{:S(2)}) %collective-permute-start.4) | collective-permute-done | bytes 196640 | tf_op jit(solution)/shard_map/ppermute | solution.py:211
  161.9 6.4 %leave_out.1 = (bf16[384,2048]{1,0:T(8,128)(2,1)}, bf16[4,4,64,512]{3,2,1,0:T(8,128)(2,1)}, bf16[4,4,64,512]{3,2,1,0:T(8,128)(2,1)}) custom-call(s32[2]{0:T(128)S(1)} %pad_add_fusion.where_ref, bf16[2,4,32,384]{3,2,1,0:T(8,128)(2,1)S(1)} %get-tuple-element.49.refs_0_, bf16[2,4,32,384]{3,2,1,0:T(8,128)(2,1)S(1)} %collective-permute-done.3.refs_1_, ...), custom_call_target="tpu_custom_call" | custom-call | tf_op jit(solution)/shard_map/leave_out/pallas_call | solution.py:189
  176.2 4.9 %collective-permute-done.37 = bf16[2,2,64,512]{3,2,0,1:T(8,128)(2,1)S(1)} collective-permute-done((bf16[2,2,64,512]{3,2,0,1:T(8,128)(2,1)S(1)}, bf16[2,2,64,512]{3,2,0,1:T(8,128)(2,1)S(1)}, u32[]{:S(2)}, u32[]{:S(2)}) %collective-permute-start.37) | collective-permute-done | bytes 262176 | tf_op jit(solution)/shard_map/ppermute | solution.py:217
  182.6 3.3 %collective-permute-done.19 = bf16[2,2,64,512]{3,2,0,1:T(8,128)(2,1)S(1)} collective-permute-done((bf16[2,2,64,512]{3,2,0,1:T(8,128)(2,1)S(1)}, bf16[2,2,64,512]{3,2,0,1:T(8,128)(2,1)S(1)}, u32[]{:S(2)}, u32[]{:S(2)}) %collective-permute-start.19) | collective-permute-done | bytes 262176 | tf_op jit(solution)/shard_map/ppermute | solution.py:217
  187.9 4.0 %collective-permute-done.38 = bf16[2,64,512]{2,1,0:T(8,128)(2,1)S(1)} collective-permute-done((bf16[2,64,512]{2,1,0:T(8,128)(2,1)S(1)}, bf16[2,64,512]{2,1,0:T(8,128)(2,1)S(1)}, u32[]{:S(2)}, u32[]{:S(2)}) %collective-permute-start.38) | collective-permute-done | bytes 131104 | tf_op jit(solution)/shard_map/ppermute | solution.py:217
  193.4 3.6 %collective-permute-done.20 = bf16[2,64,512]{2,1,0:T(8,128)(2,1)S(1)} collective-permute-done((bf16[2,64,512]{2,1,0:T(8,128)(2,1)S(1)}, bf16[2,64,512]{2,1,0:T(8,128)(2,1)S(1)}, u32[]{:S(2)}, u32[]{:S(2)}) %collective-permute-start.20) | collective-permute-done | bytes 131104 | tf_op jit(solution)/shard_map/ppermute | solution.py:217
  198.6 3.4 %collective-permute-done.41 = bf16[2,64,512]{2,1,0:T(8,128)(2,1)S(1)} collective-permute-done((bf16[2,64,512]{2,1,0:T(8,128)(2,1)S(1)}, bf16[2,64,512]{2,1,0:T(8,128)(2,1)S(1)}, u32[]{:S(2)}, u32[]{:S(2)}) %collective-permute-start.41) | collective-permute-done | bytes 131104 | tf_op jit(solution)/shard_map/ppermute | solution.py:217
  204.4 2.6 collective-permute-done.23
  207.8 2.8 %constant_dynamic-slice_fusion.14 = (bf16[2,2,1,64,2048]{4,3,2,1,0:T(8,128)(2,1)S(1)}, bf16[2,2,1,64,2048]{4,3,2,1,0:T(8,128)(2,1)S(1)}, bf16[2,2,1,64,2048]{4,3...) fusion(bf16[2,2,2,64,2048]{4,3,2,1,0:T(8,128)(2,1)} %bitcast.24, s32[]{:T(128)S(6)} %select_n.87, s32[]{:T(128)S(6)} %select_n.89, ...), kind=kLoop, calls=%fused_computation.98 | loop fusion | bytes 8388616 | tf_op jit(solution)/shard_map/jit(dynamic_index_in_dim)/dynamic_slice | solution.py:236
  218.1 19.2 %collective-permute-done.28 = bf16[2,2,64,2048]{3,2,0,1:T(8,128)(2,1)S(1)} collective-permute-done((bf16[2,2,64,2048]{3,2,0,1:T(8,128)(2,1)S(1)}, bf16[2,2,64,2048]{3,2,0,1:T(8,128)(2,1)S(1)}, u32[]{:S(2)}, u32[]{:S(2)}) %collective-permute-start.28) | collective-permute-done | bytes 1048608 | tf_op jit(solution)/shard_map/ppermute | solution.py:217
  239.3 16.0 %collective-permute-done.25 = bf16[2,2,64,2048]{3,2,0,1:T(8,128)(2,1)S(1)} collective-permute-done((bf16[2,2,64,2048]{3,2,0,1:T(8,128)(2,1)S(1)}, bf16[2,2,64,2048]{3,2,0,1:T(8,128)(2,1)S(1)}, u32[]{:S(2)}, u32[]{:S(2)}) %collective-permute-start.25) | collective-permute-done | bytes 1048608 | tf_op jit(solution)/shard_map/ppermute | solution.py:217
  255.5 2.6 collective-permute-start.26
  259.7 3.4 %collective-permute-done.31 = bf16[2,2,256,512]{3,2,0,1:T(8,128)(2,1)S(1)} collective-permute-done((bf16[2,2,256,512]{3,2,0,1:T(8,128)(2,1)S(1)}, bf16[2,2,256,512]{3,2,0,1:T(8,128)(2,1)S(1)}, u32[]{:S(2)}, u32[]{:S(2)}) %collective-permute-start.31) | collective-permute-done | bytes 1048608 | tf_op jit(solution)/shard_map/ppermute | solution.py:217
  264.7 9.8 %collective-permute-done.29 = bf16[2,64,2048]{2,1,0:T(8,128)(2,1)S(1)} collective-permute-done((bf16[2,64,2048]{2,1,0:T(8,128)(2,1)S(1)}, bf16[2,64,2048]{2,1,0:T(8,128)(2,1)S(1)}, u32[]{:S(2)}, u32[]{:S(2)}) %collective-permute-start.29) | collective-permute-done | bytes 524320 | tf_op jit(solution)/shard_map/ppermute | solution.py:217
  274.6 6.2 %collective-permute-done.26 = bf16[2,64,2048]{2,1,0:T(8,128)(2,1)S(1)} collective-permute-done((bf16[2,64,2048]{2,1,0:T(8,128)(2,1)S(1)}, bf16[2,64,2048]{2,1,0:T(8,128)(2,1)S(1)}, u32[]{:S(2)}, u32[]{:S(2)}) %collective-permute-start.26) | collective-permute-done | bytes 524320 | tf_op jit(solution)/shard_map/ppermute | solution.py:217
  (138 shorter events, 50.3 us)
Async XLA Ops:
  7.9 15.4 %collective-permute-start.6 = (bf16[2,2,4,32,384]{4,3,2,1,0:T(8,128)(2,1)}, bf16[2,2,4,32,384]{4,3,2,1,0:T(8,128)(2,1)S(1)}, u32[]{:S(2)}, u32[]{:S(2)}) collective-permute-start(bf16[2,2,4,32,384]{4,3,2,1,0:T(8,128)(2,1)} %get-tuple-element.54), channel_id=1, source_target_pairs={{0,1},{1,2},{2,3},{3,0},{4,5},{5,6},{6,7},{7,4},{8,9},{9,10},{10,1... | collective-permute-start | bytes 1179656 | tf_op jit(solution)/shard_map/ppermute | solution.py:211
  10.9 29.3 %collective-permute-start.7 = (bf16[2,2,4,32,384]{4,3,2,1,0:T(8,128)(2,1)}, bf16[2,2,4,32,384]{4,3,2,1,0:T(8,128)(2,1)}, u32[]{:S(2)}, u32[]{:S(2)}) collective-permute-start(bf16[2,2,4,32,384]{4,3,2,1,0:T(8,128)(2,1)} %get-tuple-element.55), channel_id=1, source_target_pairs={{0,2},{1,3},{2,0},{3,1},{4,6},{5,7},{6,4},{7,5},{8,10},{9,11},{10,... | collective-permute-start | bytes 1179656 | tf_op jit(solution)/shard_map/ppermute | solution.py:211
  13.5 26.7 %collective-permute-start.8 = (bf16[2,2,4,32,384]{4,3,2,1,0:T(8,128)(2,1)}, bf16[2,2,4,32,384]{4,3,2,1,0:T(8,128)(2,1)}, u32[]{:S(2)}, u32[]{:S(2)}) collective-permute-start(bf16[2,2,4,32,384]{4,3,2,1,0:T(8,128)(2,1)} %get-tuple-element.56), channel_id=1, source_target_pairs={{0,3},{1,0},{2,1},{3,2},{4,7},{5,4},{6,5},{7,6},{8,11},{9,8},{10,9... | collective-permute-start | bytes 1179656 | tf_op jit(solution)/shard_map/ppermute | solution.py:211
  14.9 74.1 %collective-permute-start = (bf16[2,2,4,32,384]{4,3,2,1,0:T(8,128)(2,1)S(1)}, bf16[2,2,4,32,384]{4,3,2,1,0:T(8,128)(2,1)S(1)}, u32[]{:S(2)}, u32[]{:S(2)}) collective-permute-start(bf16[2,2,4,32,384]{4,3,2,1,0:T(8,128)(2,1)S(1)} %get-tuple-element.46), channel_id=1, source_target_pairs={{0,1},{1,2},{2,3},{3,0},{4,5},{5,6},{6,7},{7,4},{8,9},{9,10},{10,1... | collective-permute-start | bytes 1179656 | tf_op jit(solution)/shard_map/ppermute | solution.py:211
  15.5 73.4 %collective-permute-start.1 = (bf16[2,2,4,32,384]{4,3,2,1,0:T(8,128)(2,1)S(1)}, bf16[2,2,4,32,384]{4,3,2,1,0:T(8,128)(2,1)S(1)}, u32[]{:S(2)}, u32[]{:S(2)}) collective-permute-start(bf16[2,2,4,32,384]{4,3,2,1,0:T(8,128)(2,1)S(1)} %get-tuple-element.47), channel_id=1, source_target_pairs={{0,2},{1,3},{2,0},{3,1},{4,6},{5,7},{6,4},{7,5},{8,10},{9,11},{10,... | collective-permute-start | bytes 1179656 | tf_op jit(solution)/shard_map/ppermute | solution.py:211
  23.2 65.7 %collective-permute-start.2 = (bf16[2,2,4,32,384]{4,3,2,1,0:T(8,128)(2,1)S(1)}, bf16[2,2,4,32,384]{4,3,2,1,0:T(8,128)(2,1)S(1)}, u32[]{:S(2)}, u32[]{:S(2)}) collective-permute-start(bf16[2,2,4,32,384]{4,3,2,1,0:T(8,128)(2,1)S(1)} %get-tuple-element.48), channel_id=1, source_target_pairs={{0,3},{1,0},{2,1},{3,2},{4,7},{5,4},{6,5},{7,6},{8,11},{9,8},{10,9... | collective-permute-start | bytes 1179656 | tf_op jit(solution)/shard_map/ppermute | solution.py:211
  61.3 55.0 %collective-permute-start.15 = (bf16[2,4,32,384]{3,2,1,0:T(8,128)(2,1)S(1)}, bf16[2,4,32,384]{3,2,1,0:T(8,128)(2,1)S(1)}, u32[]{:S(2)}, u32[]{:S(2)}) collective-permute-start(bf16[2,4,32,384]{3,2,1,0:T(8,128)(2,1)S(1)} %get-tuple-element.67), channel_id=1, source_target_pairs={{0,1},{1,2},{2,3},{3,0},{4,5},{5,6},{6,7},{7,4},{8,9},{9,10},{10,1... | collective-permute-start | bytes 589832 | tf_op jit(solution)/shard_map/ppermute | solution.py:211
  86.3 34.0 %collective-permute-start.16 = (bf16[2,4,32,384]{3,2,1,0:T(8,128)(2,1)S(1)}, bf16[2,4,32,384]{3,2,1,0:T(8,128)(2,1)S(1)}, u32[]{:S(2)}, u32[]{:S(2)}) collective-permute-start(bf16[2,4,32,384]{3,2,1,0:T(8,128)(2,1)S(1)} %get-tuple-element.68), channel_id=1, source_target_pairs={{0,2},{1,3},{2,0},{3,1},{4,6},{5,7},{6,4},{7,5},{8,10},{9,11},{10,... | collective-permute-start | bytes 589832 | tf_op jit(solution)/shard_map/ppermute | solution.py:211
  88.9 32.3 %collective-permute-start.17 = (bf16[2,4,32,384]{3,2,1,0:T(8,128)(2,1)S(1)}, bf16[2,4,32,384]{3,2,1,0:T(8,128)(2,1)S(1)}, u32[]{:S(2)}, u32[]{:S(2)}) collective-permute-start(bf16[2,4,32,384]{3,2,1,0:T(8,128)(2,1)S(1)} %get-tuple-element.69), channel_id=1, source_target_pairs={{0,3},{1,0},{2,1},{3,2},{4,7},{5,4},{6,5},{7,6},{8,11},{9,8},{10,9... | collective-permute-start | bytes 589832 | tf_op jit(solution)/shard_map/ppermute | solution.py:211
  111.1 11.8 %collective-permute-start.12 = (bf16[2,4,32,384]{3,2,1,0:T(8,128)(2,1)S(1)}, bf16[2,4,32,384]{3,2,1,0:T(8,128)(2,1)S(1)}, u32[]{:S(2)}, u32[]{:S(2)}) collective-permute-start(bf16[2,4,32,384]{3,2,1,0:T(8,128)(2,1)S(1)} %get-tuple-element.63), channel_id=1, source_target_pairs={{0,1},{1,2},{2,3},{3,0},{4,5},{5,6},{6,7},{7,4},{8,9},{9,10},{10,1... | collective-permute-start | bytes 589832 | tf_op jit(solution)/shard_map/ppermute | solution.py:211
  112.9 20.9 %collective-permute-start.13 = (bf16[2,4,32,384]{3,2,1,0:T(8,128)(2,1)S(1)}, bf16[2,4,32,384]{3,2,1,0:T(8,128)(2,1)S(1)}, u32[]{:S(2)}, u32[]{:S(2)}) collective-permute-start(bf16[2,4,32,384]{3,2,1,0:T(8,128)(2,1)S(1)} %get-tuple-element.64), channel_id=1, source_target_pairs={{0,2},{1,3},{2,0},{3,1},{4,6},{5,7},{6,4},{7,5},{8,10},{9,11},{10,... | collective-permute-start | bytes 589832 | tf_op jit(solution)/shard_map/ppermute | solution.py:211
  116.4 22.5 %collective-permute-start.14 = (bf16[2,4,32,384]{3,2,1,0:T(8,128)(2,1)S(1)}, bf16[2,4,32,384]{3,2,1,0:T(8,128)(2,1)S(1)}, u32[]{:S(2)}, u32[]{:S(2)}) collective-permute-start(bf16[2,4,32,384]{3,2,1,0:T(8,128)(2,1)S(1)} %get-tuple-element.65), channel_id=1, source_target_pairs={{0,3},{1,0},{2,1},{3,2},{4,7},{5,4},{6,5},{7,6},{8,11},{9,8},{10,9... | collective-permute-start | bytes 589832 | tf_op jit(solution)/shard_map/ppermute | solution.py:211
  120.3 30.2 %collective-permute-start.9 = (bf16[2,4,32,384]{3,2,1,0:T(8,128)(2,1)S(1)}, bf16[2,4,32,384]{3,2,1,0:T(8,128)(2,1)S(1)}, u32[]{:S(2)}, u32[]{:S(2)}) collective-permute-start(bf16[2,4,32,384]{3,2,1,0:T(8,128)(2,1)S(1)} %get-tuple-element.58), channel_id=1, source_target_pairs={{0,1},{1,2},{2,3},{3,0},{4,5},{5,6},{6,7},{7,4},{8,9},{9,10},{10,1... | collective-permute-start | bytes 589832 | tf_op jit(solution)/shard_map/ppermute | solution.py:211
  121.3 36.0 %collective-permute-start.10 = (bf16[2,4,32,384]{3,2,1,0:T(8,128)(2,1)S(1)}, bf16[2,4,32,384]{3,2,1,0:T(8,128)(2,1)S(1)}, u32[]{:S(2)}, u32[]{:S(2)}) collective-permute-start(bf16[2,4,32,384]{3,2,1,0:T(8,128)(2,1)S(1)} %get-tuple-element.59), channel_id=1, source_target_pairs={{0,2},{1,3},{2,0},{3,1},{4,6},{5,7},{6,4},{7,5},{8,10},{9,11},{10,... | collective-permute-start | bytes 589832 | tf_op jit(solution)/shard_map/ppermute | solution.py:211
  122.9 34.5 %collective-permute-start.11 = (bf16[2,4,32,384]{3,2,1,0:T(8,128)(2,1)S(1)}, bf16[2,4,32,384]{3,2,1,0:T(8,128)(2,1)S(1)}, u32[]{:S(2)}, u32[]{:S(2)}) collective-permute-start(bf16[2,4,32,384]{3,2,1,0:T(8,128)(2,1)S(1)} %get-tuple-element.60), channel_id=1, source_target_pairs={{0,3},{1,0},{2,1},{3,2},{4,7},{5,4},{6,5},{7,6},{8,11},{9,8},{10,9... | collective-permute-start | bytes 589832 | tf_op jit(solution)/shard_map/ppermute | solution.py:211
  133.8 24.0 %collective-permute-start.3 = (bf16[2,4,32,384]{3,2,1,0:T(8,128)(2,1)S(1)}, bf16[2,4,32,384]{3,2,1,0:T(8,128)(2,1)S(1)}, u32[]{:S(2)}, u32[]{:S(2)}) collective-permute-start(bf16[2,4,32,384]{3,2,1,0:T(8,128)(2,1)S(1)} %get-tuple-element.50), channel_id=1, source_target_pairs={{0,1},{1,2},{2,3},{3,0},{4,5},{5,6},{6,7},{7,4},{8,9},{9,10},{10,1... | collective-permute-start | bytes 589832 | tf_op jit(solution)/shard_map/ppermute | solution.py:211
  138.9 22.2 %collective-permute-start.4 = (bf16[2,4,32,384]{3,2,1,0:T(8,128)(2,1)S(1)}, bf16[2,4,32,384]{3,2,1,0:T(8,128)(2,1)S(1)}, u32[]{:S(2)}, u32[]{:S(2)}) collective-permute-start(bf16[2,4,32,384]{3,2,1,0:T(8,128)(2,1)S(1)} %get-tuple-element.51), channel_id=1, source_target_pairs={{0,2},{1,3},{2,0},{3,1},{4,6},{5,7},{6,4},{7,5},{8,10},{9,11},{10,... | collective-permute-start | bytes 589832 | tf_op jit(solution)/shard_map/ppermute | solution.py:211
  157.3 50.5 %collective-permute-start.27 = (bf16[2,4,64,2048]{3,2,1,0:T(8,128)(2,1)}, bf16[2,4,64,2048]{3,2,1,0:T(8,128)(2,1)}, u32[]{:S(2)}, u32[]{:S(2)}) collective-permute-start(bf16[2,4,64,2048]{3,2,1,0:T(8,128)(2,1)} %get-tuple-element.77), channel_id=1, source_target_pairs={{0,4},{4,0},{8,12},{12,8},{16,20},{20,16},{24,28},{28,24},{1,5},{5... | collective-permute-start | bytes 6291464 | tf_op jit(solution)/shard_map/ppermute | solution.py:217
  157.4 50.4 %collective-permute-start.24 = (bf16[2,4,64,2048]{3,2,1,0:T(8,128)(2,1)}, bf16[2,4,64,2048]{3,2,1,0:T(8,128)(2,1)}, u32[]{:S(2)}, u32[]{:S(2)}) collective-permute-start(bf16[2,4,64,2048]{3,2,1,0:T(8,128)(2,1)} %get-tuple-element.75), channel_id=1, source_target_pairs={{0,4},{4,0},{8,12},{12,8},{16,20},{20,16},{24,28},{28,24},{1,5},{5... | collective-permute-start | bytes 6291464 | tf_op jit(solution)/shard_map/ppermute | solution.py:217
  157.9 12.7 %collective-permute-start.18 = (bf16[2,4,64,512]{3,2,1,0:T(8,128)(2,1)S(1)}, bf16[2,4,64,512]{3,2,1,0:T(8,128)(2,1)S(1)}, u32[]{:S(2)}, u32[]{:S(2)}) collective-permute-start(bf16[2,4,64,512]{3,2,1,0:T(8,128)(2,1)S(1)} %get-tuple-element.106), channel_id=1, source_target_pairs={{0,4},{4,0},{8,12},{12,8},{16,20},{20,16},{24,28},{28,24},{1,5},{5... | collective-permute-start | bytes 1572872 | tf_op jit(solution)/shard_map/ppermute | solution.py:217
  173.5 12.4 %collective-permute-start.19 = (bf16[2,2,64,512]{3,2,0,1:T(8,128)(2,1)S(1)}, bf16[2,2,64,512]{3,2,0,1:T(8,128)(2,1)S(1)}, u32[]{:S(2)}, u32[]{:S(2)}) collective-permute-start(bf16[2,2,64,512]{3,2,0,1:T(8,128)(2,1)S(1)} %fusion.20), channel_id=1, source_target_pairs={{0,8},{4,12},{8,0},{12,4},{16,24},{20,28},{24,16},{28,20},{1,9},{5... | collective-permute-start | bytes 786440 | tf_op jit(solution)/shard_map/ppermute | solution.py:217
  174.2 11.7 %collective-permute-start.40 = (bf16[2,2,64,512]{3,2,0,1:T(8,128)(2,1)S(1)}, bf16[2,2,64,512]{3,2,0,1:T(8,128)(2,1)S(1)}, u32[]{:S(2)}, u32[]{:S(2)}) collective-permute-start(bf16[2,2,64,512]{3,2,0,1:T(8,128)(2,1)S(1)} %fusion.23), channel_id=1, source_target_pairs={{0,16},{4,20},{8,24},{12,28},{16,0},{20,4},{24,8},{28,12},{1,17},{... | collective-permute-start | bytes 786440 | tf_op jit(solution)/shard_map/ppermute | solution.py:217
  185.8 28.0 %collective-permute-start.33 = (bf16[2,4,256,512]{3,2,1,0:T(8,128)(2,1)S(1)}, bf16[2,4,256,512]{3,2,1,0:T(8,128)(2,1)S(1)}, u32[]{:S(2)}, u32[]{:S(2)}) collective-permute-start(bf16[2,4,256,512]{3,2,1,0:T(8,128)(2,1)S(1)} %copy-done.12), channel_id=1, source_target_pairs={{0,4},{4,0},{8,12},{12,8},{16,20},{20,16},{24,28},{28,24},{1,5},{5... | collective-permute-start | bytes 6291464 | tf_op jit(solution)/shard_map/ppermute | solution.py:217
  187.8 26.1 %collective-permute-start.30 = (bf16[2,4,256,512]{3,2,1,0:T(8,128)(2,1)S(1)}, bf16[2,4,256,512]{3,2,1,0:T(8,128)(2,1)S(1)}, u32[]{:S(2)}, u32[]{:S(2)}) collective-permute-start(bf16[2,4,256,512]{3,2,1,0:T(8,128)(2,1)S(1)} %copy-done.13), channel_id=1, source_target_pairs={{0,4},{4,0},{8,12},{12,8},{16,20},{20,16},{24,28},{28,24},{1,5},{5... | collective-permute-start | bytes 6291464 | tf_op jit(solution)/shard_map/ppermute | solution.py:217
  211.1 26.2 %collective-permute-start.28 = (bf16[2,2,64,2048]{3,2,0,1:T(8,128)(2,1)S(1)}, bf16[2,2,64,2048]{3,2,0,1:T(8,128)(2,1)S(1)}, u32[]{:S(2)}, u32[]{:S(2)}) collective-permute-start(bf16[2,2,64,2048]{3,2,0,1:T(8,128)(2,1)S(1)} %fusion.1), channel_id=1, source_target_pairs={{0,8},{4,12},{8,0},{12,4},{16,24},{20,28},{24,16},{28,20},{1,9},{5... | collective-permute-start | bytes 3145736 | tf_op jit(solution)/shard_map/ppermute | solution.py:217
  213.1 42.3 %collective-permute-start.25 = (bf16[2,2,64,2048]{3,2,0,1:T(8,128)(2,1)S(1)}, bf16[2,2,64,2048]{3,2,0,1:T(8,128)(2,1)S(1)}, u32[]{:S(2)}, u32[]{:S(2)}) collective-permute-start(bf16[2,2,64,2048]{3,2,0,1:T(8,128)(2,1)S(1)} %fusion), channel_id=1, source_target_pairs={{0,8},{4,12},{8,0},{12,4},{16,24},{20,28},{24,16},{28,20},{1,9},{5... | collective-permute-start | bytes 3145736 | tf_op jit(solution)/shard_map/ppermute | solution.py:217
  214.6 43.5 %collective-permute-start.34 = (bf16[2,2,256,512]{3,2,0,1:T(8,128)(2,1)S(1)}, bf16[2,2,256,512]{3,2,0,1:T(8,128)(2,1)S(1)}, u32[]{:S(2)}, u32[]{:S(2)}) collective-permute-start(bf16[2,2,256,512]{3,2,0,1:T(8,128)(2,1)S(1)} %fusion.3), channel_id=1, source_target_pairs={{0,16},{4,20},{8,24},{12,28},{16,0},{20,4},{24,8},{28,12},{1,17},{... | collective-permute-start | bytes 3145736 | tf_op jit(solution)/shard_map/ppermute | solution.py:217
  216.4 46.8 %collective-permute-start.31 = (bf16[2,2,256,512]{3,2,0,1:T(8,128)(2,1)S(1)}, bf16[2,2,256,512]{3,2,0,1:T(8,128)(2,1)S(1)}, u32[]{:S(2)}, u32[]{:S(2)}) collective-permute-start(bf16[2,2,256,512]{3,2,0,1:T(8,128)(2,1)S(1)} %fusion.2), channel_id=1, source_target_pairs={{0,16},{4,20},{8,24},{12,28},{16,0},{20,4},{24,8},{28,12},{1,17},{... | collective-permute-start | bytes 3145736 | tf_op jit(solution)/shard_map/ppermute | solution.py:217
  237.4 37.0 %collective-permute-start.29 = (bf16[2,64,2048]{2,1,0:T(8,128)(2,1)S(1)}, bf16[2,64,2048]{2,1,0:T(8,128)(2,1)S(1)}, u32[]{:S(2)}, u32[]{:S(2)}) collective-permute-start(bf16[2,64,2048]{2,1,0:T(8,128)(2,1)S(1)} %fusion.15), channel_id=1, source_target_pairs={{0,16},{4,20},{8,24},{12,28},{16,0},{20,4},{24,8},{28,12},{1,17},{... | collective-permute-start | bytes 1572872 | tf_op jit(solution)/shard_map/ppermute | solution.py:217
  255.5 25.4 %collective-permute-start.26 = (bf16[2,64,2048]{2,1,0:T(8,128)(2,1)S(1)}, bf16[2,64,2048]{2,1,0:T(8,128)(2,1)S(1)}, u32[]{:S(2)}, u32[]{:S(2)}) collective-permute-start(bf16[2,64,2048]{2,1,0:T(8,128)(2,1)S(1)} %fusion.13), channel_id=1, source_target_pairs={{0,16},{4,20},{8,24},{12,28},{16,0},{20,4},{24,8},{28,12},{1,17},{... | collective-permute-start | bytes 1572872 | tf_op jit(solution)/shard_map/ppermute | solution.py:217
  258.2 22.9 %collective-permute-start.35 = (bf16[2,256,512]{2,1,0:T(8,128)(2,1)S(1)}, bf16[2,256,512]{2,1,0:T(8,128)(2,1)S(1)}, u32[]{:S(2)}, u32[]{:S(2)}) collective-permute-start(bf16[2,256,512]{2,1,0:T(8,128)(2,1)S(1)} %fusion.19), channel_id=1, source_target_pairs={{0,8},{4,12},{8,0},{12,4},{16,24},{20,28},{24,16},{28,20},{1,9},{5... | collective-permute-start | bytes 1572872 | tf_op jit(solution)/shard_map/ppermute | solution.py:217
  263.3 19.5 %collective-permute-start.32 = (bf16[2,256,512]{2,1,0:T(8,128)(2,1)S(1)}, bf16[2,256,512]{2,1,0:T(8,128)(2,1)S(1)}, u32[]{:S(2)}, u32[]{:S(2)}) collective-permute-start(bf16[2,256,512]{2,1,0:T(8,128)(2,1)S(1)} %fusion.17), channel_id=1, source_target_pairs={{0,8},{4,12},{8,0},{12,4},{16,24},{20,28},{24,16},{28,20},{1,9},{5... | collective-permute-start | bytes 1572872 | tf_op jit(solution)/shard_map/ppermute | solution.py:217
  (24 other events, 144.3 us)

commit v2 on v1

v2 whole, which is shorter than its diff:
```python
import jax
import jax.numpy as jnp
from jax import lax
from jax.experimental import pallas as pl
from jax.experimental.pallas import tpu as pltpu
from jax.sharding import PartitionSpec as P

NB = 16
N_CHUNK = 2

gelu_coeff = 0.7978845608028654
cubic_coeff = 0.044715

BF16 = jnp.bfloat16
F32 = jnp.float32


def gelu_pair(hidden):
    inner_arg = gelu_coeff * (hidden + cubic_coeff * hidden * hidden * hidden)
    tangent = jnp.tanh(inner_arg)
    gelu_value = 0.5 * hidden * (1.0 + tangent)
    gelu_slope = 0.5 * (1.0 + tangent) + 0.5 * hidden * (1.0 - tangent * tangent) * gelu_coeff * (
        1.0 + 3.0 * cubic_coeff * hidden * hidden
    )
    return gelu_value, gelu_slope


def dot(a, b, ca, cb):
    return lax.dot_general(a, b, (((ca,), (cb,)), ((), ())), preferred_element_type=F32)


def params(mebibytes):
    return pltpu.CompilerParams(vmem_limit_bytes=mebibytes * 1024 * 1024)


def held(*values):
    return [pltpu.with_memory_space_constraint(v, pltpu.HBM) for v in values]


def spec(block, index_map):
    return pl.BlockSpec(block, index_map)


LIGHT = pl.CostEstimate(flops=0, transcendentals=0, bytes_accessed=0)


def enter(tokens, up_first, cotangent, down_second, sizes):
    T, L, BS, NT, G, SW, Q, _ = sizes
    rows = BS // (2 * Q)

    def kernel(x_ref, w_ref, g_ref, d_ref, xt_ref, *outs):
        turned = x_ref[...].T
        xt_ref[0] = turned.reshape(Q, 2, rows, T)
        up = dot(w_ref[0], turned, 0, 0).astype(BF16).reshape(NT, L, SW, T)
        back = dot(d_ref[0], g_ref[...], 1, 1).astype(BF16).reshape(NT, L, SW, T)
        for chunk in range(N_CHUNK):
            outs[chunk][:, 0, :, 0] = up[:, chunk * G : (chunk + 1) * G]
            outs[chunk][:, 1, :, 0] = back[:, chunk * G : (chunk + 1) * G]

    cols = spec((T, BS), lambda b: (0, b))
    square = spec((1, BS, BS), lambda b: (b, 0, 0))
    outs = pl.pallas_call(
        kernel,
        name="enter",
        grid=(L,),
        in_specs=[cols, square, cols, square],
        out_specs=[spec((1, Q, 2, rows, T), lambda b: (b, 0, 0, 0, 0))]
        + [spec((NT, 2, G, 1, SW, T), lambda b: (0, 0, 0, b, 0, 0))] * N_CHUNK,
        out_shape=[pltpu.HBM((L, Q, 2, rows, T), BF16)]
        + [pltpu.HBM((NT, 2, G, L, SW, T), BF16)] * N_CHUNK,
        compiler_params=params(56),
        cost_estimate=LIGHT,
    )(*held(tokens, up_first, cotangent, down_second))
    return outs[0], outs[1:]


def middle(where, received, up_second, down_first, chunk, scale, sizes, joint):
    T, L, BS, NT, G, SW, Q, HB = sizes
    rows_up, rows_down = BS // (2 * Q), HB // (2 * Q)
    tile = min(512, HB)

    def kernel(where_ref, *refs):
        in_ref, up_ref, down_ref = refs[:3]
        up_send, up_keep, down_send, down_keep, rs_scr, act_scr, at_scr, gp_scr = refs[-8:]
        if joint:
            down_out, back_out = refs[3].at[:, 0], refs[3].at[:, 1]
        else:
            down_out, back_out = refs[3:5]
        core = where_ref[0]
        regrouped = in_ref[:, 0, 0].reshape(BS, T)
        rs_scr[...] = regrouped.reshape(Q, 2, rows_up, T)
        turned = regrouped.T
        grad_mid = in_ref[:, 1, 0].reshape(BS, T).T
        for start in range(0, HB, tile):
            pre = dot(turned, up_ref[0, :, start : start + tile], 1, 0)
            value, slope = gelu_pair(pre)
            value = value.astype(BF16)
            act_scr[:, start : start + tile] = value
            at_scr[start : start + tile] = value.T
            grad_act = dot(grad_mid, down_ref[0, start : start + tile], 1, 1)
            gp_scr[:, start : start + tile] = (grad_act * slope).astype(BF16)
        activated = act_scr[...]
        grad_pre = gp_scr[...]
        down_out[:, 0] = dot(activated, down_ref[0], 1, 0).astype(BF16).T.reshape(NT, L, SW, T)
        back_out[:, 0] = dot(grad_pre, up_ref[0], 1, 1).astype(BF16).T.reshape(NT, L, SW, T)
        for send, ref in ((True, up_send), (False, up_keep)):
            half = rs_scr[:, 1 - core if send else core].reshape(Q * rows_up, T)
            part = scale * dot(half, grad_pre, 1, 0)
            ref[0] = part.astype(BF16).reshape(Q, rows_up, HB)
        for send, ref in ((True, down_send), (False, down_keep)):
            for q in range(Q):
                first = (2 * q + (1 - core if send else core)) * rows_down
                half = at_scr[pl.ds(pl.multiple_of(first, rows_down), rows_down)]
                ref[0, q] = (scale * dot(half, grad_mid, 1, 0)).astype(BF16)

    base = chunk * G
    if joint:
        pieces = [pltpu.HBM((NT, 2, G, L, SW, T), BF16)]
        piece_specs = [spec((NT, 2, 1, L, SW, T), lambda g, s: (0, 0, g, 0, 0, 0))]
    else:
        pieces = [pltpu.HBM((NT, G, L, SW, T), BF16)] * 2
        piece_specs = [spec((NT, 1, L, SW, T), lambda g, s: (0, g, 0, 0, 0))] * 2
    up_part = pltpu.HBM((G, Q, rows_up, HB), BF16)
    down_part = pltpu.HBM((G, Q, rows_down, BS), BF16)
    outs = pl.pallas_call(
        kernel,
        name="middle",
        grid_spec=pltpu.PrefetchScalarGridSpec(
            num_scalar_prefetch=1,
            grid=(G,),
            in_specs=[
                spec((NT, 2, 1, L, SW, T), lambda g, s: (0, 0, g, 0, 0, 0)),
                spec((1, BS, HB), lambda g, s: (base + g, 0, 0)),
                spec((1, HB, BS), lambda g, s: (base + g, 0, 0)),
            ],
            out_specs=piece_specs
            + [spec((1, Q, rows_up, HB), lambda g, s: (g, 0, 0, 0))] * 2
            + [spec((1, Q, rows_down, BS), lambda g, s: (g, 0, 0, 0))] * 2,
            scratch_shapes=[
                pltpu.VMEM((Q, 2, rows_up, T), BF16),
                pltpu.VMEM((T, HB), BF16),
                pltpu.VMEM((HB, T), BF16),
                pltpu.VMEM((T, HB), BF16),
            ],
        ),
        out_shape=pieces + [up_part] * 2 + [down_part] * 2,
        compiler_params=params(32),
        cost_estimate=LIGHT,
    )(where, *held(received, up_second, down_first))
    return outs[:-4], outs[-4:-2], outs[-2:]


def leave(where, received, weight, base_rows, left, scale, sizes, backward):
    T, L, BS, NT, G, SW, Q, _ = sizes
    rows = BS // (2 * Q)

    def kernel(where_ref, *refs):
        ins, (w_ref, base_ref, left_ref) = refs[:N_CHUNK], refs[N_CHUNK : N_CHUNK + 3]
        out_ref, send_ref, keep_ref, scr, slab_scr = refs[N_CHUNK + 3 :]
        core = where_ref[0]
        scr[:, 0] = ins[0][:, 0, :, 0]
        scr[:, 1] = ins[1][:, :, 0]
        regrouped = scr[...].reshape(BS, T)
        if backward:
            branch = dot(regrouped.T, w_ref[0], 1, 1)
        else:
            branch = dot(regrouped, w_ref[0], 0, 0)
            slab_scr[...] = regrouped.reshape(Q, 2, rows, T)
        out_ref[...] = (base_ref[...].astype(F32) + branch).astype(BF16)
        for send, ref in ((True, send_ref), (False, keep_ref)):
            which = 1 - core if send else core
            if backward:
                half = left_ref[0, :, which].reshape(Q * rows, T)
                part = dot(half, regrouped, 1, 1)
            else:
                half = slab_scr[:, which].reshape(Q * rows, T)
                part = dot(half, left_ref[...], 1, 0)
            ref[0] = (scale * part).astype(BF16).reshape(Q, rows, BS)

    side = 1 if backward else 0
    cols = spec((T, BS), lambda b, s: (0, b))
    part = jax.ShapeDtypeStruct((L, Q, rows, BS), BF16)
    part_spec = spec((1, Q, rows, BS), lambda b, s: (b, 0, 0, 0))
    left_spec = spec((1, Q, 2, rows, T), lambda b, s: (b, 0, 0, 0, 0)) if backward else cols
    return pl.pallas_call(
        kernel,
        name="leave_back" if backward else "leave_out",
        grid_spec=pltpu.PrefetchScalarGridSpec(
            num_scalar_prefetch=1,
            grid=(L,),
            in_specs=[
                spec((NT, 1, G, 1, SW, T), lambda b, s: (0, side, 0, b, 0, 0)),
                spec((NT, G, 1, SW, T), lambda b, s: (0, 0, b, 0, 0)),
                spec((1, BS, BS), lambda b, s: (b, 0, 0)),
                cols,
                left_spec,
            ],
            out_specs=[cols, part_spec, part_spec],
            scratch_shapes=[
                pltpu.VMEM((NT, N_CHUNK, G, SW, T), BF16),
                pltpu.VMEM((Q, 2, rows, T), BF16),
            ],
        ),
        out_shape=[pltpu.HBM((T, L * BS), BF16), part, part],
        compiler_params=params(24),
        cost_estimate=LIGHT,
    )(where, *held(*received, weight, base_rows, left))


def together(*values):
    return lax.optimization_barrier(values)


def regroup(pieces, label):
    with jax.named_scope(label):
        return lax.all_to_all(pieces, "tensor", split_axis=0, concat_axis=0, tiled=True)


def swap(value, bit, label):
    count = lax.axis_size("dp")
    with jax.named_scope(label):
        return lax.ppermute(value, "dp", [(s, s ^ (1 << bit)) for s in range(count)])


def split(which, pairs, sizes):
    lead, count = sizes
    n = len(pairs)

    def kernel(which_ref, *refs):
        ins, outs = refs[: 4 * n], refs[4 * n :]
        for i in range(2 * n):
            a, b = ins[2 * i][...].astype(F32), ins[2 * i + 1][...].astype(F32)
            outs[i][...] = (a + b).astype(BF16)

    in_specs, operands, out_specs, out_shape = [], [], [], []
    for i, (keep, got, first, place) in enumerate(pairs):
        rows, width = keep.shape[2:]
        for stays in (0, 1):

            def index(a, r, which_ref, i=i, first=first, place=place, stays=stays):
                mine = which_ref[i]
                chosen = mine if stays else 1 - mine
                low = r & ((1 << place) - 1)
                return (first + a, ((r >> place) << (place + 1)) | (chosen << place) | low, 0, 0)

            in_specs += [spec((1, 1, rows, width), index)] * 2
            operands += [keep, got]
            out_specs.append(spec((1, 1, rows, width), lambda a, r, w: (a, r, 0, 0)))
            out_shape.append(pltpu.HBM((lead, count // 2, rows, width), BF16))
    outs = pl.pallas_call(
        kernel,
        name="split",
        grid_spec=pltpu.PrefetchScalarGridSpec(
            num_scalar_prefetch=1, grid=(lead, count // 2), in_specs=in_specs, out_specs=out_specs
        ),
        out_shape=out_shape,
        compiler_params=params(16),
        cost_estimate=LIGHT,
    )(which, *held(*operands))
    return [(outs[2 * i], outs[2 * i + 1]) for i in range(n)]


def whole():
    return pl.BlockSpec(memory_space=pltpu.VMEM)


def split_small(which, pairs, lead):
    n = len(pairs)

    def kernel(which_ref, *refs):
        ins, outs = refs[: 2 * n], refs[2 * n :]
        for i, (keep, _, first, place) in enumerate(pairs):
            for stays in (0, 1):
                chosen = which_ref[i] if stays else 1 - which_ref[i]
                for r in range(keep.shape[1] // 2):
                    low = r & ((1 << place) - 1)
                    q = ((r >> place) << (place + 1)) + low + chosen * (1 << place)
                    for a in range(lead):
                        total = ins[2 * i][first + a, q].astype(F32) + ins[2 * i + 1][first + a, q].astype(F32)
                        outs[2 * i + stays][a, r] = total.astype(BF16)

    out_shape = []
    for keep, _, _, _ in pairs:
        out_shape += [jax.ShapeDtypeStruct((lead, keep.shape[1] // 2) + keep.shape[2:], BF16)] * 2
    outs = pl.pallas_call(
        kernel,
        name="small",
        in_specs=[pl.BlockSpec(memory_space=pltpu.SMEM)] + [whole()] * (2 * n),
        out_specs=[whole()] * (2 * n),
        out_shape=out_shape,
        compiler_params=params(8),
        cost_estimate=LIGHT,
    )(which, *[array for keep, got, _, _ in pairs for array in (keep, got)])
    return [(outs[2 * i], outs[2 * i + 1]) for i in range(n)]


def finish(groups):
    n = len(groups)
    lead = groups[0][0].shape[0]

    def kernel(*refs):
        ins, outs = refs[: 4 * n], refs[4 * n :]
        for i in range(n):
            for j in range(2):
                a, b = ins[4 * i + 2 * j], ins[4 * i + 2 * j + 1]
                outs[i][j * lead : (j + 1) * lead] = a[:, 0].astype(F32) + b[:, 0].astype(F32)

    return pl.pallas_call(
        kernel,
        name="finish",
        in_specs=[whole()] * (4 * n),
        out_shape=[jax.ShapeDtypeStruct((2 * lead,) + group[0].shape[2:], F32) for group in groups],
        compiler_params=params(16),
        cost_estimate=LIGHT,
    )(*[array for group in groups for array in group])


class Halving:
    def __init__(self, streams, label, large):
        self.label = label
        self.large = large
        self.bits = bits = (lax.axis_size("dp") // 2).bit_length() - 1
        self.orders = [list(range(bits)), list(range(bits))[::-1]]
        self.held = [list(range(bits)), list(range(bits))]
        self.streams = streams

    def add(self, lead):
        index = lax.axis_index("dp")
        pairs, mine = [], []
        self.moving = []
        for (keep, got, first), order, held in zip(self.streams, self.orders, self.held):
            bit = order.pop(0)
            pairs.append((keep, got, first, held.index(bit)))
            held.remove(bit)
            mine.append((index >> (bit + 1)) & 1)
            self.moving.append(bit)
        which = jnp.stack(mine).astype(jnp.int32)
        if self.large and len(self.held[0]) == self.bits - 1:
            self.parts = split(which, pairs, (lead, pairs[0][0].shape[1]))
        else:
            self.parts = split_small(which, pairs, lead)
        return [outgoing for outgoing, _ in self.parts]

    def move(self, outgoing):
        self.streams = [
            (staying, swap(out, bit + 1, "%s_bit%d" % (self.label, bit)), 0)
            for out, (_, staying), bit in zip(outgoing, self.parts, self.moving)
        ]

    def got(self):
        return [got for _, got, _ in self.streams]

    def replace(self, arrived):
        self.streams = [(keep, got, first) for (keep, _, first), got in zip(self.streams, arrived)]

    def run(self, lead):
        while self.orders[0]:
            self.move(self.add(lead))
        return [(keep, got) for keep, got, _ in self.streams]


def body(tokens, up_first, up_second, down_first, down_second, cotangent):
    T = tokens.shape[0]
    L, BS = up_first.shape[0], up_first.shape[1]
    HB = up_second.shape[2]
    NT = lax.axis_size("tensor")
    n_dp = lax.axis_size("dp")
    scale = (T * n_dp) ** (-0.5)
    sizes = (T, L, BS, NT, L // N_CHUNK, BS // NB, n_dp // 2, HB)
    where = (lax.axis_index("dp") % 2).astype(jnp.int32).reshape(1)

    lead = L // N_CHUNK

    def middle_sums(parts, label, before):
        (up_send, up_keep), (down_send, down_keep) = parts
        if before is not None:
            up_send, down_send, *got = together(up_send, down_send, *before.got())
            before.replace(got)
        got_up, got_down = swap(up_send, 0, label + "_core"), swap(down_send, 0, label + "_core")
        return Halving([(up_keep, got_up, 0), (down_keep, got_down, 0)], label, True)

    def edge_sums(parts, label):
        send, keep = parts
        got = swap(send, 0, label + "_core")
        return Halving([(keep, got, 0), (keep, got, lead)], label, False)

    x_turned, (first_0, first_1) = enter(tokens, up_first, cotangent, down_second, sizes)
    in_0 = regroup(first_0, "z1")
    in_0, first_1 = together(in_0, first_1)
    in_1 = regroup(first_1, "z2")
    (both_0,), *parts = middle(where, in_0, up_second, down_first, 0, scale, sizes, True)
    mid_0 = middle_sums(parts, "mid0", None)
    leaving_0 = mid_0.add(lead)
    in_1, both_0 = together(in_1, both_0)
    both_0 = regroup(both_0, "z3")
    mid_0.move(leaving_0)
    in_1, *_ = together(in_1, *leaving_0)
    (down_1, back_1), *parts = middle(where, in_1, up_second, down_first, 1, scale, sizes, False)
    mid_1 = middle_sums(parts, "mid1", mid_0)
    leaving_0 = mid_0.add(lead)
    leaving_1 = mid_1.add(lead)
    both_0, back_1, *_ = together(both_0, back_1, *leaving_0)
    back_1 = regroup(back_1, "z4")
    mid_0.move(leaving_0)
    mid_1.move(leaving_1)
    back_1, down_1, *got = together(back_1, down_1, *mid_0.got(), *leaving_1)
    mid_0.replace(got[:2])
    down_1 = regroup(down_1, "z5")
    grad_tokens, *parts = leave(
        where, (both_0, back_1), up_first, cotangent, x_turned, scale, sizes, True
    )
    edge_first = edge_sums(parts, "first")
    leaving_first = edge_first.add(lead)
    leaving_1 = mid_1.add(lead) if mid_1.orders[0] else []
    edge_first.move(leaving_first)
    mid_1.move(leaving_1)
    down_1, *_ = together(down_1, *leaving_first, *leaving_1)
    layer_out, *parts = leave(
        where, (both_0, down_1), down_second, tokens, cotangent, scale, sizes, False
    )
    edge_fourth = edge_sums(parts, "fourth")
    done_0, done_1 = mid_0.run(lead), mid_1.run(lead)
    leaving_first = edge_first.add(lead)
    edge_fourth.replace(together(*edge_fourth.got(), *leaving_first)[:2])
    edge_first.move(leaving_first)
    leaving_fourth = edge_fourth.add(lead)
    edge_fourth.move(leaving_fourth)
    grad_up_second, grad_down_first = finish([done_0[0] + done_1[0], done_0[1] + done_1[1]])
    (grad_up_first,) = finish([sum(edge_first.run(lead), ())])
    got = together(*edge_fourth.got(), grad_up_second, grad_down_first)
    edge_fourth.replace(got[:2])
    (grad_down_second,) = finish([sum(edge_fourth.run(lead), ())])
    return (
        layer_out,
        grad_tokens,
        grad_up_first.reshape(L, -1, BS),
        got[2].reshape(L, -1, HB),
        got[3].reshape(L, -1, BS),
        grad_down_second.reshape(L, -1, BS),
    )


def solution(mesh):
    in_specs = (
        P("dp", "tensor"),
        P("tensor", None, None),
        P("tensor", None, None),
        P("tensor", None, None),
        P("tensor", None, None),
        P("dp", "tensor"),
    )
    out_specs = (
        P("dp", "tensor"),
        P("dp", "tensor"),
        P("tensor", "dp", None),
        P("tensor", "dp", None),
        P("tensor", "dp", None),
        P("tensor", "dp", None),
    )
    return jax.shard_map(body, mesh=mesh, in_specs=in_specs, out_specs=out_specs, check_vma=False)
```

time: 285 us -> 233 us (0.82)
  waiting for transfers between devices: 113 us -> 63.5 us
  starting transfers between devices: 86.8 us -> 41.1 us
  blocking collectives: 0 us -> 43.4 us
  Pallas kernels: 62.1 us -> 78.3 us
  other arithmetic: 9.66 us -> 0.15 us
  local copies, waits for them, and re-layouts: 12.4 us -> 5.03 us
    ppermute x18 -> x0, starting transfers between devices: 62.5 us -> none  [shifted(): lax.ppermute(pieces[k], 'tensor', [(s, (s + k) % count) for s in range(co...]
    all_to_all x0 -> x1, blocking collectives: none -> 43.4 us  [regroup(): lax.all_to_all(pieces, 'tensor', split_axis=0, concat_axis=0, tiled=True)]
    ppermute x24 -> x22, waiting for transfers between devices: 77.6 us -> 40.1 us  [swap(): return lax.ppermute(value, 'dp', [(s, s ^ 1 << bit) for s in range(count)])]
    ppermute x18 -> x0, waiting for transfers between devices: 34.9 us -> none  [shifted(): lax.ppermute(pieces[k], 'tensor', [(s, (s + k) % count) for s in range(co...]
    all_to_all x0 -> x4, waiting for transfers between devices: none -> 23.4 us  [regroup(): lax.all_to_all(pieces, 'tensor', split_axis=0, concat_axis=0, tiled=True)]
    pallas_call x1 -> x12, Pallas kernels: 7.17 us -> 28.8 us  [the longest x2 12.9 us: split(): pl.pallas_call(kernel, name='split', grid_spec=pltpu.PrefetchScalarGridSp...]
    all_to_all x0 -> x4, starting transfers between devices: none -> 17.5 us  [regroup(): lax.all_to_all(pieces, 'tensor', split_axis=0, concat_axis=0, tiled=True)]
    dynamic_slice x12 -> x0, local copies, waits for them, and re-layouts: 6.28 us -> none  [the longest x4 3.36 us: pick(): b = lax.dynamic_index_in_dim(got, which, axis, False).astype(F32)]
  transfers between devices with their start and end apart: 42 -> 26, of which waited for: 18 -> 15; matrix products, arithmetic and copies ran while one was open for 6% -> 0% of each run, Pallas kernels for 19% -> 28%
where the time goes in v2:
time: 233 us; the launch traced here: 232 us
  Pallas kernels  78.3 us (34%)
  waiting for transfers between devices  63.5 us (27%)
  blocking collectives  43.4 us (19%)
  starting transfers between devices  41.1 us (18%)
  local copies, waits for them, and re-layouts  5.03 us (2%)
    all_to_all x1, blocking collectives, regroup(): lax.all_to_all(pieces, 'tensor', split_axis=0, concat_axis=0, tiled=True)  43.4 us
    ppermute x22, waiting for transfers between devices, swap(): return lax.ppermute(value, 'dp', [(s, s ^ 1 << bit) for s in range(count)])  40.1 us
    pallas_call x2, Pallas kernels, middle(): pl.pallas_call(kernel, name='middle', grid_spec=pltpu.PrefetchScalarGridS...  37.9 us
    ppermute x22, starting transfers between devices, swap(): return lax.ppermute(value, 'dp', [(s, s ^ 1 << bit) for s in range(count)])  23.6 us
    all_to_all x4, waiting for transfers between devices, regroup(): lax.all_to_all(pieces, 'tensor', split_axis=0, concat_axis=0, tiled=True)  23.4 us
    all_to_all x4, starting transfers between devices, regroup(): lax.all_to_all(pieces, 'tensor', split_axis=0, concat_axis=0, tiled=True)  17.5 us
    pallas_call x2, Pallas kernels, split(): pl.pallas_call(kernel, name='split', grid_spec=pltpu.PrefetchScalarGridSp...  12.9 us
    pallas_call x2, Pallas kernels, leave(): pl.pallas_call(kernel, name='leave_back' if backward else 'leave_out', gr...  11.6 us
  transfers between devices with their start and end apart: 26, of which 15 were waited for; matrix products, arithmetic and copies ran while one was open for 0% of the time, Pallas kernels for 28%

profile of v2, /device:TPU:0, one launch (start us, length us, event | category | flops | bytes accessed | tf_op | source)
XLA Modules:
  0.0 232.3 jit_solution(12693631753997613377)
XLA Ops:
  0.6 7.0 %enter.1 = (bf16[4,4,2,64,384]{4,3,2,1,0:T(8,128)(2,1)}, bf16[4,2,2,4,32,384]{5,4,3,2,1,0:T(8,128)(2,1)}, bf16[4,2,2,4,32,384]{5,4,3,2,1,0:T(8,128)(2,1)}) custom-call(bf16[384,2048]{1,0:T(8,128)(2,1)} %refs_3_.3, bf16[4,512,512]{2,1,0:T(8,128)(2,1)} %refs_2_.6, bf16[384,2048]{1,0:T(8,128)(2,1)} %refs_4_.1, bf16[4,512,512]{2,1,0:T(8,128)(2,1)} %refs_2_.7), custom_call_target="tpu_custom_call" | custom-call | tf_op jit(solution)/shard_map/enter/pallas_call | solution.py:62
  7.6 43.4 %all_to_all.25.refs_0_ = bf16[4,2,2,4,32,384]{5,4,3,2,1,0:T(8,128)(2,1)} all-to-all(bf16[4,2,2,4,32,384]{5,4,3,2,1,0:T(8,128)(2,1)} %get-tuple-element.82), channel_id=1, replica_groups=mesh['dp'=8,'tensor'=4] {'tensor'}, dimensions={0} | all-to-all | bytes 3145728 | tf_op jit(solution)/shard_map/z1/all_to_all | solution.py:216
  51.0 4.3 %all-to-all-start.1 = ((bf16[4,2,2,4,32,384]{5,4,3,2,1,0:T(8,128)(2,1)}), bf16[4,2,2,4,32,384]{5,4,3,2,1,0:T(8,128)(2,1)}, u32[]{:S(2)}, u32[]{:S(2)}) async-start(bf16[4,2,2,4,32,384]{5,4,3,2,1,0:T(8,128)(2,1)} %get-tuple-element.84), calls=%async_computation.1 | async-start | bytes 3145728 | tf_op jit(solution)/shard_map/z2/all_to_all | solution.py:216
  55.4 19.0 %middle.2 = (bf16[4,2,2,4,32,384]{5,4,3,2,1,0:T(8,128)(2,1)}, bf16[2,4,64,2048]{3,2,1,0:T(8,128)(2,1)}, bf16[2,4,64,2048]{3,2,1,0:T(8,128)(2,1)}, bf16[2,4,256,5...) custom-call(s32[1]{0:T(128)} %bitcast.where_ref, bf16[4,2,2,4,32,384]{5,4,3,2,1,0:T(8,128)(2,1)} %all_to_all.25.refs_0_, ...), custom_call_target="tpu_custom_call" | custom-call | tf_op jit(solution)/shard_map/middle/pallas_call | solution.py:125
  74.8 16.7 %all-to-all-done.1.refs_0_ = bf16[4,2,2,4,32,384]{5,4,3,2,1,0:T(8,128)(2,1)} async-done(((bf16[4,2,2,4,32,384]{5,4,3,2,1,0:T(8,128)(2,1)}), bf16[4,2,2,4,32,384]{5,4,3,2,1,0:T(8,128)(2,1)}, u32[]{:S(2)}, u32[]{:S(2)}) %all-to-all-start.1) | async-done | bytes 1572896 | tf_op jit(solution)/shard_map/z2/all_to_all | solution.py:216
  91.5 4.5 %all-to-all-start.2 = ((bf16[4,2,2,4,32,384]{5,4,3,2,1,0:T(8,128)(2,1)}), bf16[4,2,2,4,32,384]{5,4,3,2,1,0:T(8,128)(2,1)}, u32[]{:S(2)}, u32[]{:S(2)}) async-start(bf16[4,2,2,4,32,384]{5,4,3,2,1,0:T(8,128)(2,1)} %get-tuple-element.87), calls=%async_computation.2 | async-start | bytes 3145728 | tf_op jit(solution)/shard_map/z3/all_to_all | solution.py:216
  97.5 6.4 %split.2 = (bf16[2,2,64,2048]{3,2,1,0:T(8,128)(2,1)}, bf16[2,2,64,2048]{3,2,1,0:T(8,128)(2,1)}, bf16[2,2,256,512]{3,2,1,0:T(8,128)(2,1)}, bf16[2,2,256,512]{3,2,1,0:T(8,128)(2,1)}) custom-call(s32[2]{0:T(128)S(1)} %pad_add_fusion.which_ref, bf16[2,4,64,2048]{3,2,1,0:T(8,128)(2,1)} %get-tuple-element.89.refs_0_.refs_2_, bf16[2,4,64,2048]{3,2,1,0:T(8,128)(2,1)} %copy-done.14, ...), custom_call_target="tpu_custom_call" | custom-call | tf_op jit(solution)/shard_map/split/pallas_call | solution.py:250
  103.9 1.6 collective-permute-start.2
  105.5 1.5 collective-permute-start.3
  107.0 18.9 %middle.3 = (bf16[4,2,4,32,384]{4,3,2,1,0:T(8,128)(2,1)}, bf16[4,2,4,32,384]{4,3,2,1,0:T(8,128)(2,1)}, bf16[2,4,64,2048]{3,2,1,0:T(8,128)(2,1)}, bf16[2,4,64,204...) custom-call(s32[1]{0:T(128)} %bitcast.where_ref, ...), custom_call_target="tpu_custom_call" | custom-call | tf_op jit(solution)/shard_map/middle/pallas_call | solution.py:125
  125.9 2.4 %collective-permute-done.2.refs_1_ = bf16[2,2,64,2048]{3,2,1,0:T(8,128)(2,1)S(1)} collective-permute-done((bf16[2,2,64,2048]{3,2,1,0:T(8,128)(2,1)}, bf16[2,2,64,2048]{3,2,1,0:T(8,128)(2,1)S(1)}, u32[]{:S(2)}, u32[]{:S(2)}) %collective-permute-start.2) | collective-permute-done | bytes 1048608 | tf_op jit(solution)/shard_map/mid0_bit0/ppermute | solution.py:222
  132.4 4.2 %all-to-all-start.3 = ((bf16[4,2,4,32,384]{4,3,2,1,0:T(8,128)(2,1)}), bf16[4,2,4,32,384]{4,3,2,1,0:T(8,128)(2,1)}, u32[]{:S(2)}, u32[]{:S(2)}) async-start(bf16[4,2,4,32,384]{4,3,2,1,0:T(8,128)(2,1)} %get-tuple-element.106), calls=%async_computation.3 | async-start | bytes 1572864 | tf_op jit(solution)/shard_map/z4/all_to_all | solution.py:216
  136.6 1.6 collective-permute-start.4
  138.2 1.5 collective-permute-start.5
  139.7 6.4 %split.3 = (bf16[2,2,64,2048]{3,2,1,0:T(8,128)(2,1)}, bf16[2,2,64,2048]{3,2,1,0:T(8,128)(2,1)}, bf16[2,2,256,512]{3,2,1,0:T(8,128)(2,1)}, bf16[2,2,256,512]{3,2,1,0:T(8,128)(2,1)}) custom-call(s32[2]{0:T(128)S(1)} %pad_add_fusion.which_ref, bf16[2,4,64,2048]{3,2,1,0:T(8,128)(2,1)} %get-tuple-element.108.refs_0_.refs_2_, ...), custom_call_target="tpu_custom_call" | custom-call | tf_op jit(solution)/shard_map/split/pallas_call | solution.py:250
  146.1 3.5 %collective-permute-done.4.refs_1_ = bf16[2,1,64,2048]{3,2,1,0:T(8,128)(2,1)S(1)} collective-permute-done((bf16[2,1,64,2048]{3,2,1,0:T(8,128)(2,1)S(1)}, bf16[2,1,64,2048]{3,2,1,0:T(8,128)(2,1)S(1)}, u32[]{:S(2)}, u32[]{:S(2)}) %collective-permute-start.4) | collective-permute-done | bytes 524320 | tf_op jit(solution)/shard_map/mid0_bit1/ppermute | solution.py:222
  150.8 5.5 %all-to-all-done.3.refs_1_ = bf16[4,2,4,32,384]{4,3,2,1,0:T(8,128)(2,1)} async-done(((bf16[4,2,4,32,384]{4,3,2,1,0:T(8,128)(2,1)}), bf16[4,2,4,32,384]{4,3,2,1,0:T(8,128)(2,1)}, u32[]{:S(2)}, u32[]{:S(2)}) %all-to-all-start.3) | async-done | bytes 786464 | tf_op jit(solution)/shard_map/z4/all_to_all | solution.py:216
  156.2 4.4 %all-to-all-start.4 = ((bf16[4,2,4,32,384]{4,3,2,1,0:T(8,128)(2,1)}), bf16[4,2,4,32,384]{4,3,2,1,0:T(8,128)(2,1)}, u32[]{:S(2)}, u32[]{:S(2)}) async-start(bf16[4,2,4,32,384]{4,3,2,1,0:T(8,128)(2,1)} %get-tuple-element.114), calls=%async_computation.4 | async-start | bytes 1572864 | tf_op jit(solution)/shard_map/z5/all_to_all | solution.py:216
  160.7 1.6 collective-permute-start.9
  162.2 1.5 collective-permute-start.10
  163.7 5.8 %leave_back.1 = (bf16[384,2048]{1,0:T(8,128)(2,1)}, bf16[4,4,64,512]{3,2,1,0:T(8,128)(2,1)S(1)}, bf16[4,4,64,512]{3,2,1,0:T(8,128)(2,1)S(1)}) custom-call(s32[1]{0:T(128)} %bitcast.where_ref, bf16[4,2,2,4,32,384]{5,4,3,2,1,0:T(8,128)(2,1)} %all-to-all-done.2.refs_0_, bf16[4,2,4,32,384]{4,3,2,1,0:T(8,128)(2,1)} %all-to-all-done.3.refs_1_, ...), custom_call_target="tpu_custom_call" | custom-call | tf_op jit(solution)/shard_map/leave_back/pallas_call | solution.py:185
  169.6 15.5 %collective-permute-done.9.refs_1_ = bf16[2,2,64,2048]{3,2,1,0:T(8,128)(2,1)S(1)} collective-permute-done((bf16[2,2,64,2048]{3,2,1,0:T(8,128)(2,1)}, bf16[2,2,64,2048]{3,2,1,0:T(8,128)(2,1)S(1)}, u32[]{:S(2)}, u32[]{:S(2)}) %collective-permute-start.9) | collective-permute-done | bytes 1048608 | tf_op jit(solution)/shard_map/mid1_bit0/ppermute | solution.py:222
  191.8 5.8 %leave_out.1 = (bf16[384,2048]{1,0:T(8,128)(2,1)}, bf16[4,4,64,512]{3,2,1,0:T(8,128)(2,1)S(1)}, bf16[4,4,64,512]{3,2,1,0:T(8,128)(2,1)S(1)}) custom-call(s32[1]{0:T(128)} %bitcast.where_ref, bf16[4,2,2,4,32,384]{5,4,3,2,1,0:T(8,128)(2,1)} %all-to-all-done.2.refs_0_, bf16[4,2,4,32,384]{4,3,2,1,0:T(8,128)(2,1)} %all-to-all-done.4.refs_1_, ...), custom_call_target="tpu_custom_call" | custom-call | tf_op jit(solution)/shard_map/leave_out/pallas_call | solution.py:185
  198.2 1.5 collective-permute-start.12
  201.7 5.0 %collective-permute-done.11.refs_1_ = bf16[2,2,64,512]{3,2,1,0:T(8,128)(2,1)S(1)} collective-permute-done((bf16[2,2,64,512]{3,2,1,0:T(8,128)(2,1)S(1)}, bf16[2,2,64,512]{3,2,1,0:T(8,128)(2,1)S(1)}, u32[]{:S(2)}, u32[]{:S(2)}) %collective-permute-start.11) | collective-permute-done | bytes 262176 | tf_op jit(solution)/shard_map/first_bit0/ppermute | solution.py:222
  208.8 1.6 collective-permute-start.16
  210.4 1.5 collective-permute-start.17
  211.9 6.7 %collective-permute-done.18.refs_3_ = bf16[2,1,64,2048]{3,2,1,0:T(8,128)(2,1)S(1)} collective-permute-done((bf16[2,1,64,2048]{3,2,1,0:T(8,128)(2,1)S(1)}, bf16[2,1,64,2048]{3,2,1,0:T(8,128)(2,1)S(1)}, u32[]{:S(2)}, u32[]{:S(2)}) %collective-permute-start.18) | collective-permute-done | bytes 524320 | tf_op jit(solution)/shard_map/mid1_bit1/ppermute | solution.py:222
  218.6 2.3 %finish.4 = (f32[4,64,2048]{2,1,0:T(8,128)}, f32[4,256,512]{2,1,0:T(8,128)}) custom-call(bf16[2,1,64,2048]{3,2,1,0:T(8,128)(2,1)S(1)} %get-tuple-element.140.refs_0_, bf16[2,1,64,2048]{3,2,1,0:T(8,128)(2,1)S(1)} %collective-permute-done.4.refs_1_, bf16[2,1,64,2048]{3,2,1,0:T(8,128)(2,1)S(1)} %get-tuple-element.142.refs_2_, ...), custom_call_target="tpu_custom_call" | custom-call | tf_op jit(solution)/shard_map/finish/pallas_call | solution.py:308
  221.0 1.6 collective-permute-start.13
  224.9 1.6 collective-permute-start.20
  229.9 1.6 collective-permute-done.21.refs_3_
  (69 shorter events, 25.2 us)
Async XLA Ops:
  51.0 40.5 %all-to-all-start.1 = ((bf16[4,2,2,4,32,384]{5,4,3,2,1,0:T(8,128)(2,1)}), bf16[4,2,2,4,32,384]{5,4,3,2,1,0:T(8,128)(2,1)}, u32[]{:S(2)}, u32[]{:S(2)}) async-start(bf16[4,2,2,4,32,384]{5,4,3,2,1,0:T(8,128)(2,1)} %get-tuple-element.84), calls=%async_computation.1 | async-start | bytes 3145728 | tf_op jit(solution)/shard_map/z2/all_to_all | solution.py:216
  74.3 21.8 %collective-permute-start = (bf16[2,4,64,2048]{3,2,1,0:T(8,128)(2,1)}, bf16[2,4,64,2048]{3,2,1,0:T(8,128)(2,1)S(1)}, u32[]{:S(2)}, u32[]{:S(2)}) collective-permute-start(bf16[2,4,64,2048]{3,2,1,0:T(8,128)(2,1)} %get-tuple-element.90), channel_id=1, source_target_pairs={{0,4},{4,0},{8,12},{12,8},{16,20},{20,16},{24,28},{28,24},{1,5},{5... | collective-permute-start | bytes 6291464 | tf_op jit(solution)/shard_map/mid0_core/ppermute | solution.py:222
  74.3 21.8 %collective-permute-start.1 = (bf16[2,4,256,512]{3,2,1,0:T(8,128)(2,1)}, bf16[2,4,256,512]{3,2,1,0:T(8,128)(2,1)}, u32[]{:S(2)}, u32[]{:S(2)}) collective-permute-start(bf16[2,4,256,512]{3,2,1,0:T(8,128)(2,1)} %get-tuple-element.92), channel_id=1, source_target_pairs={{0,4},{4,0},{8,12},{12,8},{16,20},{20,16},{24,28},{28,24},{1,5},{5... | collective-permute-start | bytes 6291464 | tf_op jit(solution)/shard_map/mid0_core/ppermute | solution.py:222
  91.5 40.9 %all-to-all-start.2 = ((bf16[4,2,2,4,32,384]{5,4,3,2,1,0:T(8,128)(2,1)}), bf16[4,2,2,4,32,384]{5,4,3,2,1,0:T(8,128)(2,1)}, u32[]{:S(2)}, u32[]{:S(2)}) async-start(bf16[4,2,2,4,32,384]{5,4,3,2,1,0:T(8,128)(2,1)} %get-tuple-element.87), calls=%async_computation.2 | async-start | bytes 3145728 | tf_op jit(solution)/shard_map/z3/all_to_all | solution.py:216
  103.9 24.4 %collective-permute-start.2 = (bf16[2,2,64,2048]{3,2,1,0:T(8,128)(2,1)}, bf16[2,2,64,2048]{3,2,1,0:T(8,128)(2,1)S(1)}, u32[]{:S(2)}, u32[]{:S(2)}) collective-permute-start(bf16[2,2,64,2048]{3,2,1,0:T(8,128)(2,1)} %get-tuple-element.93), channel_id=1, source_target_pairs={{0,8},{4,12},{8,0},{12,4},{16,24},{20,28},{24,16},{28,20},{1,9},{5... | collective-permute-start | bytes 3145736 | tf_op jit(solution)/shard_map/mid0_bit0/ppermute | solution.py:222
  105.5 24.6 %copy-start.2 = (bf16[2,2,64,2048]{3,2,1,0:T(8,128)(2,1)S(1)}, bf16[2,2,64,2048]{3,2,1,0:T(8,128)(2,1)}, u32[]{:S(2)}) copy-start(bf16[2,2,64,2048]{3,2,1,0:T(8,128)(2,1)} %get-tuple-element.97.refs_0_) | copy-start | bytes 3145732
  105.5 24.6 %copy-start.3 = (bf16[2,2,256,512]{3,2,1,0:T(8,128)(2,1)S(1)}, bf16[2,2,256,512]{3,2,1,0:T(8,128)(2,1)}, u32[]{:S(2)}) copy-start(bf16[2,2,256,512]{3,2,1,0:T(8,128)(2,1)} %get-tuple-element.101.refs_2_) | copy-start | bytes 3145732
  105.5 24.0 %collective-permute-start.3 = (bf16[2,2,256,512]{3,2,1,0:T(8,128)(2,1)}, bf16[2,2,256,512]{3,2,1,0:T(8,128)(2,1)S(1)}, u32[]{:S(2)}, u32[]{:S(2)}) collective-permute-start(bf16[2,2,256,512]{3,2,1,0:T(8,128)(2,1)} %get-tuple-element.94), channel_id=1, source_target_pairs={{0,16},{4,20},{8,24},{12,28},{16,0},{20,4},{24,8},{28,12},{1,17},{... | collective-permute-start | bytes 3145736 | tf_op jit(solution)/shard_map/mid0_bit1/ppermute | solution.py:222
  129.5 10.1 %collective-permute-start.6 = (bf16[2,4,64,2048]{3,2,1,0:T(8,128)(2,1)}, bf16[2,4,64,2048]{3,2,1,0:T(8,128)(2,1)}, u32[]{:S(2)}, u32[]{:S(2)}) collective-permute-start(bf16[2,4,64,2048]{3,2,1,0:T(8,128)(2,1)} %get-tuple-element.109), channel_id=1, source_target_pairs={{0,4},{4,0},{8,12},{12,8},{16,20},{20,16},{24,28},{28,24},{1,5},{5... | collective-permute-start | bytes 6291464 | tf_op jit(solution)/shard_map/mid1_core/ppermute | solution.py:222
  129.5 10.1 %collective-permute-start.7 = (bf16[2,4,256,512]{3,2,1,0:T(8,128)(2,1)}, bf16[2,4,256,512]{3,2,1,0:T(8,128)(2,1)}, u32[]{:S(2)}, u32[]{:S(2)}) collective-permute-start(bf16[2,4,256,512]{3,2,1,0:T(8,128)(2,1)} %get-tuple-element.111), channel_id=1, source_target_pairs={{0,4},{4,0},{8,12},{12,8},{16,20},{20,16},{24,28},{28,24},{1,5},{5... | collective-permute-start | bytes 6291464 | tf_op jit(solution)/shard_map/mid1_core/ppermute | solution.py:222
  132.4 23.8 %all-to-all-start.3 = ((bf16[4,2,4,32,384]{4,3,2,1,0:T(8,128)(2,1)}), bf16[4,2,4,32,384]{4,3,2,1,0:T(8,128)(2,1)}, u32[]{:S(2)}, u32[]{:S(2)}) async-start(bf16[4,2,4,32,384]{4,3,2,1,0:T(8,128)(2,1)} %get-tuple-element.106), calls=%async_computation.3 | async-start | bytes 1572864 | tf_op jit(solution)/shard_map/z4/all_to_all | solution.py:216
  136.6 12.9 %collective-permute-start.4 = (bf16[2,1,64,2048]{3,2,1,0:T(8,128)(2,1)S(1)}, bf16[2,1,64,2048]{3,2,1,0:T(8,128)(2,1)S(1)}, u32[]{:S(2)}, u32[]{:S(2)}) collective-permute-start(bf16[2,1,64,2048]{3,2,1,0:T(8,128)(2,1)S(1)} %get-tuple-element.103), channel_id=1, source_target_pairs={{0,16},{4,20},{8,24},{12,28},{16,0},{20,4},{24,8},{28,12},{1,17},{... | collective-permute-start | bytes 1572872 | tf_op jit(solution)/shard_map/mid0_bit1/ppermute | solution.py:222
  138.2 12.6 %collective-permute-start.5 = (bf16[2,1,256,512]{3,2,1,0:T(8,128)(2,1)S(1)}, bf16[2,1,256,512]{3,2,1,0:T(8,128)(2,1)S(1)}, u32[]{:S(2)}, u32[]{:S(2)}) collective-permute-start(bf16[2,1,256,512]{3,2,1,0:T(8,128)(2,1)S(1)} %get-tuple-element.104), channel_id=1, source_target_pairs={{0,8},{4,12},{8,0},{12,4},{16,24},{20,28},{24,16},{28,20},{1,9},{5... | collective-permute-start | bytes 1572872 | tf_op jit(solution)/shard_map/mid0_bit0/ppermute | solution.py:222
  156.2 35.5 %all-to-all-start.4 = ((bf16[4,2,4,32,384]{4,3,2,1,0:T(8,128)(2,1)}), bf16[4,2,4,32,384]{4,3,2,1,0:T(8,128)(2,1)}, u32[]{:S(2)}, u32[]{:S(2)}) async-start(bf16[4,2,4,32,384]{4,3,2,1,0:T(8,128)(2,1)} %get-tuple-element.114), calls=%async_computation.4 | async-start | bytes 1572864 | tf_op jit(solution)/shard_map/z5/all_to_all | solution.py:216
  160.7 24.4 %collective-permute-start.9 = (bf16[2,2,64,2048]{3,2,1,0:T(8,128)(2,1)}, bf16[2,2,64,2048]{3,2,1,0:T(8,128)(2,1)S(1)}, u32[]{:S(2)}, u32[]{:S(2)}) collective-permute-start(bf16[2,2,64,2048]{3,2,1,0:T(8,128)(2,1)} %get-tuple-element.112), channel_id=1, source_target_pairs={{0,8},{4,12},{8,0},{12,4},{16,24},{20,28},{24,16},{28,20},{1,9},{5... | collective-permute-start | bytes 3145736 | tf_op jit(solution)/shard_map/mid1_bit0/ppermute | solution.py:222
  162.2 24.0 %collective-permute-start.10 = (bf16[2,2,256,512]{3,2,1,0:T(8,128)(2,1)}, bf16[2,2,256,512]{3,2,1,0:T(8,128)(2,1)S(1)}, u32[]{:S(2)}, u32[]{:S(2)}) collective-permute-start(bf16[2,2,256,512]{3,2,1,0:T(8,128)(2,1)} %get-tuple-element.113), channel_id=1, source_target_pairs={{0,16},{4,20},{8,24},{12,28},{16,0},{20,4},{24,8},{28,12},{1,17},{... | collective-permute-start | bytes 3145736 | tf_op jit(solution)/shard_map/mid1_bit1/ppermute | solution.py:222
  163.7 22.5 %copy-start = (bf16[2,2,64,2048]{3,2,1,0:T(8,128)(2,1)S(1)}, bf16[2,2,64,2048]{3,2,1,0:T(8,128)(2,1)}, u32[]{:S(2)}) copy-start(bf16[2,2,64,2048]{3,2,1,0:T(8,128)(2,1)} %get-tuple-element.121.refs_0_) | copy-start | bytes 3145732
  163.7 22.5 %copy-start.1 = (bf16[2,2,256,512]{3,2,1,0:T(8,128)(2,1)S(1)}, bf16[2,2,256,512]{3,2,1,0:T(8,128)(2,1)}, u32[]{:S(2)}) copy-start(bf16[2,2,256,512]{3,2,1,0:T(8,128)(2,1)} %get-tuple-element.122.refs_2_) | copy-start | bytes 3145732
  169.6 19.3 %collective-permute-start.8 = (bf16[4,4,64,512]{3,2,1,0:T(8,128)(2,1)S(1)}, bf16[4,4,64,512]{3,2,1,0:T(8,128)(2,1)S(1)}, u32[]{:S(2)}, u32[]{:S(2)}) collective-permute-start(bf16[4,4,64,512]{3,2,1,0:T(8,128)(2,1)S(1)} %get-tuple-element.118), channel_id=1, source_target_pairs={{0,4},{4,0},{8,12},{12,8},{16,20},{20,16},{24,28},{28,24},{1,5},{5... | collective-permute-start | bytes 3145736 | tf_op jit(solution)/shard_map/first_core/ppermute | solution.py:222
  191.8 8.4 %copy-start.7 = (bf16[2,1,256,512]{3,2,1,0:T(8,128)(2,1)S(1)}, bf16[2,1,256,512]{3,2,1,0:T(8,128)(2,1)}, u32[]{:S(2)}) copy-start(bf16[2,1,256,512]{3,2,1,0:T(8,128)(2,1)} %copy-done.6) | copy-start | bytes 1572868
  191.8 15.6 %copy-start.5 = (bf16[2,2,64,512]{3,2,1,0:T(8,128)(2,1)S(1)}, bf16[2,2,64,512]{3,2,1,0:T(8,128)(2,1)}, u32[]{:S(2)}) copy-start(bf16[2,2,64,512]{3,2,1,0:T(8,128)(2,1)} %copy-done.4) | copy-start | bytes 786436
  197.6 10.4 %collective-permute-start.15 = (bf16[4,4,64,512]{3,2,1,0:T(8,128)(2,1)S(1)}, bf16[4,4,64,512]{3,2,1,0:T(8,128)(2,1)S(1)}, u32[]{:S(2)}, u32[]{:S(2)}) collective-permute-start(bf16[4,4,64,512]{3,2,1,0:T(8,128)(2,1)S(1)} %get-tuple-element.135), channel_id=1, source_target_pairs={{0,4},{4,0},{8,12},{12,8},{16,20},{20,16},{24,28},{28,24},{1,5},{5... | collective-permute-start | bytes 3145736 | tf_op jit(solution)/shard_map/fourth_core/ppermute | solution.py:222
  197.6 9.2 %collective-permute-start.11 = (bf16[2,2,64,512]{3,2,1,0:T(8,128)(2,1)S(1)}, bf16[2,2,64,512]{3,2,1,0:T(8,128)(2,1)S(1)}, u32[]{:S(2)}, u32[]{:S(2)}) collective-permute-start(bf16[2,2,64,512]{3,2,1,0:T(8,128)(2,1)S(1)} %copy-done.13), channel_id=1, source_target_pairs={{0,8},{4,12},{8,0},{12,4},{16,24},{20,28},{24,16},{28,20},{1,9},{5... | collective-permute-start | bytes 786440 | tf_op jit(solution)/shard_map/first_bit0/ppermute | solution.py:222
  198.2 9.1 %collective-permute-start.12 = (bf16[2,2,64,512]{3,2,1,0:T(8,128)(2,1)S(1)}, bf16[2,2,64,512]{3,2,1,0:T(8,128)(2,1)S(1)}, u32[]{:S(2)}, u32[]{:S(2)}) collective-permute-start(bf16[2,2,64,512]{3,2,1,0:T(8,128)(2,1)S(1)} %copy-done.11), channel_id=1, source_target_pairs={{0,16},{4,20},{8,24},{12,28},{16,0},{20,4},{24,8},{28,12},{1,17},{... | collective-permute-start | bytes 786440 | tf_op jit(solution)/shard_map/first_bit1/ppermute | solution.py:222
  199.8 18.8 %collective-permute-start.18 = (bf16[2,1,64,2048]{3,2,1,0:T(8,128)(2,1)S(1)}, bf16[2,1,64,2048]{3,2,1,0:T(8,128)(2,1)S(1)}, u32[]{:S(2)}, u32[]{:S(2)}) collective-permute-start(bf16[2,1,64,2048]{3,2,1,0:T(8,128)(2,1)S(1)} %copy-done.9), channel_id=1, source_target_pairs={{0,16},{4,20},{8,24},{12,28},{16,0},{20,4},{24,8},{28,12},{1,17},{... | collective-permute-start | bytes 1572872 | tf_op jit(solution)/shard_map/mid1_bit1/ppermute | solution.py:222
  200.2 18.4 %collective-permute-start.19 = (bf16[2,1,256,512]{3,2,1,0:T(8,128)(2,1)S(1)}, bf16[2,1,256,512]{3,2,1,0:T(8,128)(2,1)S(1)}, u32[]{:S(2)}, u32[]{:S(2)}) collective-permute-start(bf16[2,1,256,512]{3,2,1,0:T(8,128)(2,1)S(1)} %copy-done.7), channel_id=1, source_target_pairs={{0,8},{4,12},{8,0},{12,4},{16,24},{20,28},{24,16},{28,20},{1,9},{5... | collective-permute-start | bytes 1572872 | tf_op jit(solution)/shard_map/mid1_bit0/ppermute | solution.py:222
  208.8 15.1 %collective-permute-start.16 = (bf16[2,2,64,512]{3,2,1,0:T(8,128)(2,1)S(1)}, bf16[2,2,64,512]{3,2,1,0:T(8,128)(2,1)S(1)}, u32[]{:S(2)}, u32[]{:S(2)}) collective-permute-start(bf16[2,2,64,512]{3,2,1,0:T(8,128)(2,1)S(1)} %get-tuple-element.138), channel_id=1, source_target_pairs={{0,8},{4,12},{8,0},{12,4},{16,24},{20,28},{24,16},{28,20},{1,9},{5... | collective-permute-start | bytes 786440 | tf_op jit(solution)/shard_map/fourth_bit0/ppermute | solution.py:222
  210.4 13.8 %collective-permute-start.17 = (bf16[2,2,64,512]{3,2,1,0:T(8,128)(2,1)S(1)}, bf16[2,2,64,512]{3,2,1,0:T(8,128)(2,1)S(1)}, u32[]{:S(2)}, u32[]{:S(2)}) collective-permute-start(bf16[2,2,64,512]{3,2,1,0:T(8,128)(2,1)S(1)} %get-tuple-element.139), channel_id=1, source_target_pairs={{0,16},{4,20},{8,24},{12,28},{16,0},{20,4},{24,8},{28,12},{1,17},{... | collective-permute-start | bytes 786440 | tf_op jit(solution)/shard_map/fourth_bit1/ppermute | solution.py:222
  221.0 7.0 %collective-permute-start.13 = (bf16[2,1,64,512]{3,2,1,0:T(8,128)(2,1)S(1)}, bf16[2,1,64,512]{3,2,1,0:T(8,128)(2,1)S(1)}, u32[]{:S(2)}, u32[]{:S(2)}) collective-permute-start(bf16[2,1,64,512]{3,2,1,0:T(8,128)(2,1)S(1)} %get-tuple-element.131), channel_id=1, source_target_pairs={{0,16},{4,20},{8,24},{12,28},{16,0},{20,4},{24,8},{28,12},{1,17},{... | collective-permute-start | bytes 393224 | tf_op jit(solution)/shard_map/first_bit1/ppermute | solution.py:222
  222.5 5.5 %collective-permute-start.14 = (bf16[2,1,64,512]{3,2,1,0:T(8,128)(2,1)S(1)}, bf16[2,1,64,512]{3,2,1,0:T(8,128)(2,1)S(1)}, u32[]{:S(2)}, u32[]{:S(2)}) collective-permute-start(bf16[2,1,64,512]{3,2,1,0:T(8,128)(2,1)S(1)} %get-tuple-element.133), channel_id=1, source_target_pairs={{0,8},{4,12},{8,0},{12,4},{16,24},{20,28},{24,16},{28,20},{1,9},{5... | collective-permute-start | bytes 393224 | tf_op jit(solution)/shard_map/first_bit0/ppermute | solution.py:222
  224.9 5.0 %collective-permute-start.20 = (bf16[2,1,64,512]{3,2,1,0:T(8,128)(2,1)S(1)}, bf16[2,1,64,512]{3,2,1,0:T(8,128)(2,1)S(1)}, u32[]{:S(2)}, u32[]{:S(2)}) collective-permute-start(bf16[2,1,64,512]{3,2,1,0:T(8,128)(2,1)S(1)} %get-tuple-element.155), channel_id=1, source_target_pairs={{0,16},{4,20},{8,24},{12,28},{16,0},{20,4},{24,8},{28,12},{1,17},{... | collective-permute-start | bytes 393224 | tf_op jit(solution)/shard_map/fourth_bit1/ppermute | solution.py:222
  226.5 5.0 %collective-permute-start.21 = (bf16[2,1,64,512]{3,2,1,0:T(8,128)(2,1)S(1)}, bf16[2,1,64,512]{3,2,1,0:T(8,128)(2,1)S(1)}, u32[]{:S(2)}, u32[]{:S(2)}) collective-permute-start(bf16[2,1,64,512]{3,2,1,0:T(8,128)(2,1)S(1)} %get-tuple-element.157), channel_id=1, source_target_pairs={{0,8},{4,12},{8,0},{12,4},{16,24},{20,28},{24,16},{28,20},{1,9},{5... | collective-permute-start | bytes 393224 | tf_op jit(solution)/shard_map/fourth_bit0/ppermute | solution.py:222
  (9 other events, 25.2 us)

commit v3 on v2

--- a/solution.py
+++ b/solution.py
@@ -46,12 +46,9 @@
 
 def enter(tokens, up_first, cotangent, down_second, sizes):
     T, L, BS, NT, G, SW, Q, _ = sizes
-    rows = BS // (2 * Q)
-
-    def kernel(x_ref, w_ref, g_ref, d_ref, xt_ref, *outs):
-        turned = x_ref[...].T
-        xt_ref[0] = turned.reshape(Q, 2, rows, T)
-        up = dot(w_ref[0], turned, 0, 0).astype(BF16).reshape(NT, L, SW, T)
+
+    def kernel(x_ref, w_ref, g_ref, d_ref, *outs):
+        up = dot(x_ref[...], w_ref[0], 1, 0).astype(BF16).T.reshape(NT, L, SW, T)
         back = dot(d_ref[0], g_ref[...], 1, 1).astype(BF16).reshape(NT, L, SW, T)
         for chunk in range(N_CHUNK):
             outs[chunk][:, 0, :, 0] = up[:, chunk * G : (chunk + 1) * G]
@@ -64,28 +61,42 @@
         name="enter",
         grid=(L,),
         in_specs=[cols, square, cols, square],
-        out_specs=[spec((1, Q, 2, rows, T), lambda b: (b, 0, 0, 0, 0))]
-        + [spec((NT, 2, G, 1, SW, T), lambda b: (0, 0, 0, b, 0, 0))] * N_CHUNK,
-        out_shape=[pltpu.HBM((L, Q, 2, rows, T), BF16)]
-        + [pltpu.HBM((NT, 2, G, L, SW, T), BF16)] * N_CHUNK,
+        out_specs=[spec((NT, 2, G, 1, SW, T), lambda b: (0, 0, 0, b, 0, 0))] * N_CHUNK,
+        out_shape=[pltpu.HBM((NT, 2, G, L, SW, T), BF16)] * N_CHUNK,
         compiler_params=params(56),
         cost_estimate=LIGHT,
     )(*held(tokens, up_first, cotangent, down_second))
-    return outs[0], outs[1:]
+    return outs
+
+
+def turn(tokens, sizes):
+    T, L, BS, _, _, _, Q, _ = sizes
+    rows = BS // (2 * Q)
+
+    def kernel(x_ref, out_ref):
+        out_ref[0] = x_ref[...].T.reshape(Q, 2, rows, T)
+
+    return pl.pallas_call(
+        kernel,
+        name="turn",
+        grid=(L,),
+        in_specs=[spec((T, BS), lambda b: (0, b))],
+        out_specs=spec((1, Q, 2, rows, T), lambda b: (b, 0, 0, 0, 0)),
+        out_shape=pltpu.HBM((L, Q, 2, rows, T), BF16),
+        compiler_params=params(56),
+        cost_estimate=LIGHT,
+    )(*held(tokens))
 
 
 def middle(where, received, up_second, down_first, chunk, scale, sizes, joint):
     T, L, BS, NT, G, SW, Q, HB = sizes
     rows_up, rows_down = BS // (2 * Q), HB // (2 * Q)
+    cut = max(L // 4, 1)
     tile = min(512, HB)
 
     def kernel(where_ref, *refs):
         in_ref, up_ref, down_ref = refs[:3]
         up_send, up_keep, down_send, down_keep, rs_scr, act_scr, at_scr, gp_scr = refs[-8:]
-        if joint:
-            down_out, back_out = refs[3].at[:, 0], refs[3].at[:, 1]
-        else:
-            down_out, back_out = refs[3:5]
         core = where_ref[0]
         regrouped = in_ref[:, 0, 0].reshape(BS, T)
         rs_scr[...] = regrouped.reshape(Q, 2, rows_up, T)
@@ -101,8 +112,15 @@
             gp_scr[:, start : start + tile] = (grad_act * slope).astype(BF16)
         activated = act_scr[...]
         grad_pre = gp_scr[...]
-        down_out[:, 0] = dot(activated, down_ref[0], 1, 0).astype(BF16).T.reshape(NT, L, SW, T)
-        back_out[:, 0] = dot(grad_pre, up_ref[0], 1, 1).astype(BF16).T.reshape(NT, L, SW, T)
+        down = dot(activated, down_ref[0], 1, 0).astype(BF16).T.reshape(NT, L, SW, T)
+        back = dot(grad_pre, up_ref[0], 1, 1).astype(BF16).T.reshape(NT, L, SW, T)
+        if joint:
+            refs[3][:, 0, :L] = back
+            refs[3][:, 0, L:] = down
+        else:
+            refs[3][:, 0, :L] = back
+            refs[3][:, 0, L:] = down[:, :cut]
+            refs[4][:, 0] = down[:, cut:]
         for send, ref in ((True, up_send), (False, up_keep)):
             half = rs_scr[:, 1 - core if send else core].reshape(Q * rows_up, T)
             part = scale * dot(half, grad_pre, 1, 0)
@@ -114,12 +132,9 @@
                 ref[0, q] = (scale * dot(half, grad_mid, 1, 0)).astype(BF16)
 
     base = chunk * G
-    if joint:
-        pieces = [pltpu.HBM((NT, 2, G, L, SW, T), BF16)]
-        piece_specs = [spec((NT, 2, 1, L, SW, T), lambda g, s: (0, 0, g, 0, 0, 0))]
-    else:
-        pieces = [pltpu.HBM((NT, G, L, SW, T), BF16)] * 2
-        piece_specs = [spec((NT, 1, L, SW, T), lambda g, s: (0, g, 0, 0, 0))] * 2
+    widths = [2 * L] if joint else [L + cut, L - cut]
+    pieces = [pltpu.HBM((NT, G, w, SW, T), BF16) for w in widths]
+    piece_specs = [spec((NT, 1, w, SW, T), lambda g, s: (0, g, 0, 0, 0)) for w in widths]
     up_part = pltpu.HBM((G, Q, rows_up, HB), BF16)
     down_part = pltpu.HBM((G, Q, rows_down, BS), BF16)
     outs = pl.pallas_call(
@@ -150,15 +165,15 @@
     return outs[:-4], outs[-4:-2], outs[-2:]
 
 
-def leave(where, received, weight, base_rows, left, scale, sizes, backward):
+def leave(where, received, places, weight, base_rows, left, scale, sizes, backward, first, count, onto=None):
     T, L, BS, NT, G, SW, Q, _ = sizes
     rows = BS // (2 * Q)
 
     def kernel(where_ref, *refs):
         ins, (w_ref, base_ref, left_ref) = refs[:N_CHUNK], refs[N_CHUNK : N_CHUNK + 3]
-        out_ref, send_ref, keep_ref, scr, slab_scr = refs[N_CHUNK + 3 :]
+        out_ref, send_ref, keep_ref, scr, slab_scr = refs[-5:]
         core = where_ref[0]
-        scr[:, 0] = ins[0][:, 0, :, 0]
+        scr[:, 0] = ins[0][:, :, 0]
         scr[:, 1] = ins[1][:, :, 0]
         regrouped = scr[...].reshape(BS, T)
         if backward:
@@ -177,24 +192,26 @@
                 part = dot(half, left_ref[...], 1, 0)
             ref[0] = (scale * part).astype(BF16).reshape(Q, rows, BS)
 
-    side = 1 if backward else 0
-    cols = spec((T, BS), lambda b, s: (0, b))
-    part = jax.ShapeDtypeStruct((L, Q, rows, BS), BF16)
+    cols = spec((T, BS), lambda b, s: (0, first + b))
+    part = jax.ShapeDtypeStruct((count, Q, rows, BS), BF16)
     part_spec = spec((1, Q, rows, BS), lambda b, s: (b, 0, 0, 0))
-    left_spec = spec((1, Q, 2, rows, T), lambda b, s: (b, 0, 0, 0, 0)) if backward else cols
+    left_spec = spec((1, Q, 2, rows, T), lambda b, s: (first + b, 0, 0, 0, 0)) if backward else cols
+    operands = held(*received, weight, base_rows, left)
+    more, aliases = [], {}
+    if onto is not None:
+        operands += held(onto)
+        more, aliases = [pl.BlockSpec(memory_space=pl.ANY)], {N_CHUNK + 4: 0}
     return pl.pallas_call(
         kernel,
         name="leave_back" if backward else "leave_out",
         grid_spec=pltpu.PrefetchScalarGridSpec(
             num_scalar_prefetch=1,
-            grid=(L,),
+            grid=(count,),
             in_specs=[
-                spec((NT, 1, G, 1, SW, T), lambda b, s: (0, side, 0, b, 0, 0)),
-                spec((NT, G, 1, SW, T), lambda b, s: (0, 0, b, 0, 0)),
-                spec((1, BS, BS), lambda b, s: (b, 0, 0)),
-                cols,
-                left_spec,
-            ],
+                spec((NT, G, 1, SW, T), lambda b, s, place=place: (0, 0, place + b, 0, 0)) for place in places
+            ]
+            + [spec((1, BS, BS), lambda b, s: (first + b, 0, 0)), cols, left_spec]
+            + more,
             out_specs=[cols, part_spec, part_spec],
             scratch_shapes=[
                 pltpu.VMEM((NT, N_CHUNK, G, SW, T), BF16),
@@ -202,9 +219,10 @@
             ],
         ),
         out_shape=[pltpu.HBM((T, L * BS), BF16), part, part],
+        input_output_aliases=aliases,
         compiler_params=params(24),
         cost_estimate=LIGHT,
-    )(where, *held(*received, weight, base_rows, left))
+    )(where, *operands)
 
 
 def together(*values):
@@ -295,33 +313,35 @@
 
 
 def finish(groups):
-    n = len(groups)
-    lead = groups[0][0].shape[0]
+    shapes = [(sum(keep.shape[0] for keep, _ in pairs),) + pairs[0][0].shape[2:] for pairs in groups]
+    n_in = sum(2 * len(pairs) for pairs in groups)
 
     def kernel(*refs):
-        ins, outs = refs[: 4 * n], refs[4 * n :]
-        for i in range(n):
-            for j in range(2):
-                a, b = ins[4 * i + 2 * j], ins[4 * i + 2 * j + 1]
-                outs[i][j * lead : (j + 1) * lead] = a[:, 0].astype(F32) + b[:, 0].astype(F32)
+        ins, outs = list(refs[:n_in]), refs[n_in:]
+        for pairs, out in zip(groups, outs):
+            start = 0
+            for keep, _ in pairs:
+                a, b = ins.pop(0), ins.pop(0)
+                out[start : start + keep.shape[0]] = a[:, 0].astype(F32) + b[:, 0].astype(F32)
+                start += keep.shape[0]
 
     return pl.pallas_call(
         kernel,
         name="finish",
-        in_specs=[whole()] * (4 * n),
-        out_shape=[jax.ShapeDtypeStruct((2 * lead,) + group[0].shape[2:], F32) for group in groups],
+        in_specs=[whole()] * n_in,
+        out_shape=[jax.ShapeDtypeStruct(shape, F32) for shape in shapes],
         compiler_params=params(16),
         cost_estimate=LIGHT,
-    )(*[array for group in groups for array in group])
+    )(*[array for pairs in groups for pair in pairs for array in pair])
 
 
 class Halving:
-    def __init__(self, streams, label, large):
+    def __init__(self, streams, label, large, turned=0):
         self.label = label
         self.large = large
         self.bits = bits = (lax.axis_size("dp") // 2).bit_length() - 1
-        self.orders = [list(range(bits)), list(range(bits))[::-1]]
-        self.held = [list(range(bits)), list(range(bits))]
+        self.orders = [list(range(bits))[:: -1 if (i + turned) % 2 else 1] for i in range(len(streams))]
+        self.held = [list(range(bits)) for _ in streams]
         self.streams = streams
 
     def add(self, lead):
@@ -370,6 +390,8 @@
     where = (lax.axis_index("dp") % 2).astype(jnp.int32).reshape(1)
 
     lead = L // N_CHUNK
+    half = L // 2
+    cut = max(L // 4, 1)
 
     def middle_sums(parts, label, before):
         (up_send, up_keep), (down_send, down_keep) = parts
@@ -379,63 +401,92 @@
         got_up, got_down = swap(up_send, 0, label + "_core"), swap(down_send, 0, label + "_core")
         return Halving([(up_keep, got_up, 0), (down_keep, got_down, 0)], label, True)
 
-    def edge_sums(parts, label):
-        send, keep = parts
-        got = swap(send, 0, label + "_core")
-        return Halving([(keep, got, 0), (keep, got, lead)], label, False)
-
-    x_turned, (first_0, first_1) = enter(tokens, up_first, cotangent, down_second, sizes)
+    first_0, first_1 = enter(tokens, up_first, cotangent, down_second, sizes)
     in_0 = regroup(first_0, "z1")
-    in_0, first_1 = together(in_0, first_1)
+    x_turned = turn(tokens, sizes)
+    in_0, first_1, x_turned = together(in_0, first_1, x_turned)
     in_1 = regroup(first_1, "z2")
     (both_0,), *parts = middle(where, in_0, up_second, down_first, 0, scale, sizes, True)
     mid_0 = middle_sums(parts, "mid0", None)
     leaving_0 = mid_0.add(lead)
-    in_1, both_0 = together(in_1, both_0)
+    in_1, both_0, *_ = together(in_1, both_0, *leaving_0)
     both_0 = regroup(both_0, "z3")
     mid_0.move(leaving_0)
-    in_1, *_ = together(in_1, *leaving_0)
-    (down_1, back_1), *parts = middle(where, in_1, up_second, down_first, 1, scale, sizes, False)
+    (most_1, rest_1), *parts = middle(where, in_1, up_second, down_first, 1, scale, sizes, False)
     mid_1 = middle_sums(parts, "mid1", mid_0)
     leaving_0 = mid_0.add(lead)
+    both_0, most_1, *_ = together(both_0, most_1, *leaving_0)
+    most_1 = regroup(most_1, "z4")
+    mid_0.move(leaving_0)
+    got = together(*mid_0.got(), *mid_1.got())
+    mid_0.replace(got[:2])
+    mid_1.replace(got[2:])
     leaving_1 = mid_1.add(lead)
-    both_0, back_1, *_ = together(both_0, back_1, *leaving_0)
-    back_1 = regroup(back_1, "z4")
-    mid_0.move(leaving_0)
     mid_1.move(leaving_1)
-    back_1, down_1, *got = together(back_1, down_1, *mid_0.got(), *leaving_1)
-    mid_0.replace(got[:2])
-    down_1 = regroup(down_1, "z5")
-    grad_tokens, *parts = leave(
-        where, (both_0, back_1), up_first, cotangent, x_turned, scale, sizes, True
+    most_1, rest_1, *_ = together(most_1, rest_1, *leaving_1)
+    rest_1 = regroup(rest_1, "z5")
+    grad_tokens, parts = None, []
+    for start, count in ((0, half), (half, L - half)):
+        grad_tokens, *part = leave(
+            where,
+            (both_0, most_1),
+            (start, start),
+            up_first,
+            cotangent,
+            x_turned,
+            scale,
+            sizes,
+            True,
+            start,
+            count,
+            grad_tokens,
+        )
+        parts.append(part)
+    edge_first = Halving([(keep, swap(send, 0, "first_core"), 0) for send, keep in parts], "first", False)
+    layer_out, *low = leave(
+        where, (both_0, most_1), (L, L), down_second, tokens, cotangent, scale, sizes, False, 0, cut
     )
-    edge_first = edge_sums(parts, "first")
+    edge_low = Halving([(low[1], swap(low[0], 0, "low_core"), 0)], "low", False)
     leaving_first = edge_first.add(lead)
+    leaving_low = edge_low.add(cut)
     leaving_1 = mid_1.add(lead) if mid_1.orders[0] else []
     edge_first.move(leaving_first)
+    edge_low.move(leaving_low)
     mid_1.move(leaving_1)
-    down_1, *_ = together(down_1, *leaving_first, *leaving_1)
-    layer_out, *parts = leave(
-        where, (both_0, down_1), down_second, tokens, cotangent, scale, sizes, False
+    rest_1, *_ = together(rest_1, *leaving_first, *leaving_low, *leaving_1)
+    layer_out, *high = leave(
+        where,
+        (both_0, rest_1),
+        (L + cut, 0),
+        down_second,
+        tokens,
+        cotangent,
+        scale,
+        sizes,
+        False,
+        cut,
+        L - cut,
+        layer_out,
     )
-    edge_fourth = edge_sums(parts, "fourth")
+    high[0], *got = together(high[0], *edge_first.got(), *edge_low.got())
+    edge_first.replace(got[:2])
+    edge_low.replace(got[2:])
+    edge_high = Halving([(high[1], swap(high[0], 0, "high_core"), 0)], "high", False, 1)
+    edge_high.move(edge_high.add(L - cut))
     done_0, done_1 = mid_0.run(lead), mid_1.run(lead)
-    leaving_first = edge_first.add(lead)
-    edge_fourth.replace(together(*edge_fourth.got(), *leaving_first)[:2])
-    edge_first.move(leaving_first)
-    leaving_fourth = edge_fourth.add(lead)
-    edge_fourth.move(leaving_fourth)
-    grad_up_second, grad_down_first = finish([done_0[0] + done_1[0], done_0[1] + done_1[1]])
-    (grad_up_first,) = finish([sum(edge_first.run(lead), ())])
-    got = together(*edge_fourth.got(), grad_up_second, grad_down_first)
-    edge_fourth.replace(got[:2])
-    (grad_down_second,) = finish([sum(edge_fourth.run(lead), ())])
+    grad_up_second, grad_down_first = finish([[done_0[0], done_1[0]], [done_0[1], done_1[1]]])
+    done_first, done_low = edge_first.run(lead), edge_low.run(cut)
+    got = together(*edge_high.got(), grad_up_second, grad_down_first)
+    edge_high.replace(got[:1])
+    done_high = edge_high.run(L - cut)
+    (grad_up_first,) = finish([done_first])
+    (grad_down_second,) = finish([done_low + done_high])
     return (
         layer_out,
         grad_tokens,
         grad_up_first.reshape(L, -1, BS),
-        got[2].reshape(L, -1, HB),
-        got[3].reshape(L, -1, BS),
+        got[-2].reshape(L, -1, HB),
+        got[-1].reshape(L, -1, BS),
         grad_down_second.reshape(L, -1, BS),
     )
 

time: 233 us -> 228 us (0.979)
  blocking collectives: 43.4 us -> 0 us
  waiting for transfers between devices: 63.5 us -> 89.5 us
  Pallas kernels: 78.3 us -> 86.2 us
  starting transfers between devices: 41.1 us -> 44.9 us
    all_to_all x1 -> x0, blocking collectives: 43.4 us -> none  [regroup(): lax.all_to_all(pieces, 'tensor', split_axis=0, concat_axis=0, tiled=True)]
    all_to_all x4 -> x5, waiting for transfers between devices: 23.4 us -> 45.6 us  [regroup(): lax.all_to_all(pieces, 'tensor', split_axis=0, concat_axis=0, tiled=True)]
    all_to_all x4 -> x5, starting transfers between devices: 17.5 us -> 24.1 us  [regroup(): lax.all_to_all(pieces, 'tensor', split_axis=0, concat_axis=0, tiled=True)]
    ppermute x22 -> x24, waiting for transfers between devices: 40.1 us -> 44 us  [swap(): return lax.ppermute(value, 'dp', [(s, s ^ 1 << bit) for s in range(count)])]
    pallas_call x3 -> x4, Pallas kernels: 4.04 us -> 7.89 us  [the longest x3 4.04 us: finish(): pl.pallas_call(kernel, name='finish', in_specs=[whole()] * n_in, out_shap...]
    pallas_call x2 -> x4, Pallas kernels: 11.6 us -> 14.6 us  [leave(): pl.pallas_call(kernel, name='leave_back' if backward else 'leave_out', gr...]
    ppermute x22 -> x24, starting transfers between devices: 23.6 us -> 20.8 us  [swap(): return lax.ppermute(value, 'dp', [(s, s ^ 1 << bit) for s in range(count)])]
    pallas_call x6 -> x8, Pallas kernels: 4.94 us -> 6.61 us  [split_small(): pl.pallas_call(kernel, name='small', in_specs=[pl.BlockSpec(memory_space=...]
  transfers between devices with their start and end apart: 26 -> 29, of which waited for: 15 -> 17; matrix products, arithmetic and copies ran while one was open for 0% -> 0% of each run, Pallas kernels for 28% -> 35%
where the time goes in v3:
time: 228 us; the launch traced here: 227 us
  waiting for transfers between devices  89.5 us (39%)
  Pallas kernels  86.2 us (38%)
  starting transfers between devices  44.9 us (20%)
  local copies, waits for them, and re-layouts  5.39 us (2%)
    all_to_all x5, waiting for transfers between devices, regroup(): lax.all_to_all(pieces, 'tensor', split_axis=0, concat_axis=0, tiled=True)  45.6 us
    ppermute x24, waiting for transfers between devices, swap(): return lax.ppermute(value, 'dp', [(s, s ^ 1 << bit) for s in range(count)])  44 us
    pallas_call x2, Pallas kernels, middle(): pl.pallas_call(kernel, name='middle', grid_spec=pltpu.PrefetchScalarGridS...  37.9 us
    all_to_all x5, starting transfers between devices, regroup(): lax.all_to_all(pieces, 'tensor', split_axis=0, concat_axis=0, tiled=True)  24.1 us
    ppermute x24, starting transfers between devices, swap(): return lax.ppermute(value, 'dp', [(s, s ^ 1 << bit) for s in range(count)])  20.8 us
    pallas_call x4, Pallas kernels, leave(): pl.pallas_call(kernel, name='leave_back' if backward else 'leave_out', gr...  14.6 us
    pallas_call x2, Pallas kernels, split(): pl.pallas_call(kernel, name='split', grid_spec=pltpu.PrefetchScalarGridSp...  12.8 us
    pallas_call x8, Pallas kernels, split_small(): pl.pallas_call(kernel, name='small', in_specs=[pl.BlockSpec(memory_space=...  6.61 us
  transfers between devices with their start and end apart: 29, of which 17 were waited for; matrix products, arithmetic and copies ran while one was open for 0% of the time, Pallas kernels for 35%

profile of v3, /device:TPU:0, one launch (start us, length us, event | category | flops | bytes accessed | tf_op | source)
XLA Modules:
  0.0 227.0 jit_solution(17175091313808440644)
XLA Ops:
  0.6 6.3 %enter.1 = (bf16[4,2,2,4,32,384]{5,4,3,2,1,0:T(8,128)(2,1)}, bf16[4,2,2,4,32,384]{5,4,3,2,1,0:T(8,128)(2,1)}) custom-call(bf16[384,2048]{1,0:T(8,128)(2,1)} %refs_3_.7, bf16[4,512,512]{2,1,0:T(8,128)(2,1)} %refs_2_.9, bf16[384,2048]{1,0:T(8,128)(2,1)} %refs_4_.3, bf16[4,512,512]{2,1,0:T(8,128)(2,1)} %refs_2_.11), custom_call_target="tpu_custom_call" | custom-call | tf_op jit(solution)/shard_map/enter/pallas_call | solution.py:59
  7.0 6.3 %all-to-all-start = ((bf16[4,2,2,4,32,384]{5,4,3,2,1,0:T(8,128)(2,1)}), bf16[4,2,2,4,32,384]{5,4,3,2,1,0:T(8,128)(2,1)S(1)}, u32[]{:S(2)}, u32[]{:S(2)}) async-start(bf16[4,2,2,4,32,384]{5,4,3,2,1,0:T(8,128)(2,1)} %get-tuple-element.90), calls=%async_computation | async-start | bytes 3145728 | tf_op jit(solution)/shard_map/z1/all_to_all | solution.py:234
  13.3 3.8 %turn.1.refs_4_ = bf16[4,4,2,64,384]{4,3,2,1,0:T(8,128)(2,1)} custom-call(bf16[384,2048]{1,0:T(8,128)(2,1)} %refs_3_.7), custom_call_target="tpu_custom_call" | custom-call | tf_op jit(solution)/shard_map/turn/pallas_call | solution.py:79
  17.1 33.1 %all-to-all-done.refs_0_ = bf16[4,2,2,4,32,384]{5,4,3,2,1,0:T(8,128)(2,1)S(1)} async-done(((bf16[4,2,2,4,32,384]{5,4,3,2,1,0:T(8,128)(2,1)}), bf16[4,2,2,4,32,384]{5,4,3,2,1,0:T(8,128)(2,1)S(1)}, u32[]{:S(2)}, u32[]{:S(2)}) %all-to-all-start) | async-done | bytes 1572896 | tf_op jit(solution)/shard_map/z1/all_to_all | solution.py:234
  50.3 4.3 %all-to-all-start.1 = ((bf16[4,2,2,4,32,384]{5,4,3,2,1,0:T(8,128)(2,1)}), bf16[4,2,2,4,32,384]{5,4,3,2,1,0:T(8,128)(2,1)}, u32[]{:S(2)}, u32[]{:S(2)}) async-start(bf16[4,2,2,4,32,384]{5,4,3,2,1,0:T(8,128)(2,1)} %get-tuple-element.92), calls=%async_computation.1 | async-start | bytes 3145728 | tf_op jit(solution)/shard_map/z2/all_to_all | solution.py:234
  54.6 19.0 %middle.2 = (bf16[4,2,8,32,384]{4,3,2,1,0:T(8,128)(2,1)}, bf16[2,4,64,2048]{3,2,1,0:T(8,128)(2,1)}, bf16[2,4,64,2048]{3,2,1,0:T(8,128)(2,1)}, bf16[2,4,256,512]{3,2,1,0:T(8,128)(2,1)}, bf16[2,4,256,512]{3,2,1,0:T(8,128)(2,1)}) custom-call(s32[1]{0:T(128)} %bitcast.where_ref, bf16[4,2,2,4,32,384]{5,4,3,2,1,0:T(8,128)(2,1)} %copy-done.19, ...), custom_call_target="tpu_custom_call" | custom-call | tf_op jit(solution)/shard_map/middle/pallas_call | solution.py:140
  74.2 6.1 %collective-permute-done.refs_1_.refs_3_ = bf16[2,4,64,2048]{3,2,1,0:T(8,128)(2,1)S(1)} collective-permute-done((bf16[2,4,64,2048]{3,2,1,0:T(8,128)(2,1)}, bf16[2,4,64,2048]{3,2,1,0:T(8,128)(2,1)S(1)}, u32[]{:S(2)}, u32[]{:S(2)}) %collective-permute-start) | collective-permute-done | bytes 2097184 | tf_op jit(solution)/shard_map/mid0_core/ppermute | solution.py:240
  81.6 6.4 %split.2 = (bf16[2,2,64,2048]{3,2,1,0:T(8,128)(2,1)}, bf16[2,2,64,2048]{3,2,1,0:T(8,128)(2,1)}, bf16[2,2,256,512]{3,2,1,0:T(8,128)(2,1)}, bf16[2,2,256,512]{3,2,1,0:T(8,128)(2,1)}) custom-call(s32[2]{0:T(128)S(1)} %get-tuple-element.174.which_ref, bf16[2,4,64,2048]{3,2,1,0:T(8,128)(2,1)} %get-tuple-element.95.refs_0_.refs_2_, ...), custom_call_target="tpu_custom_call" | custom-call | tf_op jit(solution)/shard_map/split/pallas_call | solution.py:268
  88.0 3.1 %all-to-all-done.1.refs_0_ = bf16[4,2,2,4,32,384]{5,4,3,2,1,0:T(8,128)(2,1)} async-done(((bf16[4,2,2,4,32,384]{5,4,3,2,1,0:T(8,128)(2,1)}), bf16[4,2,2,4,32,384]{5,4,3,2,1,0:T(8,128)(2,1)}, u32[]{:S(2)}, u32[]{:S(2)}) %all-to-all-start.1) | async-done | bytes 1572896 | tf_op jit(solution)/shard_map/z2/all_to_all | solution.py:234
  91.1 4.5 %all-to-all-start.2 = ((bf16[4,2,8,32,384]{4,3,2,1,0:T(8,128)(2,1)}), bf16[4,2,8,32,384]{4,3,2,1,0:T(8,128)(2,1)}, u32[]{:S(2)}, u32[]{:S(2)}) async-start(bf16[4,2,8,32,384]{4,3,2,1,0:T(8,128)(2,1)} %get-tuple-element.101), calls=%async_computation.2 | async-start | bytes 3145728 | tf_op jit(solution)/shard_map/z3/all_to_all | solution.py:234
  95.7 1.6 collective-permute-start.2
  97.2 1.5 collective-permute-start.3
  98.8 19.0 %middle.3 = (bf16[4,2,5,32,384]{4,3,2,1,0:T(8,128)(2,1)}, bf16[4,2,3,32,384]{4,3,2,1,0:T(8,128)(2,1)}, bf16[2,4,64,2048]{3,2,1,0:T(8,128)(2,1)}, bf16[2,4,64,204...) custom-call(s32[1]{0:T(128)} %bitcast.where_ref, ...), custom_call_target="tpu_custom_call" | custom-call | tf_op jit(solution)/shard_map/middle/pallas_call | solution.py:140
  117.7 2.1 collective-permute-done.2.refs_1_
  122.6 9.4 %all-to-all-done.2.refs_0_ = bf16[4,2,8,32,384]{4,3,2,1,0:T(8,128)(2,1)} async-done(((bf16[4,2,8,32,384]{4,3,2,1,0:T(8,128)(2,1)}), bf16[4,2,8,32,384]{4,3,2,1,0:T(8,128)(2,1)}, u32[]{:S(2)}, u32[]{:S(2)}) %all-to-all-start.2) | async-done | bytes 1572896 | tf_op jit(solution)/shard_map/z3/all_to_all | solution.py:234
  132.0 4.2 %all-to-all-start.3 = ((bf16[4,2,5,32,384]{4,3,2,1,0:T(8,128)(2,1)}), bf16[4,2,5,32,384]{4,3,2,1,0:T(8,128)(2,1)}, u32[]{:S(2)}, u32[]{:S(2)}) async-start(bf16[4,2,5,32,384]{4,3,2,1,0:T(8,128)(2,1)} %get-tuple-element.113), calls=%async_computation.3 | async-start | bytes 1966080 | tf_op jit(solution)/shard_map/z4/all_to_all | solution.py:234
  136.2 1.6 collective-permute-start.4
  139.3 9.9 %collective-permute-done.4.refs_1_ = bf16[2,1,64,2048]{3,2,1,0:T(8,128)(2,1)S(1)} collective-permute-done((bf16[2,1,64,2048]{3,2,1,0:T(8,128)(2,1)S(1)}, bf16[2,1,64,2048]{3,2,1,0:T(8,128)(2,1)S(1)}, u32[]{:S(2)}, u32[]{:S(2)}) %collective-permute-start.4) | collective-permute-done | bytes 524320 | tf_op jit(solution)/shard_map/mid0_bit1/ppermute | solution.py:240
  151.2 6.4 %split.3 = (bf16[2,2,64,2048]{3,2,1,0:T(8,128)(2,1)}, bf16[2,2,64,2048]{3,2,1,0:T(8,128)(2,1)}, bf16[2,2,256,512]{3,2,1,0:T(8,128)(2,1)}, bf16[2,2,256,512]{3,2,1,0:T(8,128)(2,1)}) custom-call(s32[2]{0:T(128)S(1)} %get-tuple-element.174.which_ref, bf16[2,4,64,2048]{3,2,1,0:T(8,128)(2,1)} %get-tuple-element.115.refs_0_.refs_2_, ...), custom_call_target="tpu_custom_call" | custom-call | tf_op jit(solution)/shard_map/split/pallas_call | solution.py:268
  157.6 1.6 collective-permute-start.11
  160.3 4.7 %all-to-all-start.4 = ((bf16[4,2,3,32,384]{4,3,2,1,0:T(8,128)(2,1)}), bf16[4,2,3,32,384]{4,3,2,1,0:T(8,128)(2,1)}, u32[]{:S(2)}, u32[]{:S(2)}) async-start(bf16[4,2,3,32,384]{4,3,2,1,0:T(8,128)(2,1)} %get-tuple-element.123), calls=%async_computation.4 | async-start | bytes 1179648 | tf_op jit(solution)/shard_map/z5/all_to_all | solution.py:234
  165.0 3.4 %leave_back.2 = (bf16[384,2048]{1,0:T(8,128)(2,1)}, bf16[2,4,64,512]{3,2,1,0:T(8,128)(2,1)S(1)}, bf16[2,4,64,512]{3,2,1,0:T(8,128)(2,1)S(1)}) custom-call(s32[1]{0:T(128)} %bitcast.where_ref, bf16[4,2,8,32,384]{4,3,2,1,0:T(8,128)(2,1)} %all-to-all-done.2.refs_0_, bf16[4,2,5,32,384]{4,3,2,1,0:T(8,128)(2,1)} %all-to-all-done.3.refs_1_, ...), custom_call_target="tpu_custom_call" | custom-call | tf_op jit(solution)/shard_map/leave_back/pallas_call | solution.py:204
  168.3 3.4 %leave_back.3 = (bf16[384,2048]{1,0:T(8,128)(2,1)}, bf16[2,4,64,512]{3,2,1,0:T(8,128)(2,1)S(1)}, bf16[2,4,64,512]{3,2,1,0:T(8,128)(2,1)S(1)}) custom-call(s32[1]{0:T(128)} %bitcast.where_ref, bf16[4,2,8,32,384]{4,3,2,1,0:T(8,128)(2,1)} %all-to-all-done.2.refs_0_, ...), custom_call_target="tpu_custom_call", output_to_operand_aliasing={{0}: (6, {})} | custom-call | tf_op jit(solution)/shard_map/leave_back/pallas_call | solution.py:204
  172.2 2.8 %leave_out.2 = (bf16[384,2048]{1,0:T(8,128)(2,1)}, bf16[1,4,64,512]{3,2,1,0:T(8,128)(2,1)S(1)}, bf16[1,4,64,512]{3,2,1,0:T(8,128)(2,1)S(1)}) custom-call(s32[1]{0:T(128)} %bitcast.where_ref, bf16[4,2,8,32,384]{4,3,2,1,0:T(8,128)(2,1)} %all-to-all-done.2.refs_0_, bf16[4,2,5,32,384]{4,3,2,1,0:T(8,128)(2,1)} %all-to-all-done.3.refs_1_, ...), custom_call_target="tpu_custom_call" | custom-call | tf_op jit(solution)/shard_map/leave_out/pallas_call | solution.py:204
  177.6 1.5 collective-permute-start.14
  180.3 1.6 collective-permute-done.11.refs_1_
  181.9 1.6 collective-permute-done.12.refs_3_
  187.9 5.1 %leave_out.3 = (bf16[384,2048]{1,0:T(8,128)(2,1)}, bf16[3,4,64,512]{3,2,1,0:T(8,128)(2,1)S(1)}, bf16[3,4,64,512]{3,2,1,0:T(8,128)(2,1)S(1)}) custom-call(s32[1]{0:T(128)} %bitcast.where_ref, bf16[4,2,8,32,384]{4,3,2,1,0:T(8,128)(2,1)} %all-to-all-done.2.refs_0_, bf16[4,2,3,32,384]{4,3,2,1,0:T(8,128)(2,1)} %all-to-all-done.4.refs_1_, ...), custom_call_target="tpu_custom_call", output_to_operand_aliasing={{0}: (6, {})} | custom-call | tf_op jit(solution)/shard_map/leave_out/pallas_call | solution.py:204
  196.8 11.1 %collective-permute-done.20.refs_3_ = bf16[2,1,64,2048]{3,2,1,0:T(8,128)(2,1)S(1)} collective-permute-done((bf16[2,1,64,2048]{3,2,1,0:T(8,128)(2,1)S(1)}, bf16[2,1,64,2048]{3,2,1,0:T(8,128)(2,1)S(1)}, u32[]{:S(2)}, u32[]{:S(2)}) %collective-permute-start.20) | collective-permute-done | bytes 524320 | tf_op jit(solution)/shard_map/mid1_bit1/ppermute | solution.py:240
  208.4 2.3 %finish.4 = (f32[4,64,2048]{2,1,0:T(8,128)}, f32[4,256,512]{2,1,0:T(8,128)}) custom-call(bf16[2,1,64,2048]{3,2,1,0:T(8,128)(2,1)S(1)} %get-tuple-element.156.refs_0_, bf16[2,1,64,2048]{3,2,1,0:T(8,128)(2,1)S(1)} %copy-done.5, bf16[2,1,64,2048]{3,2,1,0:T(8,128)(2,1)S(1)} %copy-done.9, bf16[2,1,64,2048]{3,2,1,0:T(8,128)(2,1)S(1)} %collective-permute-done.20.refs_3_, ...), custom_call_target="tpu_custom_call" | custom-call | tf_op jit(solution)/shard_map/finish/pallas_call | solution.py:328
  210.7 5.1 %collective-permute-done.19.refs_1_ = bf16[3,2,64,512]{3,2,1,0:T(8,128)(2,1)S(1)} collective-permute-done((bf16[3,2,64,512]{3,2,1,0:T(8,128)(2,1)S(1)}, bf16[3,2,64,512]{3,2,1,0:T(8,128)(2,1)S(1)}, u32[]{:S(2)}, u32[]{:S(2)}) %collective-permute-start.19) | collective-permute-done | bytes 393248 | tf_op jit(solution)/shard_map/high_bit1/ppermute | solution.py:240
  222.5 2.8 %collective-permute-done.17.refs_3_ = bf16[2,1,64,512]{3,2,1,0:T(8,128)(2,1)S(1)} collective-permute-done((bf16[2,1,64,512]{3,2,1,0:T(8,128)(2,1)S(1)}, bf16[2,1,64,512]{3,2,1,0:T(8,128)(2,1)S(1)}, u32[]{:S(2)}, u32[]{:S(2)}) %collective-permute-start.17) | collective-permute-done | bytes 131104 | tf_op jit(solution)/shard_map/first_bit0/ppermute | solution.py:240
  (92 shorter events, 30.4 us)
Async XLA Ops:
  7.0 43.3 %all-to-all-start = ((bf16[4,2,2,4,32,384]{5,4,3,2,1,0:T(8,128)(2,1)}), bf16[4,2,2,4,32,384]{5,4,3,2,1,0:T(8,128)(2,1)S(1)}, u32[]{:S(2)}, u32[]{:S(2)}) async-start(bf16[4,2,2,4,32,384]{5,4,3,2,1,0:T(8,128)(2,1)} %get-tuple-element.90), calls=%async_computation | async-start | bytes 3145728 | tf_op jit(solution)/shard_map/z1/all_to_all | solution.py:234
  50.3 40.9 %all-to-all-start.1 = ((bf16[4,2,2,4,32,384]{5,4,3,2,1,0:T(8,128)(2,1)}), bf16[4,2,2,4,32,384]{5,4,3,2,1,0:T(8,128)(2,1)}, u32[]{:S(2)}, u32[]{:S(2)}) async-start(bf16[4,2,2,4,32,384]{5,4,3,2,1,0:T(8,128)(2,1)} %get-tuple-element.92), calls=%async_computation.1 | async-start | bytes 3145728 | tf_op jit(solution)/shard_map/z2/all_to_all | solution.py:234
  73.6 6.7 %collective-permute-start = (bf16[2,4,64,2048]{3,2,1,0:T(8,128)(2,1)}, bf16[2,4,64,2048]{3,2,1,0:T(8,128)(2,1)S(1)}, u32[]{:S(2)}, u32[]{:S(2)}) collective-permute-start(bf16[2,4,64,2048]{3,2,1,0:T(8,128)(2,1)} %get-tuple-element.96), channel_id=1, source_target_pairs={{0,4},{4,0},{8,12},{12,8},{16,20},{20,16},{24,28},{28,24},{1,5},{5... | collective-permute-start | bytes 6291464 | tf_op jit(solution)/shard_map/mid0_core/ppermute | solution.py:240
  73.6 7.5 %collective-permute-start.1 = (bf16[2,4,256,512]{3,2,1,0:T(8,128)(2,1)}, bf16[2,4,256,512]{3,2,1,0:T(8,128)(2,1)}, u32[]{:S(2)}, u32[]{:S(2)}) collective-permute-start(bf16[2,4,256,512]{3,2,1,0:T(8,128)(2,1)} %get-tuple-element.98), channel_id=1, source_target_pairs={{0,4},{4,0},{8,12},{12,8},{16,20},{20,16},{24,28},{28,24},{1,5},{5... | collective-permute-start | bytes 6291464 | tf_op jit(solution)/shard_map/mid0_core/ppermute | solution.py:240
  91.1 40.9 %all-to-all-start.2 = ((bf16[4,2,8,32,384]{4,3,2,1,0:T(8,128)(2,1)}), bf16[4,2,8,32,384]{4,3,2,1,0:T(8,128)(2,1)}, u32[]{:S(2)}, u32[]{:S(2)}) async-start(bf16[4,2,8,32,384]{4,3,2,1,0:T(8,128)(2,1)} %get-tuple-element.101), calls=%async_computation.2 | async-start | bytes 3145728 | tf_op jit(solution)/shard_map/z3/all_to_all | solution.py:234
  95.7 25.9 %copy-start.2 = (bf16[2,2,64,2048]{3,2,1,0:T(8,128)(2,1)S(1)}, bf16[2,2,64,2048]{3,2,1,0:T(8,128)(2,1)}, u32[]{:S(2)}) copy-start(bf16[2,2,64,2048]{3,2,1,0:T(8,128)(2,1)} %get-tuple-element.104.refs_0_) | copy-start | bytes 3145732
  95.7 25.9 %copy-start.3 = (bf16[2,2,256,512]{3,2,1,0:T(8,128)(2,1)S(1)}, bf16[2,2,256,512]{3,2,1,0:T(8,128)(2,1)}, u32[]{:S(2)}) copy-start(bf16[2,2,256,512]{3,2,1,0:T(8,128)(2,1)} %get-tuple-element.108.refs_2_) | copy-start | bytes 3145732
  95.7 24.2 %collective-permute-start.2 = (bf16[2,2,64,2048]{3,2,1,0:T(8,128)(2,1)S(1)}, bf16[2,2,64,2048]{3,2,1,0:T(8,128)(2,1)S(1)}, u32[]{:S(2)}, u32[]{:S(2)}) collective-permute-start(bf16[2,2,64,2048]{3,2,1,0:T(8,128)(2,1)S(1)} %copy-done.21), channel_id=1, source_target_pairs={{0,8},{4,12},{8,0},{12,4},{16,24},{20,28},{24,16},{28,20},{1,9},{5... | collective-permute-start | bytes 3145736 | tf_op jit(solution)/shard_map/mid0_bit0/ppermute | solution.py:240
  97.2 23.8 %collective-permute-start.3 = (bf16[2,2,256,512]{3,2,1,0:T(8,128)(2,1)S(1)}, bf16[2,2,256,512]{3,2,1,0:T(8,128)(2,1)S(1)}, u32[]{:S(2)}, u32[]{:S(2)}) collective-permute-start(bf16[2,2,256,512]{3,2,1,0:T(8,128)(2,1)S(1)} %copy-done.20), channel_id=1, source_target_pairs={{0,16},{4,20},{8,24},{12,28},{16,0},{20,4},{24,8},{28,12},{1,17},{... | collective-permute-start | bytes 3145736 | tf_op jit(solution)/shard_map/mid0_bit1/ppermute | solution.py:240
  121.1 30.1 %collective-permute-start.6 = (bf16[2,4,64,2048]{3,2,1,0:T(8,128)(2,1)}, bf16[2,4,64,2048]{3,2,1,0:T(8,128)(2,1)}, u32[]{:S(2)}, u32[]{:S(2)}) collective-permute-start(bf16[2,4,64,2048]{3,2,1,0:T(8,128)(2,1)} %get-tuple-element.116), channel_id=1, source_target_pairs={{0,4},{4,0},{8,12},{12,8},{16,20},{20,16},{24,28},{28,24},{1,5},{5... | collective-permute-start | bytes 6291464 | tf_op jit(solution)/shard_map/mid1_core/ppermute | solution.py:240
  121.1 30.1 %collective-permute-start.7 = (bf16[2,4,256,512]{3,2,1,0:T(8,128)(2,1)}, bf16[2,4,256,512]{3,2,1,0:T(8,128)(2,1)}, u32[]{:S(2)}, u32[]{:S(2)}) collective-permute-start(bf16[2,4,256,512]{3,2,1,0:T(8,128)(2,1)} %get-tuple-element.117), channel_id=1, source_target_pairs={{0,4},{4,0},{8,12},{12,8},{16,20},{20,16},{24,28},{28,24},{1,5},{5... | collective-permute-start | bytes 6291464 | tf_op jit(solution)/shard_map/mid1_core/ppermute | solution.py:240
  132.0 28.3 %all-to-all-start.3 = ((bf16[4,2,5,32,384]{4,3,2,1,0:T(8,128)(2,1)}), bf16[4,2,5,32,384]{4,3,2,1,0:T(8,128)(2,1)}, u32[]{:S(2)}, u32[]{:S(2)}) async-start(bf16[4,2,5,32,384]{4,3,2,1,0:T(8,128)(2,1)} %get-tuple-element.113), calls=%async_computation.3 | async-start | bytes 1966080 | tf_op jit(solution)/shard_map/z4/all_to_all | solution.py:234
  136.2 12.9 %collective-permute-start.4 = (bf16[2,1,64,2048]{3,2,1,0:T(8,128)(2,1)S(1)}, bf16[2,1,64,2048]{3,2,1,0:T(8,128)(2,1)S(1)}, u32[]{:S(2)}, u32[]{:S(2)}) collective-permute-start(bf16[2,1,64,2048]{3,2,1,0:T(8,128)(2,1)S(1)} %get-tuple-element.110), channel_id=1, source_target_pairs={{0,16},{4,20},{8,24},{12,28},{16,0},{20,4},{24,8},{28,12},{1,17},{... | collective-permute-start | bytes 1572872 | tf_op jit(solution)/shard_map/mid0_bit1/ppermute | solution.py:240
  137.8 12.6 %collective-permute-start.5 = (bf16[2,1,256,512]{3,2,1,0:T(8,128)(2,1)S(1)}, bf16[2,1,256,512]{3,2,1,0:T(8,128)(2,1)S(1)}, u32[]{:S(2)}, u32[]{:S(2)}) collective-permute-start(bf16[2,1,256,512]{3,2,1,0:T(8,128)(2,1)S(1)} %get-tuple-element.111), channel_id=1, source_target_pairs={{0,8},{4,12},{8,0},{12,4},{16,24},{20,28},{24,16},{28,20},{1,9},{5... | collective-permute-start | bytes 1572872 | tf_op jit(solution)/shard_map/mid0_bit0/ppermute | solution.py:240
  157.6 24.3 %collective-permute-start.11 = (bf16[2,2,64,2048]{3,2,1,0:T(8,128)(2,1)}, bf16[2,2,64,2048]{3,2,1,0:T(8,128)(2,1)S(1)}, u32[]{:S(2)}, u32[]{:S(2)}) collective-permute-start(bf16[2,2,64,2048]{3,2,1,0:T(8,128)(2,1)} %get-tuple-element.121), channel_id=1, source_target_pairs={{0,8},{4,12},{8,0},{12,4},{16,24},{20,28},{24,16},{28,20},{1,9},{5... | collective-permute-start | bytes 3145736 | tf_op jit(solution)/shard_map/mid1_bit0/ppermute | solution.py:240
  159.2 24.4 %collective-permute-start.12 = (bf16[2,2,256,512]{3,2,1,0:T(8,128)(2,1)}, bf16[2,2,256,512]{3,2,1,0:T(8,128)(2,1)S(1)}, u32[]{:S(2)}, u32[]{:S(2)}) collective-permute-start(bf16[2,2,256,512]{3,2,1,0:T(8,128)(2,1)} %get-tuple-element.122), channel_id=1, source_target_pairs={{0,16},{4,20},{8,24},{12,28},{16,0},{20,4},{24,8},{28,12},{1,17},{... | collective-permute-start | bytes 3145736 | tf_op jit(solution)/shard_map/mid1_bit1/ppermute | solution.py:240
  160.3 27.6 %all-to-all-start.4 = ((bf16[4,2,3,32,384]{4,3,2,1,0:T(8,128)(2,1)}), bf16[4,2,3,32,384]{4,3,2,1,0:T(8,128)(2,1)}, u32[]{:S(2)}, u32[]{:S(2)}) async-start(bf16[4,2,3,32,384]{4,3,2,1,0:T(8,128)(2,1)} %get-tuple-element.123), calls=%async_computation.4 | async-start | bytes 1179648 | tf_op jit(solution)/shard_map/z5/all_to_all | solution.py:234
  171.7 3.3 %collective-permute-start.9 = (bf16[2,4,64,512]{3,2,1,0:T(8,128)(2,1)S(1)}, bf16[2,4,64,512]{3,2,1,0:T(8,128)(2,1)S(1)}, u32[]{:S(2)}, u32[]{:S(2)}) collective-permute-start(bf16[2,4,64,512]{3,2,1,0:T(8,128)(2,1)S(1)} %get-tuple-element.130), channel_id=1, source_target_pairs={{0,4},{4,0},{8,12},{12,8},{16,20},{20,16},{24,28},{28,24},{1,5},{5... | collective-permute-start | bytes 1572872 | tf_op jit(solution)/shard_map/first_core/ppermute | solution.py:240
  171.7 3.3 %collective-permute-start.8 = (bf16[2,4,64,512]{3,2,1,0:T(8,128)(2,1)S(1)}, bf16[2,4,64,512]{3,2,1,0:T(8,128)(2,1)S(1)}, u32[]{:S(2)}, u32[]{:S(2)}) collective-permute-start(bf16[2,4,64,512]{3,2,1,0:T(8,128)(2,1)S(1)} %get-tuple-element.127), channel_id=1, source_target_pairs={{0,4},{4,0},{8,12},{12,8},{16,20},{20,16},{24,28},{28,24},{1,5},{5... | collective-permute-start | bytes 1572872 | tf_op jit(solution)/shard_map/first_core/ppermute | solution.py:240
  175.0 4.1 %collective-permute-start.10 = (bf16[1,4,64,512]{3,2,1,0:T(8,128)(2,1)S(1)}, bf16[1,4,64,512]{3,2,1,0:T(8,128)(2,1)S(1)}, u32[]{:S(2)}, u32[]{:S(2)}) collective-permute-start(bf16[1,4,64,512]{3,2,1,0:T(8,128)(2,1)S(1)} %get-tuple-element.134), channel_id=1, source_target_pairs={{0,4},{4,0},{8,12},{12,8},{16,20},{20,16},{24,28},{28,24},{1,5},{5... | collective-permute-start | bytes 786440 | tf_op jit(solution)/shard_map/low_core/ppermute | solution.py:240
  176.5 16.5 %collective-permute-start.13 = (bf16[2,2,64,512]{3,2,1,0:T(8,128)(2,1)}, bf16[2,2,64,512]{3,2,1,0:T(8,128)(2,1)}, u32[]{:S(2)}, u32[]{:S(2)}) collective-permute-start(bf16[2,2,64,512]{3,2,1,0:T(8,128)(2,1)} %get-tuple-element.131), channel_id=1, source_target_pairs={{0,8},{4,12},{8,0},{12,4},{16,24},{20,28},{24,16},{28,20},{1,9},{5... | collective-permute-start | bytes 786440 | tf_op jit(solution)/shard_map/first_bit0/ppermute | solution.py:240
  177.6 15.4 %collective-permute-start.14 = (bf16[2,2,64,512]{3,2,1,0:T(8,128)(2,1)}, bf16[2,2,64,512]{3,2,1,0:T(8,128)(2,1)}, u32[]{:S(2)}, u32[]{:S(2)}) collective-permute-start(bf16[2,2,64,512]{3,2,1,0:T(8,128)(2,1)} %get-tuple-element.132), channel_id=1, source_target_pairs={{0,16},{4,20},{8,24},{12,28},{16,0},{20,4},{24,8},{28,12},{1,17},{... | collective-permute-start | bytes 786440 | tf_op jit(solution)/shard_map/first_bit1/ppermute | solution.py:240
  179.8 13.2 %collective-permute-start.15 = (bf16[1,2,64,512]{3,2,1,0:T(8,128)(2,1)}, bf16[1,2,64,512]{3,2,1,0:T(8,128)(2,1)}, u32[]{:S(2)}, u32[]{:S(2)}) collective-permute-start(bf16[1,2,64,512]{3,2,1,0:T(8,128)(2,1)} %get-tuple-element.135), channel_id=1, source_target_pairs={{0,8},{4,12},{8,0},{12,4},{16,24},{20,28},{24,16},{28,20},{1,9},{5... | collective-permute-start | bytes 393224 | tf_op jit(solution)/shard_map/low_bit0/ppermute | solution.py:240
  187.8 20.5 %copy-start.5 = (bf16[2,1,64,2048]{3,2,1,0:T(8,128)(2,1)S(1)}, bf16[2,1,64,2048]{3,2,1,0:T(8,128)(2,1)}, u32[]{:S(2)}) copy-start(bf16[2,1,64,2048]{3,2,1,0:T(8,128)(2,1)} %copy-done.4) | copy-start | bytes 1572868
  193.0 2.4 %collective-permute-start.18 = (bf16[3,4,64,512]{3,2,1,0:T(8,128)(2,1)S(1)}, bf16[3,4,64,512]{3,2,1,0:T(8,128)(2,1)S(1)}, u32[]{:S(2)}, u32[]{:S(2)}) collective-permute-start(bf16[3,4,64,512]{3,2,1,0:T(8,128)(2,1)S(1)} %get-tuple-element.154), channel_id=1, source_target_pairs={{0,4},{4,0},{8,12},{12,8},{16,20},{20,16},{24,28},{28,24},{1,5},{5... | collective-permute-start | bytes 2359304 | tf_op jit(solution)/shard_map/high_core/ppermute | solution.py:240
  193.1 14.8 %collective-permute-start.20 = (bf16[2,1,64,2048]{3,2,1,0:T(8,128)(2,1)S(1)}, bf16[2,1,64,2048]{3,2,1,0:T(8,128)(2,1)S(1)}, u32[]{:S(2)}, u32[]{:S(2)}) collective-permute-start(bf16[2,1,64,2048]{3,2,1,0:T(8,128)(2,1)S(1)} %copy-done.17), channel_id=1, source_target_pairs={{0,16},{4,20},{8,24},{12,28},{16,0},{20,4},{24,8},{28,12},{1,17},{... | collective-permute-start | bytes 1572872 | tf_op jit(solution)/shard_map/mid1_bit1/ppermute | solution.py:240
  194.4 14.0 %collective-permute-start.21 = (bf16[2,1,256,512]{3,2,1,0:T(8,128)(2,1)S(1)}, bf16[2,1,256,512]{3,2,1,0:T(8,128)(2,1)S(1)}, u32[]{:S(2)}, u32[]{:S(2)}) collective-permute-start(bf16[2,1,256,512]{3,2,1,0:T(8,128)(2,1)S(1)} %copy-done.15), channel_id=1, source_target_pairs={{0,8},{4,12},{8,0},{12,4},{16,24},{20,28},{24,16},{28,20},{1,9},{5... | collective-permute-start | bytes 1572872 | tf_op jit(solution)/shard_map/mid1_bit0/ppermute | solution.py:240
  195.5 20.3 %collective-permute-start.19 = (bf16[3,2,64,512]{3,2,1,0:T(8,128)(2,1)S(1)}, bf16[3,2,64,512]{3,2,1,0:T(8,128)(2,1)S(1)}, u32[]{:S(2)}, u32[]{:S(2)}) collective-permute-start(bf16[3,2,64,512]{3,2,1,0:T(8,128)(2,1)S(1)} %get-tuple-element.155), channel_id=1, source_target_pairs={{0,16},{4,20},{8,24},{12,28},{16,0},{20,4},{24,8},{28,12},{1,17},{... | collective-permute-start | bytes 1179656 | tf_op jit(solution)/shard_map/high_bit1/ppermute | solution.py:240
  216.0 10.2 %collective-permute-start.23 = (bf16[3,1,64,512]{3,2,1,0:T(8,128)(2,1)S(1)}, bf16[3,1,64,512]{3,2,1,0:T(8,128)(2,1)S(1)}, u32[]{:S(2)}, u32[]{:S(2)}) collective-permute-start(bf16[3,1,64,512]{3,2,1,0:T(8,128)(2,1)S(1)} %get-tuple-element.173), channel_id=1, source_target_pairs={{0,8},{4,12},{8,0},{12,4},{16,24},{20,28},{24,16},{28,20},{1,9},{5... | collective-permute-start | bytes 589832 | tf_op jit(solution)/shard_map/high_bit0/ppermute | solution.py:240
  217.5 5.0 %collective-permute-start.16 = (bf16[2,1,64,512]{3,2,1,0:T(8,128)(2,1)S(1)}, bf16[2,1,64,512]{3,2,1,0:T(8,128)(2,1)S(1)}, u32[]{:S(2)}, u32[]{:S(2)}) collective-permute-start(bf16[2,1,64,512]{3,2,1,0:T(8,128)(2,1)S(1)} %get-tuple-element.150), channel_id=1, source_target_pairs={{0,16},{4,20},{8,24},{12,28},{16,0},{20,4},{24,8},{28,12},{1,17},{... | collective-permute-start | bytes 393224 | tf_op jit(solution)/shard_map/first_bit1/ppermute | solution.py:240
  219.0 6.3 %collective-permute-start.17 = (bf16[2,1,64,512]{3,2,1,0:T(8,128)(2,1)S(1)}, bf16[2,1,64,512]{3,2,1,0:T(8,128)(2,1)S(1)}, u32[]{:S(2)}, u32[]{:S(2)}) collective-permute-start(bf16[2,1,64,512]{3,2,1,0:T(8,128)(2,1)S(1)} %get-tuple-element.152), channel_id=1, source_target_pairs={{0,8},{4,12},{8,0},{12,4},{16,24},{20,28},{24,16},{28,20},{1,9},{5... | collective-permute-start | bytes 393224 | tf_op jit(solution)/shard_map/first_bit0/ppermute | solution.py:240
  221.4 4.7 %collective-permute-start.22 = (bf16[1,1,64,512]{3,2,1,0:T(8,128)(2,1)S(1)}, bf16[1,1,64,512]{3,2,1,0:T(8,128)(2,1)S(1)}, u32[]{:S(2)}, u32[]{:S(2)}) collective-permute-start(bf16[1,1,64,512]{3,2,1,0:T(8,128)(2,1)S(1)} %get-tuple-element.169), channel_id=1, source_target_pairs={{0,16},{4,20},{8,24},{12,28},{16,0},{20,4},{24,8},{28,12},{1,17},{... | collective-permute-start | bytes 196616 | tf_op jit(solution)/shard_map/low_bit1/ppermute | solution.py:240
  (19 other events, 132.9 us)

commit v4 on v3

--- a/solution.py
+++ b/solution.py
@@ -165,13 +165,14 @@
     return outs[:-4], outs[-4:-2], outs[-2:]
 
 
-def leave(where, received, places, weight, base_rows, left, scale, sizes, backward, first, count, onto=None):
+def leave(where, received, places, weight, base_rows, left, scale, sizes, backward, first, count, onto=None, apart=False):
     T, L, BS, NT, G, SW, Q, _ = sizes
     rows = BS // (2 * Q)
 
     def kernel(where_ref, *refs):
         ins, (w_ref, base_ref, left_ref) = refs[:N_CHUNK], refs[N_CHUNK : N_CHUNK + 3]
-        out_ref, send_ref, keep_ref, scr, slab_scr = refs[-5:]
+        out_ref, low_ref, high_ref, *keeps = refs[-7 if apart else -6 : -2]
+        scr, slab_scr = refs[-2:]
         core = where_ref[0]
         scr[:, 0] = ins[0][:, :, 0]
         scr[:, 1] = ins[1][:, :, 0]
@@ -182,7 +183,7 @@
             branch = dot(regrouped, w_ref[0], 0, 0)
             slab_scr[...] = regrouped.reshape(Q, 2, rows, T)
         out_ref[...] = (base_ref[...].astype(F32) + branch).astype(BF16)
-        for send, ref in ((True, send_ref), (False, keep_ref)):
+        for send in (True, False):
             which = 1 - core if send else core
             if backward:
                 half = left_ref[0, :, which].reshape(Q * rows, T)
@@ -190,11 +191,19 @@
             else:
                 half = slab_scr[:, which].reshape(Q * rows, T)
                 part = dot(half, left_ref[...], 1, 0)
-            ref[0] = (scale * part).astype(BF16).reshape(Q, rows, BS)
+            part = (scale * part).astype(BF16).reshape(Q, rows, BS)
+            if send:
+                low_ref[0], high_ref[0] = part[:, : rows // 2], part[:, rows // 2 :]
+            elif apart:
+                keeps[0][0], keeps[1][0] = part[:, : rows // 2], part[:, rows // 2 :]
+            else:
+                keeps[0][0] = part
 
     cols = spec((T, BS), lambda b, s: (0, first + b))
     part = jax.ShapeDtypeStruct((count, Q, rows, BS), BF16)
     part_spec = spec((1, Q, rows, BS), lambda b, s: (b, 0, 0, 0))
+    piece = jax.ShapeDtypeStruct((count, Q, rows // 2, BS), BF16)
+    piece_spec = spec((1, Q, rows // 2, BS), lambda b, s: (b, 0, 0, 0))
     left_spec = spec((1, Q, 2, rows, T), lambda b, s: (first + b, 0, 0, 0, 0)) if backward else cols
     operands = held(*received, weight, base_rows, left)
     more, aliases = [], {}
@@ -212,13 +221,13 @@
             ]
             + [spec((1, BS, BS), lambda b, s: (first + b, 0, 0)), cols, left_spec]
             + more,
-            out_specs=[cols, part_spec, part_spec],
+            out_specs=[cols, piece_spec, piece_spec] + ([piece_spec] * 2 if apart else [part_spec]),
             scratch_shapes=[
                 pltpu.VMEM((NT, N_CHUNK, G, SW, T), BF16),
                 pltpu.VMEM((Q, 2, rows, T), BF16),
             ],
         ),
-        out_shape=[pltpu.HBM((T, L * BS), BF16), part, part],
+        out_shape=[pltpu.HBM((T, L * BS), BF16), piece, piece] + ([piece] * 2 if apart else [part]),
         input_output_aliases=aliases,
         compiler_params=params(24),
         cost_estimate=LIGHT,
@@ -284,18 +293,26 @@
 
 def split_small(which, pairs, lead):
     n = len(pairs)
+    operands = []
+    for keep, got, _, _ in pairs:
+        operands += [keep] + list(got)
 
     def kernel(which_ref, *refs):
-        ins, outs = refs[: 2 * n], refs[2 * n :]
-        for i, (keep, _, first, place) in enumerate(pairs):
+        ins, outs = list(refs[: len(operands)]), refs[len(operands) :]
+        for i, (keep, got, first, place) in enumerate(pairs):
+            keep_ref, got_refs = ins.pop(0), [ins.pop(0) for _ in got]
             for stays in (0, 1):
                 chosen = which_ref[i] if stays else 1 - which_ref[i]
                 for r in range(keep.shape[1] // 2):
                     low = r & ((1 << place) - 1)
                     q = ((r >> place) << (place + 1)) + low + chosen * (1 << place)
                     for a in range(lead):
-                        total = ins[2 * i][first + a, q].astype(F32) + ins[2 * i + 1][first + a, q].astype(F32)
-                        outs[2 * i + stays][a, r] = total.astype(BF16)
+                        start = 0
+                        for got_ref, came in zip(got_refs, got):
+                            stop = start + came.shape[2]
+                            total = keep_ref[first + a, q, start:stop].astype(F32) + got_ref[first + a, q].astype(F32)
+                            outs[2 * i + stays][a, r, start:stop] = total.astype(BF16)
+                            start = stop
 
     out_shape = []
     for keep, _, _, _ in pairs:
@@ -303,36 +320,48 @@
     outs = pl.pallas_call(
         kernel,
         name="small",
-        in_specs=[pl.BlockSpec(memory_space=pltpu.SMEM)] + [whole()] * (2 * n),
+        in_specs=[pl.BlockSpec(memory_space=pltpu.SMEM)] + [whole()] * len(operands),
         out_specs=[whole()] * (2 * n),
         out_shape=out_shape,
         compiler_params=params(8),
         cost_estimate=LIGHT,
-    )(which, *[array for keep, got, _, _ in pairs for array in (keep, got)])
+    )(which, *operands)
     return [(outs[2 * i], outs[2 * i + 1]) for i in range(n)]
 
 
 def finish(groups):
-    shapes = [(sum(keep.shape[0] for keep, _ in pairs),) + pairs[0][0].shape[2:] for pairs in groups]
-    n_in = sum(2 * len(pairs) for pairs in groups)
+    flat, shapes = [], []
+    for pairs in groups:
+        leads, rows = 0, 0
+        for pair in pairs:
+            halves = pair if isinstance(pair[0], tuple) else (pair,)
+            leads += halves[0][0].shape[0]
+            rows = sum(keep.shape[2] for keep, _ in halves)
+            flat += [array for half in halves for array in half]
+        shapes.append((leads, rows, flat[-1].shape[3]))
 
     def kernel(*refs):
-        ins, outs = list(refs[:n_in]), refs[n_in:]
+        ins, outs = list(refs[: len(flat)]), refs[len(flat) :]
         for pairs, out in zip(groups, outs):
             start = 0
-            for keep, _ in pairs:
-                a, b = ins.pop(0), ins.pop(0)
-                out[start : start + keep.shape[0]] = a[:, 0].astype(F32) + b[:, 0].astype(F32)
-                start += keep.shape[0]
+            for pair in pairs:
+                halves = pair if isinstance(pair[0], tuple) else (pair,)
+                row, leads = 0, halves[0][0].shape[0]
+                for keep, _ in halves:
+                    a, b = ins.pop(0), ins.pop(0)
+                    rows = keep.shape[2]
+                    out[start : start + leads, row : row + rows] = a[:, 0].astype(F32) + b[:, 0].astype(F32)
+                    row += rows
+                start += leads
 
     return pl.pallas_call(
         kernel,
         name="finish",
-        in_specs=[whole()] * n_in,
+        in_specs=[whole()] * len(flat),
         out_shape=[jax.ShapeDtypeStruct(shape, F32) for shape in shapes],
         compiler_params=params(16),
         cost_estimate=LIGHT,
-    )(*[array for pairs in groups for pair in pairs for array in pair])
+    )(*flat)
 
 
 class Halving:
@@ -356,6 +385,7 @@
             self.moving.append(bit)
         which = jnp.stack(mine).astype(jnp.int32)
         if self.large and len(self.held[0]) == self.bits - 1:
+            pairs = [(keep, got[0], first, place) for keep, got, first, place in pairs]
             self.parts = split(which, pairs, (lead, pairs[0][0].shape[1]))
         else:
             self.parts = split_small(which, pairs, lead)
@@ -363,20 +393,23 @@
 
     def move(self, outgoing):
         self.streams = [
-            (staying, swap(out, bit + 1, "%s_bit%d" % (self.label, bit)), 0)
+            (staying, [swap(out, bit + 1, "%s_bit%d" % (self.label, bit))], 0)
             for out, (_, staying), bit in zip(outgoing, self.parts, self.moving)
         ]
 
     def got(self):
-        return [got for _, got, _ in self.streams]
+        return [array for _, got, _ in self.streams for array in got]
 
     def replace(self, arrived):
-        self.streams = [(keep, got, first) for (keep, _, first), got in zip(self.streams, arrived)]
+        arrived = list(arrived)
+        self.streams = [
+            (keep, [arrived.pop(0) for _ in got], first) for keep, got, first in self.streams
+        ]
 
     def run(self, lead):
         while self.orders[0]:
             self.move(self.add(lead))
-        return [(keep, got) for keep, got, _ in self.streams]
+        return [(keep, got[0]) for keep, got, _ in self.streams]
 
 
 def body(tokens, up_first, up_second, down_first, down_second, cotangent):
@@ -399,7 +432,7 @@
             up_send, down_send, *got = together(up_send, down_send, *before.got())
             before.replace(got)
         got_up, got_down = swap(up_send, 0, label + "_core"), swap(down_send, 0, label + "_core")
-        return Halving([(up_keep, got_up, 0), (down_keep, got_down, 0)], label, True)
+        return Halving([(up_keep, [got_up], 0), (down_keep, [got_down], 0)], label, True)
 
     first_0, first_1 = enter(tokens, up_first, cotangent, down_second, sizes)
     in_0 = regroup(first_0, "z1")
@@ -418,10 +451,10 @@
     both_0, most_1, *_ = together(both_0, most_1, *leaving_0)
     most_1 = regroup(most_1, "z4")
     mid_0.move(leaving_0)
-    got = together(*mid_0.got(), *mid_1.got())
+    leaving_1 = mid_1.add(lead)
+    got = together(*mid_0.got(), *leaving_1)
     mid_0.replace(got[:2])
-    mid_1.replace(got[2:])
-    leaving_1 = mid_1.add(lead)
+    leaving_1 = got[2:]
     mid_1.move(leaving_1)
     most_1, rest_1, *_ = together(most_1, rest_1, *leaving_1)
     rest_1 = regroup(rest_1, "z5")
@@ -442,11 +475,15 @@
             grad_tokens,
         )
         parts.append(part)
-    edge_first = Halving([(keep, swap(send, 0, "first_core"), 0) for send, keep in parts], "first", False)
+    def edge_sums(halves, label, turned):
+        streams = [(part[2], [swap(piece, 0, label + "_core") for piece in part[:2]], 0) for part in halves]
+        return Halving(streams, label, False, turned)
+
+    edge_first = edge_sums(parts, "first", 0)
     layer_out, *low = leave(
         where, (both_0, most_1), (L, L), down_second, tokens, cotangent, scale, sizes, False, 0, cut
     )
-    edge_low = Halving([(low[1], swap(low[0], 0, "low_core"), 0)], "low", False)
+    edge_low = edge_sums([low], "low", 0)
     leaving_first = edge_first.add(lead)
     leaving_low = edge_low.add(cut)
     leaving_1 = mid_1.add(lead) if mid_1.orders[0] else []
@@ -467,20 +504,25 @@
         cut,
         L - cut,
         layer_out,
+        True,
     )
-    high[0], *got = together(high[0], *edge_first.got(), *edge_low.got())
-    edge_first.replace(got[:2])
-    edge_low.replace(got[2:])
-    edge_high = Halving([(high[1], swap(high[0], 0, "high_core"), 0)], "high", False, 1)
+    waited = (mid_1,)
+    high[0], high[1], *got = together(*high[:2], *[array for sums in waited for array in sums.got()])
+    for sums in waited:
+        count = len(sums.got())
+        sums.replace(got[:count])
+        got = got[count:]
+    streams = [(keep, [swap(send, 0, "high_core")], 0) for send, keep in zip(high[:2], high[2:])]
+    edge_high = Halving(streams, "high", False)
     edge_high.move(edge_high.add(L - cut))
     done_0, done_1 = mid_0.run(lead), mid_1.run(lead)
     grad_up_second, grad_down_first = finish([[done_0[0], done_1[0]], [done_0[1], done_1[1]]])
     done_first, done_low = edge_first.run(lead), edge_low.run(cut)
     got = together(*edge_high.got(), grad_up_second, grad_down_first)
-    edge_high.replace(got[:1])
+    edge_high.replace(got[:-2])
     done_high = edge_high.run(L - cut)
     (grad_up_first,) = finish([done_first])
-    (grad_down_second,) = finish([done_low + done_high])
+    (grad_down_second,) = finish([done_low + [tuple(done_high)]])
     return (
         layer_out,
         grad_tokens,

time: 228 us -> 219 us (0.961)
  waiting for transfers between devices: 89.5 us -> 78.9 us
    ppermute x24 -> x30, waiting for transfers between devices: 44 us -> 24.3 us  [swap(): return lax.ppermute(value, 'dp', [(s, s ^ 1 << bit) for s in range(count)])]
    all_to_all x5, waiting for transfers between devices: 45.6 us -> 54.6 us  [regroup(): lax.all_to_all(pieces, 'tensor', split_axis=0, concat_axis=0, tiled=True)]
    ppermute x24 -> x30, starting transfers between devices: 20.8 us -> 22.3 us  [swap(): return lax.ppermute(value, 'dp', [(s, s ^ 1 << bit) for s in range(count)])]
    unnamed x44 -> x36, local copies, waits for them, and re-layouts: 5.39 us -> 6.06 us
  transfers between devices with their start and end apart: 29 -> 35, of which waited for: 17 -> 15; matrix products, arithmetic and copies ran while one was open for 0% -> 0% of each run, Pallas kernels for 35% -> 36%
where the time goes in v4:
time: 219 us
  Pallas kernels  86 us (39%)
  waiting for transfers between devices  78.9 us (36%)
  starting transfers between devices  46.6 us (21%)
  local copies, waits for them, and re-layouts  6.06 us (3%)
    all_to_all x5, waiting for transfers between devices, regroup(): lax.all_to_all(pieces, 'tensor', split_axis=0, concat_axis=0, tiled=True)  54.6 us
    pallas_call x2, Pallas kernels, middle(): pl.pallas_call(kernel, name='middle', grid_spec=pltpu.PrefetchScalarGridS...  38.2 us
    ppermute x30, waiting for transfers between devices, swap(): return lax.ppermute(value, 'dp', [(s, s ^ 1 << bit) for s in range(count)])  24.3 us
    all_to_all x5, starting transfers between devices, regroup(): lax.all_to_all(pieces, 'tensor', split_axis=0, concat_axis=0, tiled=True)  24.3 us
    ppermute x30, starting transfers between devices, swap(): return lax.ppermute(value, 'dp', [(s, s ^ 1 << bit) for s in range(count)])  22.3 us
    pallas_call x4, Pallas kernels, leave(): pl.pallas_call(kernel, name='leave_back' if backward else 'leave_out', gr...  14.9 us
    pallas_call x2, Pallas kernels, split(): pl.pallas_call(kernel, name='split', grid_spec=pltpu.PrefetchScalarGridSp...  12.8 us
    pallas_call x1, Pallas kernels, enter(): pl.pallas_call(kernel, name='enter', grid=(L,), in_specs=[cols, square, c...  6.34 us
  transfers between devices with their start and end apart: 35, of which 15 were waited for; matrix products, arithmetic and copies ran while one was open for 0% of the time, Pallas kernels for 36%

profile of v4, /device:TPU:0, one launch (start us, length us, event | category | flops | bytes accessed | tf_op | source)
XLA Modules:
  0.0 218.6 jit_solution(3164101525589194764)
XLA Ops:
  0.6 6.3 %enter.1 = (bf16[4,2,2,4,32,384]{5,4,3,2,1,0:T(8,128)(2,1)}, bf16[4,2,2,4,32,384]{5,4,3,2,1,0:T(8,128)(2,1)}) custom-call(bf16[384,2048]{1,0:T(8,128)(2,1)} %refs_3_.7, bf16[4,512,512]{2,1,0:T(8,128)(2,1)} %refs_2_.9, bf16[384,2048]{1,0:T(8,128)(2,1)} %refs_4_.3, bf16[4,512,512]{2,1,0:T(8,128)(2,1)} %refs_2_.11), custom_call_target="tpu_custom_call" | custom-call | tf_op jit(solution)/shard_map/enter/pallas_call | solution.py:59
  7.0 6.3 %all-to-all-start = ((bf16[4,2,2,4,32,384]{5,4,3,2,1,0:T(8,128)(2,1)}), bf16[4,2,2,4,32,384]{5,4,3,2,1,0:T(8,128)(2,1)S(1)}, u32[]{:S(2)}, u32[]{:S(2)}) async-start(bf16[4,2,2,4,32,384]{5,4,3,2,1,0:T(8,128)(2,1)} %get-tuple-element.100), calls=%async_computation | async-start | bytes 3145728 | tf_op jit(solution)/shard_map/z1/all_to_all | solution.py:243
  13.3 3.8 %turn.1.refs_4_ = bf16[4,4,2,64,384]{4,3,2,1,0:T(8,128)(2,1)} custom-call(bf16[384,2048]{1,0:T(8,128)(2,1)} %refs_3_.7), custom_call_target="tpu_custom_call" | custom-call | tf_op jit(solution)/shard_map/turn/pallas_call | solution.py:79
  17.1 33.1 %all-to-all-done.refs_0_ = bf16[4,2,2,4,32,384]{5,4,3,2,1,0:T(8,128)(2,1)S(1)} async-done(((bf16[4,2,2,4,32,384]{5,4,3,2,1,0:T(8,128)(2,1)}), bf16[4,2,2,4,32,384]{5,4,3,2,1,0:T(8,128)(2,1)S(1)}, u32[]{:S(2)}, u32[]{:S(2)}) %all-to-all-start) | async-done | bytes 1572896 | tf_op jit(solution)/shard_map/z1/all_to_all | solution.py:243
  50.3 4.3 %all-to-all-start.1 = ((bf16[4,2,2,4,32,384]{5,4,3,2,1,0:T(8,128)(2,1)}), bf16[4,2,2,4,32,384]{5,4,3,2,1,0:T(8,128)(2,1)}, u32[]{:S(2)}, u32[]{:S(2)}) async-start(bf16[4,2,2,4,32,384]{5,4,3,2,1,0:T(8,128)(2,1)} %get-tuple-element.102), calls=%async_computation.1 | async-start | bytes 3145728 | tf_op jit(solution)/shard_map/z2/all_to_all | solution.py:243
  54.6 19.0 %middle.2 = (bf16[4,2,8,32,384]{4,3,2,1,0:T(8,128)(2,1)}, bf16[2,4,64,2048]{3,2,1,0:T(8,128)(2,1)}, bf16[2,4,64,2048]{3,2,1,0:T(8,128)(2,1)}, bf16[2,4,256,512]{3,2,1,0:T(8,128)(2,1)}, bf16[2,4,256,512]{3,2,1,0:T(8,128)(2,1)}) custom-call(s32[1]{0:T(128)} %bitcast.where_ref, bf16[4,2,2,4,32,384]{5,4,3,2,1,0:T(8,128)(2,1)} %copy-done.17, ...), custom_call_target="tpu_custom_call" | custom-call | tf_op jit(solution)/shard_map/middle/pallas_call | solution.py:140
  74.3 6.1 %collective-permute-done.refs_1_.refs_3_ = bf16[2,4,64,2048]{3,2,1,0:T(8,128)(2,1)S(1)} collective-permute-done((bf16[2,4,64,2048]{3,2,1,0:T(8,128)(2,1)}, bf16[2,4,64,2048]{3,2,1,0:T(8,128)(2,1)S(1)}, u32[]{:S(2)}, u32[]{:S(2)}) %collective-permute-start) | collective-permute-done | bytes 2097184 | tf_op jit(solution)/shard_map/mid0_core/ppermute | solution.py:249
  81.7 6.4 %split.2 = (bf16[2,2,64,2048]{3,2,1,0:T(8,128)(2,1)}, bf16[2,2,64,2048]{3,2,1,0:T(8,128)(2,1)}, bf16[2,2,256,512]{3,2,1,0:T(8,128)(2,1)}, bf16[2,2,256,512]{3,2,1,0:T(8,128)(2,1)}) custom-call(s32[2]{0:T(128)S(1)} %pad_add_fusion.which_ref, bf16[2,4,64,2048]{3,2,1,0:T(8,128)(2,1)} %get-tuple-element.105.refs_0_.refs_2_, bf16[2,4,64,2048]{3,2,1,0:T(8,128)(2,1)} %copy-done.16, ...), custom_call_target="tpu_custom_call" | custom-call | tf_op jit(solution)/shard_map/split/pallas_call | solution.py:277
  88.1 1.5 collective-permute-start.2
  89.7 1.5 collective-permute-start.3
  91.2 5.0 %all-to-all-start.2 = ((bf16[4,2,8,32,384]{4,3,2,1,0:T(8,128)(2,1)}), bf16[4,2,8,32,384]{4,3,2,1,0:T(8,128)(2,1)}, u32[]{:S(2)}, u32[]{:S(2)}) async-start(bf16[4,2,8,32,384]{4,3,2,1,0:T(8,128)(2,1)} %get-tuple-element.111), calls=%async_computation.2 | async-start | bytes 3145728 | tf_op jit(solution)/shard_map/z3/all_to_all | solution.py:243
  96.2 19.2 %middle.3 = (bf16[4,2,5,32,384]{4,3,2,1,0:T(8,128)(2,1)}, bf16[4,2,3,32,384]{4,3,2,1,0:T(8,128)(2,1)}, bf16[2,4,64,2048]{3,2,1,0:T(8,128)(2,1)}, bf16[2,4,64,204...) custom-call(s32[1]{0:T(128)} %bitcast.where_ref, ...), custom_call_target="tpu_custom_call" | custom-call | tf_op jit(solution)/shard_map/middle/pallas_call | solution.py:140
  118.7 14.3 %all-to-all-done.2.refs_0_ = bf16[4,2,8,32,384]{4,3,2,1,0:T(8,128)(2,1)} async-done(((bf16[4,2,8,32,384]{4,3,2,1,0:T(8,128)(2,1)}), bf16[4,2,8,32,384]{4,3,2,1,0:T(8,128)(2,1)}, u32[]{:S(2)}, u32[]{:S(2)}) %all-to-all-start.2) | async-done | bytes 1572896 | tf_op jit(solution)/shard_map/z3/all_to_all | solution.py:243
  133.0 4.2 %all-to-all-start.3 = ((bf16[4,2,5,32,384]{4,3,2,1,0:T(8,128)(2,1)}), bf16[4,2,5,32,384]{4,3,2,1,0:T(8,128)(2,1)}, u32[]{:S(2)}, u32[]{:S(2)}) async-start(bf16[4,2,5,32,384]{4,3,2,1,0:T(8,128)(2,1)} %get-tuple-element.123), calls=%async_computation.3 | async-start | bytes 1966080 | tf_op jit(solution)/shard_map/z4/all_to_all | solution.py:243
  137.8 1.4 collective-permute-start.5
  139.3 6.4 %split.3 = (bf16[2,2,64,2048]{3,2,1,0:T(8,128)(2,1)}, bf16[2,2,64,2048]{3,2,1,0:T(8,128)(2,1)}, bf16[2,2,256,512]{3,2,1,0:T(8,128)(2,1)}, bf16[2,2,256,512]{3,2,1,0:T(8,128)(2,1)}) custom-call(s32[2]{0:T(128)S(1)} %pad_add_fusion.which_ref, bf16[2,4,64,2048]{3,2,1,0:T(8,128)(2,1)} %get-tuple-element.125.refs_0_.refs_2_, ...), custom_call_target="tpu_custom_call" | custom-call | tf_op jit(solution)/shard_map/split/pallas_call | solution.py:277
  145.7 4.7 %collective-permute-done.4.refs_1_ = bf16[2,1,64,2048]{3,2,1,0:T(8,128)(2,1)S(1)} collective-permute-done((bf16[2,1,64,2048]{3,2,1,0:T(8,128)(2,1)}, bf16[2,1,64,2048]{3,2,1,0:T(8,128)(2,1)S(1)}, u32[]{:S(2)}, u32[]{:S(2)}) %collective-permute-start.4) | collective-permute-done | bytes 524320 | tf_op jit(solution)/shard_map/mid0_bit1/ppermute | solution.py:249
  154.0 7.1 %all-to-all-done.3.refs_1_ = bf16[4,2,5,32,384]{4,3,2,1,0:T(8,128)(2,1)} async-done(((bf16[4,2,5,32,384]{4,3,2,1,0:T(8,128)(2,1)}), bf16[4,2,5,32,384]{4,3,2,1,0:T(8,128)(2,1)}, u32[]{:S(2)}, u32[]{:S(2)}) %all-to-all-start.3) | async-done | bytes 983072 | tf_op jit(solution)/shard_map/z4/all_to_all | solution.py:243
  161.1 4.4 %all-to-all-start.4 = ((bf16[4,2,3,32,384]{4,3,2,1,0:T(8,128)(2,1)}), bf16[4,2,3,32,384]{4,3,2,1,0:T(8,128)(2,1)}, u32[]{:S(2)}, u32[]{:S(2)}) async-start(bf16[4,2,3,32,384]{4,3,2,1,0:T(8,128)(2,1)} %get-tuple-element.133), calls=%async_computation.4 | async-start | bytes 1179648 | tf_op jit(solution)/shard_map/z5/all_to_all | solution.py:243
  165.5 3.5 %leave_back.2 = (bf16[384,2048]{1,0:T(8,128)(2,1)}, bf16[2,4,32,512]{3,2,1,0:T(8,128)(2,1)S(1)}, bf16[2,4,32,512]{3,2,1,0:T(8,128)(2,1)S(1)}, bf16[2,4,64,512]{3,2,1,0:T(8,128)(2,1)S(1)}) custom-call(s32[1]{0:T(128)} %bitcast.where_ref, bf16[4,2,8,32,384]{4,3,2,1,0:T(8,128)(2,1)} %all-to-all-done.2.refs_0_, ...), custom_call_target="tpu_custom_call" | custom-call | tf_op jit(solution)/shard_map/leave_back/pallas_call | solution.py:213
  169.0 3.7 %leave_back.3 = (bf16[384,2048]{1,0:T(8,128)(2,1)}, bf16[2,4,32,512]{3,2,1,0:T(8,128)(2,1)S(1)}, bf16[2,4,32,512]{3,2,1,0:T(8,128)(2,1)S(1)}, bf16[2,4,64,512]{3,2,1,0:T(8,128)(2,1)S(1)}) custom-call(s32[1]{0:T(128)} %bitcast.where_ref, bf16[4,2,8,32,384]{4,3,2,1,0:T(8,128)(2,1)} %all-to-all-done.2.refs_0_, ...), custom_call_target="tpu_custom_call", output_to_operand_aliasing={{0}: (6, {})} | custom-call | tf_op jit(solution)/shard_map/leave_back/pallas_call | solution.py:213
  172.7 2.8 %collective-permute-done.14.refs_1_ = bf16[2,2,64,2048]{3,2,1,0:T(8,128)(2,1)S(1)} collective-permute-done((bf16[2,2,64,2048]{3,2,1,0:T(8,128)(2,1)}, bf16[2,2,64,2048]{3,2,1,0:T(8,128)(2,1)S(1)}, u32[]{:S(2)}, u32[]{:S(2)}) %collective-permute-start.14) | collective-permute-done | bytes 1048608 | tf_op jit(solution)/shard_map/mid1_bit0/ppermute | solution.py:249
  175.9 1.9 small.11
  179.4 1.4 collective-permute-start.20
  181.4 2.8 %leave_out.2 = (bf16[384,2048]{1,0:T(8,128)(2,1)}, bf16[1,4,32,512]{3,2,1,0:T(8,128)(2,1)S(1)}, bf16[1,4,32,512]{3,2,1,0:T(8,128)(2,1)S(1)}, bf16[1,4,64,512]{3,2,1,0:T(8,128)(2,1)S(1)}) custom-call(s32[1]{0:T(128)} %bitcast.where_ref, bf16[4,2,8,32,384]{4,3,2,1,0:T(8,128)(2,1)} %all-to-all-done.2.refs_0_, ...), custom_call_target="tpu_custom_call" | custom-call | tf_op jit(solution)/shard_map/leave_out/pallas_call | solution.py:213
  189.3 5.0 %leave_out.3 = (bf16[384,2048]{1,0:T(8,128)(2,1)}, bf16[3,4,32,512]{3,2,1,0:T(8,128)(2,1)S(1)}, bf16[3,4,32,512]{3,2,1,0:T(8,128)(2,1)S(1)}, bf16[3,4,32,512]{3,...) custom-call(s32[1]{0:T(128)} %bitcast.where_ref, ...), custom_call_target="tpu_custom_call", output_to_operand_aliasing={{0}: (6, {})} | custom-call | tf_op jit(solution)/shard_map/leave_out/pallas_call | solution.py:213
  197.7 1.5 collective-permute-start.24
  201.1 3.0 %collective-permute-done.16.refs_1_ = bf16[2,2,64,512]{3,2,1,0:T(8,128)(2,1)S(1)} collective-permute-done((bf16[2,2,64,512]{3,2,1,0:T(8,128)(2,1)S(1)}, bf16[2,2,64,512]{3,2,1,0:T(8,128)(2,1)S(1)}, u32[]{:S(2)}, u32[]{:S(2)}) %collective-permute-start.16) | collective-permute-done | bytes 262176 | tf_op jit(solution)/shard_map/first_bit0/ppermute | solution.py:249
  204.1 1.3 collective-permute-done.17.refs_3_
  206.9 1.4 collective-permute-start.19
  208.3 2.3 %finish.4 = (f32[4,64,2048]{2,1,0:T(8,128)}, f32[4,256,512]{2,1,0:T(8,128)}) custom-call(bf16[2,1,64,2048]{3,2,1,0:T(8,128)(2,1)S(1)} %get-tuple-element.171.refs_0_, bf16[2,1,64,2048]{3,2,1,0:T(8,128)(2,1)S(1)} %copy-done.5, bf16[2,1,64,2048]{3,2,1,0:T(8,128)(2,1)S(1)} %copy-done.9, bf16[2,1,64,2048]{3,2,1,0:T(8,128)(2,1)S(1)} %collective-permute-done.20.refs_3_, ...), custom_call_target="tpu_custom_call" | custom-call | tf_op jit(solution)/shard_map/finish/pallas_call | solution.py:357
  215.0 2.7 %collective-permute-done.27.refs_1_ = bf16[1,1,64,512]{3,2,1,0:T(8,128)(2,1)S(1)} collective-permute-done((bf16[1,1,64,512]{3,2,1,0:T(8,128)(2,1)S(1)}, bf16[1,1,64,512]{3,2,1,0:T(8,128)(2,1)S(1)}, u32[]{:S(2)}, u32[]{:S(2)}) %collective-permute-start.27) | collective-permute-done | bytes 65568 | tf_op jit(solution)/shard_map/low_bit1/ppermute | solution.py:249
  (97 shorter events, 28.9 us)
Async XLA Ops:
  7.0 43.3 %all-to-all-start = ((bf16[4,2,2,4,32,384]{5,4,3,2,1,0:T(8,128)(2,1)}), bf16[4,2,2,4,32,384]{5,4,3,2,1,0:T(8,128)(2,1)S(1)}, u32[]{:S(2)}, u32[]{:S(2)}) async-start(bf16[4,2,2,4,32,384]{5,4,3,2,1,0:T(8,128)(2,1)} %get-tuple-element.100), calls=%async_computation | async-start | bytes 3145728 | tf_op jit(solution)/shard_map/z1/all_to_all | solution.py:243
  50.3 40.9 %all-to-all-start.1 = ((bf16[4,2,2,4,32,384]{5,4,3,2,1,0:T(8,128)(2,1)}), bf16[4,2,2,4,32,384]{5,4,3,2,1,0:T(8,128)(2,1)}, u32[]{:S(2)}, u32[]{:S(2)}) async-start(bf16[4,2,2,4,32,384]{5,4,3,2,1,0:T(8,128)(2,1)} %get-tuple-element.102), calls=%async_computation.1 | async-start | bytes 3145728 | tf_op jit(solution)/shard_map/z2/all_to_all | solution.py:243
  73.7 6.7 %collective-permute-start = (bf16[2,4,64,2048]{3,2,1,0:T(8,128)(2,1)}, bf16[2,4,64,2048]{3,2,1,0:T(8,128)(2,1)S(1)}, u32[]{:S(2)}, u32[]{:S(2)}) collective-permute-start(bf16[2,4,64,2048]{3,2,1,0:T(8,128)(2,1)} %get-tuple-element.106), channel_id=1, source_target_pairs={{0,4},{4,0},{8,12},{12,8},{16,20},{20,16},{24,28},{28,24},{1,5},{5... | collective-permute-start | bytes 6291464 | tf_op jit(solution)/shard_map/mid0_core/ppermute | solution.py:249
  73.7 7.5 %collective-permute-start.1 = (bf16[2,4,256,512]{3,2,1,0:T(8,128)(2,1)}, bf16[2,4,256,512]{3,2,1,0:T(8,128)(2,1)}, u32[]{:S(2)}, u32[]{:S(2)}) collective-permute-start(bf16[2,4,256,512]{3,2,1,0:T(8,128)(2,1)} %get-tuple-element.108), channel_id=1, source_target_pairs={{0,4},{4,0},{8,12},{12,8},{16,20},{20,16},{24,28},{28,24},{1,5},{5... | collective-permute-start | bytes 6291464 | tf_op jit(solution)/shard_map/mid0_core/ppermute | solution.py:249
  88.1 27.3 %collective-permute-start.2 = (bf16[2,2,64,2048]{3,2,1,0:T(8,128)(2,1)}, bf16[2,2,64,2048]{3,2,1,0:T(8,128)(2,1)S(1)}, u32[]{:S(2)}, u32[]{:S(2)}) collective-permute-start(bf16[2,2,64,2048]{3,2,1,0:T(8,128)(2,1)} %get-tuple-element.109), channel_id=1, source_target_pairs={{0,8},{4,12},{8,0},{12,4},{16,24},{20,28},{24,16},{28,20},{1,9},{5... | collective-permute-start | bytes 3145736 | tf_op jit(solution)/shard_map/mid0_bit0/ppermute | solution.py:249
  89.7 25.7 %collective-permute-start.3 = (bf16[2,2,256,512]{3,2,1,0:T(8,128)(2,1)}, bf16[2,2,256,512]{3,2,1,0:T(8,128)(2,1)S(1)}, u32[]{:S(2)}, u32[]{:S(2)}) collective-permute-start(bf16[2,2,256,512]{3,2,1,0:T(8,128)(2,1)} %get-tuple-element.110), channel_id=1, source_target_pairs={{0,16},{4,20},{8,24},{12,28},{16,0},{20,4},{24,8},{28,12},{1,17},{... | collective-permute-start | bytes 3145736 | tf_op jit(solution)/shard_map/mid0_bit1/ppermute | solution.py:249
  91.2 41.8 %all-to-all-start.2 = ((bf16[4,2,8,32,384]{4,3,2,1,0:T(8,128)(2,1)}), bf16[4,2,8,32,384]{4,3,2,1,0:T(8,128)(2,1)}, u32[]{:S(2)}, u32[]{:S(2)}) async-start(bf16[4,2,8,32,384]{4,3,2,1,0:T(8,128)(2,1)} %get-tuple-element.111), calls=%async_computation.2 | async-start | bytes 3145728 | tf_op jit(solution)/shard_map/z3/all_to_all | solution.py:243
  115.4 23.9 %collective-permute-start.6 = (bf16[2,4,64,2048]{3,2,1,0:T(8,128)(2,1)}, bf16[2,4,64,2048]{3,2,1,0:T(8,128)(2,1)}, u32[]{:S(2)}, u32[]{:S(2)}) collective-permute-start(bf16[2,4,64,2048]{3,2,1,0:T(8,128)(2,1)} %get-tuple-element.126), channel_id=1, source_target_pairs={{0,4},{4,0},{8,12},{12,8},{16,20},{20,16},{24,28},{28,24},{1,5},{5... | collective-permute-start | bytes 6291464 | tf_op jit(solution)/shard_map/mid1_core/ppermute | solution.py:249
  115.5 23.8 %collective-permute-start.7 = (bf16[2,4,256,512]{3,2,1,0:T(8,128)(2,1)}, bf16[2,4,256,512]{3,2,1,0:T(8,128)(2,1)}, u32[]{:S(2)}, u32[]{:S(2)}) collective-permute-start(bf16[2,4,256,512]{3,2,1,0:T(8,128)(2,1)} %get-tuple-element.128), channel_id=1, source_target_pairs={{0,4},{4,0},{8,12},{12,8},{16,20},{20,16},{24,28},{28,24},{1,5},{5... | collective-permute-start | bytes 6291464 | tf_op jit(solution)/shard_map/mid1_core/ppermute | solution.py:249
  133.0 28.1 %all-to-all-start.3 = ((bf16[4,2,5,32,384]{4,3,2,1,0:T(8,128)(2,1)}), bf16[4,2,5,32,384]{4,3,2,1,0:T(8,128)(2,1)}, u32[]{:S(2)}, u32[]{:S(2)}) async-start(bf16[4,2,5,32,384]{4,3,2,1,0:T(8,128)(2,1)} %get-tuple-element.123), calls=%async_computation.3 | async-start | bytes 1966080 | tf_op jit(solution)/shard_map/z4/all_to_all | solution.py:243
  137.3 13.2 %collective-permute-start.4 = (bf16[2,1,64,2048]{3,2,1,0:T(8,128)(2,1)}, bf16[2,1,64,2048]{3,2,1,0:T(8,128)(2,1)S(1)}, u32[]{:S(2)}, u32[]{:S(2)}) collective-permute-start(bf16[2,1,64,2048]{3,2,1,0:T(8,128)(2,1)} %copy-done.13), channel_id=1, source_target_pairs={{0,16},{4,20},{8,24},{12,28},{16,0},{20,4},{24,8},{28,12},{1,17},{... | collective-permute-start | bytes 1572872 | tf_op jit(solution)/shard_map/mid0_bit1/ppermute | solution.py:249
  137.8 13.4 %collective-permute-start.5 = (bf16[2,1,256,512]{3,2,1,0:T(8,128)(2,1)}, bf16[2,1,256,512]{3,2,1,0:T(8,128)(2,1)S(1)}, u32[]{:S(2)}, u32[]{:S(2)}) collective-permute-start(bf16[2,1,256,512]{3,2,1,0:T(8,128)(2,1)} %copy-done.12), channel_id=1, source_target_pairs={{0,8},{4,12},{8,0},{12,4},{16,24},{20,28},{24,16},{28,20},{1,9},{5... | collective-permute-start | bytes 1572872 | tf_op jit(solution)/shard_map/mid0_bit0/ppermute | solution.py:249
  152.0 23.5 %collective-permute-start.14 = (bf16[2,2,64,2048]{3,2,1,0:T(8,128)(2,1)}, bf16[2,2,64,2048]{3,2,1,0:T(8,128)(2,1)S(1)}, u32[]{:S(2)}, u32[]{:S(2)}) collective-permute-start(bf16[2,2,64,2048]{3,2,1,0:T(8,128)(2,1)} %get-tuple-element.131), channel_id=1, source_target_pairs={{0,8},{4,12},{8,0},{12,4},{16,24},{20,28},{24,16},{28,20},{1,9},{5... | collective-permute-start | bytes 3145736 | tf_op jit(solution)/shard_map/mid1_bit0/ppermute | solution.py:249
  152.9 22.9 %collective-permute-start.15 = (bf16[2,2,256,512]{3,2,1,0:T(8,128)(2,1)}, bf16[2,2,256,512]{3,2,1,0:T(8,128)(2,1)S(1)}, u32[]{:S(2)}, u32[]{:S(2)}) collective-permute-start(bf16[2,2,256,512]{3,2,1,0:T(8,128)(2,1)} %get-tuple-element.132), channel_id=1, source_target_pairs={{0,16},{4,20},{8,24},{12,28},{16,0},{20,4},{24,8},{28,12},{1,17},{... | collective-permute-start | bytes 3145736 | tf_op jit(solution)/shard_map/mid1_bit1/ppermute | solution.py:249
  161.1 28.2 %all-to-all-start.4 = ((bf16[4,2,3,32,384]{4,3,2,1,0:T(8,128)(2,1)}), bf16[4,2,3,32,384]{4,3,2,1,0:T(8,128)(2,1)}, u32[]{:S(2)}, u32[]{:S(2)}) async-start(bf16[4,2,3,32,384]{4,3,2,1,0:T(8,128)(2,1)} %get-tuple-element.133), calls=%async_computation.4 | async-start | bytes 1179648 | tf_op jit(solution)/shard_map/z5/all_to_all | solution.py:243
  172.7 13.4 %collective-permute-start.10 = (bf16[2,4,32,512]{3,2,1,0:T(8,128)(2,1)S(1)}, bf16[2,4,32,512]{3,2,1,0:T(8,128)(2,1)S(1)}, u32[]{:S(2)}, u32[]{:S(2)}) collective-permute-start(bf16[2,4,32,512]{3,2,1,0:T(8,128)(2,1)S(1)} %get-tuple-element.141), channel_id=1, source_target_pairs={{0,4},{4,0},{8,12},{12,8},{16,20},{20,16},{24,28},{28,24},{1,5},{5... | collective-permute-start | bytes 786440 | tf_op jit(solution)/shard_map/first_core/ppermute | solution.py:249
  179.4 15.0 %collective-permute-start.20 = (bf16[2,1,64,2048]{3,2,1,0:T(8,128)(2,1)}, bf16[2,1,64,2048]{3,2,1,0:T(8,128)(2,1)S(1)}, u32[]{:S(2)}, u32[]{:S(2)}) collective-permute-start(bf16[2,1,64,2048]{3,2,1,0:T(8,128)(2,1)} %get-tuple-element.151), channel_id=1, source_target_pairs={{0,16},{4,20},{8,24},{12,28},{16,0},{20,4},{24,8},{28,12},{1,17},{... | collective-permute-start | bytes 1572872 | tf_op jit(solution)/shard_map/mid1_bit1/ppermute | solution.py:249
  180.7 13.7 %collective-permute-start.21 = (bf16[2,1,256,512]{3,2,1,0:T(8,128)(2,1)}, bf16[2,1,256,512]{3,2,1,0:T(8,128)(2,1)S(1)}, u32[]{:S(2)}, u32[]{:S(2)}) collective-permute-start(bf16[2,1,256,512]{3,2,1,0:T(8,128)(2,1)} %get-tuple-element.152), channel_id=1, source_target_pairs={{0,8},{4,12},{8,0},{12,4},{16,24},{20,28},{24,16},{28,20},{1,9},{5... | collective-permute-start | bytes 1572872 | tf_op jit(solution)/shard_map/mid1_bit0/ppermute | solution.py:249
  185.7 1.7 collective-permute-start.8
  186.1 1.8 collective-permute-start.9
  194.4 2.5 %collective-permute-start.22 = (bf16[3,4,32,512]{3,2,1,0:T(8,128)(2,1)S(1)}, bf16[3,4,32,512]{3,2,1,0:T(8,128)(2,1)S(1)}, u32[]{:S(2)}, u32[]{:S(2)}) collective-permute-start(bf16[3,4,32,512]{3,2,1,0:T(8,128)(2,1)S(1)} %get-tuple-element.166), channel_id=1, source_target_pairs={{0,4},{4,0},{8,12},{12,8},{16,20},{20,16},{24,28},{28,24},{1,5},{5... | collective-permute-start | bytes 1179656 | tf_op jit(solution)/shard_map/high_core/ppermute | solution.py:249
  194.6 2.3 %collective-permute-start.23 = (bf16[3,4,32,512]{3,2,1,0:T(8,128)(2,1)S(1)}, bf16[3,4,32,512]{3,2,1,0:T(8,128)(2,1)S(1)}, u32[]{:S(2)}, u32[]{:S(2)}) collective-permute-start(bf16[3,4,32,512]{3,2,1,0:T(8,128)(2,1)S(1)} %get-tuple-element.168), channel_id=1, source_target_pairs={{0,4},{4,0},{8,12},{12,8},{16,20},{20,16},{24,28},{28,24},{1,5},{5... | collective-permute-start | bytes 1179656 | tf_op jit(solution)/shard_map/high_core/ppermute | solution.py:249
  195.0 9.1 %collective-permute-start.16 = (bf16[2,2,64,512]{3,2,1,0:T(8,128)(2,1)S(1)}, bf16[2,2,64,512]{3,2,1,0:T(8,128)(2,1)S(1)}, u32[]{:S(2)}, u32[]{:S(2)}) collective-permute-start(bf16[2,2,64,512]{3,2,1,0:T(8,128)(2,1)S(1)} %copy-done.15), channel_id=1, source_target_pairs={{0,8},{4,12},{8,0},{12,4},{16,24},{20,28},{24,16},{28,20},{1,9},{5... | collective-permute-start | bytes 786440 | tf_op jit(solution)/shard_map/first_bit0/ppermute | solution.py:249
  196.3 9.2 %collective-permute-start.17 = (bf16[2,2,64,512]{3,2,1,0:T(8,128)(2,1)S(1)}, bf16[2,2,64,512]{3,2,1,0:T(8,128)(2,1)S(1)}, u32[]{:S(2)}, u32[]{:S(2)}) collective-permute-start(bf16[2,2,64,512]{3,2,1,0:T(8,128)(2,1)S(1)} %get-tuple-element.144), channel_id=1, source_target_pairs={{0,16},{4,20},{8,24},{12,28},{16,0},{20,4},{24,8},{28,12},{1,17},{... | collective-permute-start | bytes 786440 | tf_op jit(solution)/shard_map/first_bit1/ppermute | solution.py:249
  197.7 13.0 %collective-permute-start.24 = (bf16[3,2,32,512]{3,2,1,0:T(8,128)(2,1)S(1)}, bf16[3,2,32,512]{3,2,1,0:T(8,128)(2,1)S(1)}, u32[]{:S(2)}, u32[]{:S(2)}) collective-permute-start(bf16[3,2,32,512]{3,2,1,0:T(8,128)(2,1)S(1)} %get-tuple-element.169), channel_id=1, source_target_pairs={{0,8},{4,12},{8,0},{12,4},{16,24},{20,28},{24,16},{28,20},{1,9},{5... | collective-permute-start | bytes 589832 | tf_op jit(solution)/shard_map/high_bit0/ppermute | solution.py:249
  199.2 11.5 %collective-permute-start.25 = (bf16[3,2,32,512]{3,2,1,0:T(8,128)(2,1)S(1)}, bf16[3,2,32,512]{3,2,1,0:T(8,128)(2,1)S(1)}, u32[]{:S(2)}, u32[]{:S(2)}) collective-permute-start(bf16[3,2,32,512]{3,2,1,0:T(8,128)(2,1)S(1)} %get-tuple-element.170), channel_id=1, source_target_pairs={{0,16},{4,20},{8,24},{12,28},{16,0},{20,4},{24,8},{28,12},{1,17},{... | collective-permute-start | bytes 589832 | tf_op jit(solution)/shard_map/high_bit1/ppermute | solution.py:249
  199.8 13.5 %collective-permute-start.26 = (bf16[1,2,64,512]{3,2,1,0:T(8,128)(2,1)S(1)}, bf16[1,2,64,512]{3,2,1,0:T(8,128)(2,1)S(1)}, u32[]{:S(2)}, u32[]{:S(2)}) collective-permute-start(bf16[1,2,64,512]{3,2,1,0:T(8,128)(2,1)S(1)} %get-tuple-element.148), channel_id=1, source_target_pairs={{0,8},{4,12},{8,0},{12,4},{16,24},{20,28},{24,16},{28,20},{1,9},{5... | collective-permute-start | bytes 393224 | tf_op jit(solution)/shard_map/low_bit0/ppermute | solution.py:249
  206.1 8.0 %collective-permute-start.18 = (bf16[2,1,64,512]{3,2,1,0:T(8,128)(2,1)S(1)}, bf16[2,1,64,512]{3,2,1,0:T(8,128)(2,1)S(1)}, u32[]{:S(2)}, u32[]{:S(2)}) collective-permute-start(bf16[2,1,64,512]{3,2,1,0:T(8,128)(2,1)S(1)} %get-tuple-element.160), channel_id=1, source_target_pairs={{0,16},{4,20},{8,24},{12,28},{16,0},{20,4},{24,8},{28,12},{1,17},{... | collective-permute-start | bytes 393224 | tf_op jit(solution)/shard_map/first_bit1/ppermute | solution.py:249
  206.9 7.2 %collective-permute-start.19 = (bf16[2,1,64,512]{3,2,1,0:T(8,128)(2,1)S(1)}, bf16[2,1,64,512]{3,2,1,0:T(8,128)(2,1)S(1)}, u32[]{:S(2)}, u32[]{:S(2)}) collective-permute-start(bf16[2,1,64,512]{3,2,1,0:T(8,128)(2,1)S(1)} %get-tuple-element.162), channel_id=1, source_target_pairs={{0,8},{4,12},{8,0},{12,4},{16,24},{20,28},{24,16},{28,20},{1,9},{5... | collective-permute-start | bytes 393224 | tf_op jit(solution)/shard_map/first_bit0/ppermute | solution.py:249
  211.3 6.4 %collective-permute-start.28 = (bf16[3,1,32,512]{3,2,1,0:T(8,128)(2,1)S(1)}, bf16[3,1,32,512]{3,2,1,0:T(8,128)(2,1)S(1)}, u32[]{:S(2)}, u32[]{:S(2)}) collective-permute-start(bf16[3,1,32,512]{3,2,1,0:T(8,128)(2,1)S(1)} %get-tuple-element.191), channel_id=1, source_target_pairs={{0,16},{4,20},{8,24},{12,28},{16,0},{20,4},{24,8},{28,12},{1,17},{... | collective-permute-start | bytes 294920 | tf_op jit(solution)/shard_map/high_bit1/ppermute | solution.py:249
  212.0 5.7 %collective-permute-start.29 = (bf16[3,1,32,512]{3,2,1,0:T(8,128)(2,1)S(1)}, bf16[3,1,32,512]{3,2,1,0:T(8,128)(2,1)S(1)}, u32[]{:S(2)}, u32[]{:S(2)}) collective-permute-start(bf16[3,1,32,512]{3,2,1,0:T(8,128)(2,1)S(1)} %get-tuple-element.193), channel_id=1, source_target_pairs={{0,8},{4,12},{8,0},{12,4},{16,24},{20,28},{24,16},{28,20},{1,9},{5... | collective-permute-start | bytes 294920 | tf_op jit(solution)/shard_map/high_bit0/ppermute | solution.py:249
  213.4 4.3 %collective-permute-start.27 = (bf16[1,1,64,512]{3,2,1,0:T(8,128)(2,1)S(1)}, bf16[1,1,64,512]{3,2,1,0:T(8,128)(2,1)S(1)}, u32[]{:S(2)}, u32[]{:S(2)}) collective-permute-start(bf16[1,1,64,512]{3,2,1,0:T(8,128)(2,1)S(1)} %get-tuple-element.185), channel_id=1, source_target_pairs={{0,16},{4,20},{8,24},{12,28},{16,0},{20,4},{24,8},{28,12},{1,17},{... | collective-permute-start | bytes 196616 | tf_op jit(solution)/shard_map/low_bit1/ppermute | solution.py:249
  (21 other events, 130.3 us)

commit v5 on v4

--- a/solution.py
+++ b/solution.py
@@ -165,17 +165,27 @@
     return outs[:-4], outs[-4:-2], outs[-2:]
 
 
-def leave(where, received, places, weight, base_rows, left, scale, sizes, backward, first, count, onto=None, apart=False):
+def leave(where, received, places, weight, base_rows, left, scale, sizes, backward, first, count, onto=None, cut=None):
     T, L, BS, NT, G, SW, Q, _ = sizes
     rows = BS // (2 * Q)
+    n_in = len(places)
 
     def kernel(where_ref, *refs):
-        ins, (w_ref, base_ref, left_ref) = refs[:N_CHUNK], refs[N_CHUNK : N_CHUNK + 3]
-        out_ref, low_ref, high_ref, *keeps = refs[-7 if apart else -6 : -2]
-        scr, slab_scr = refs[-2:]
+        ins, (w_ref, base_ref, left_ref) = refs[:n_in], refs[n_in : n_in + 3]
+        out_ref, low_ref, high_ref, low_keep, high_keep, scr, slab_scr = refs[-7:]
         core = where_ref[0]
         scr[:, 0] = ins[0][:, :, 0]
-        scr[:, 1] = ins[1][:, :, 0]
+        if cut is not None:
+
+            @pl.when(pl.program_id(0) < cut)
+            def _():
+                scr[:, 1] = ins[1][:, :, 0]
+
+            @pl.when(pl.program_id(0) >= cut)
+            def _():
+                scr[:, 1] = ins[2][:, :, 0]
+        else:
+            scr[:, 1] = ins[1][:, :, 0]
         regrouped = scr[...].reshape(BS, T)
         if backward:
             branch = dot(regrouped.T, w_ref[0], 1, 1)
@@ -194,14 +204,10 @@
             part = (scale * part).astype(BF16).reshape(Q, rows, BS)
             if send:
                 low_ref[0], high_ref[0] = part[:, : rows // 2], part[:, rows // 2 :]
-            elif apart:
-                keeps[0][0], keeps[1][0] = part[:, : rows // 2], part[:, rows // 2 :]
             else:
-                keeps[0][0] = part
+                low_keep[0], high_keep[0] = part[:, : rows // 2], part[:, rows // 2 :]
 
     cols = spec((T, BS), lambda b, s: (0, first + b))
-    part = jax.ShapeDtypeStruct((count, Q, rows, BS), BF16)
-    part_spec = spec((1, Q, rows, BS), lambda b, s: (b, 0, 0, 0))
     piece = jax.ShapeDtypeStruct((count, Q, rows // 2, BS), BF16)
     piece_spec = spec((1, Q, rows // 2, BS), lambda b, s: (b, 0, 0, 0))
     left_spec = spec((1, Q, 2, rows, T), lambda b, s: (first + b, 0, 0, 0, 0)) if backward else cols
@@ -209,7 +215,7 @@
     more, aliases = [], {}
     if onto is not None:
         operands += held(onto)
-        more, aliases = [pl.BlockSpec(memory_space=pl.ANY)], {N_CHUNK + 4: 0}
+        more, aliases = [pl.BlockSpec(memory_space=pl.ANY)], {n_in + 4: 0}
     return pl.pallas_call(
         kernel,
         name="leave_back" if backward else "leave_out",
@@ -217,17 +223,17 @@
             num_scalar_prefetch=1,
             grid=(count,),
             in_specs=[
-                spec((NT, G, 1, SW, T), lambda b, s, place=place: (0, 0, place + b, 0, 0)) for place in places
+                spec((NT, G, 1, SW, T), lambda b, s, place=place: (0, 0, place(b), 0, 0)) for place in places
             ]
             + [spec((1, BS, BS), lambda b, s: (first + b, 0, 0)), cols, left_spec]
             + more,
-            out_specs=[cols, piece_spec, piece_spec] + ([piece_spec] * 2 if apart else [part_spec]),
+            out_specs=[cols] + [piece_spec] * 4,
             scratch_shapes=[
                 pltpu.VMEM((NT, N_CHUNK, G, SW, T), BF16),
                 pltpu.VMEM((Q, 2, rows, T), BF16),
             ],
         ),
-        out_shape=[pltpu.HBM((T, L * BS), BF16), piece, piece] + ([piece] * 2 if apart else [part]),
+        out_shape=[pltpu.HBM((T, L * BS), BF16)] + [piece] * 4,
         input_output_aliases=aliases,
         compiler_params=params(24),
         cost_estimate=LIGHT,
@@ -458,53 +464,33 @@
     mid_1.move(leaving_1)
     most_1, rest_1, *_ = together(most_1, rest_1, *leaving_1)
     rest_1 = regroup(rest_1, "z5")
-    grad_tokens, parts = None, []
-    for start, count in ((0, half), (half, L - half)):
-        grad_tokens, *part = leave(
-            where,
-            (both_0, most_1),
-            (start, start),
-            up_first,
-            cotangent,
-            x_turned,
-            scale,
-            sizes,
-            True,
-            start,
-            count,
-            grad_tokens,
-        )
-        parts.append(part)
-    def edge_sums(halves, label, turned):
-        streams = [(part[2], [swap(piece, 0, label + "_core") for piece in part[:2]], 0) for part in halves]
-        return Halving(streams, label, False, turned)
-
-    edge_first = edge_sums(parts, "first", 0)
-    layer_out, *low = leave(
-        where, (both_0, most_1), (L, L), down_second, tokens, cotangent, scale, sizes, False, 0, cut
+    def edge_sums(halves, label):
+        streams = [(keep, [swap(out, 0, label + "_core")], 0) for out, keep in zip(halves[:2], halves[2:])]
+        return Halving(streams, label, False)
+
+    grad_tokens, *first = leave(
+        where, (both_0, most_1), [lambda b: b] * 2, up_first, cotangent, x_turned, scale, sizes, True, 0, L
     )
-    edge_low = edge_sums([low], "low", 0)
-    leaving_first = edge_first.add(lead)
-    leaving_low = edge_low.add(cut)
+    edge_first = edge_sums(first, "first")
+    leaving_first = edge_first.add(L)
     leaving_1 = mid_1.add(lead) if mid_1.orders[0] else []
     edge_first.move(leaving_first)
-    edge_low.move(leaving_low)
     mid_1.move(leaving_1)
-    rest_1, *_ = together(rest_1, *leaving_first, *leaving_low, *leaving_1)
+    rest_1, *_ = together(rest_1, *leaving_first, *leaving_1)
     layer_out, *high = leave(
         where,
-        (both_0, rest_1),
-        (L + cut, 0),
+        (both_0, most_1, rest_1),
+        [lambda b: L + b, lambda b: L + jnp.minimum(b, cut - 1), lambda b: jnp.maximum(b - cut, 0)],
         down_second,
         tokens,
         cotangent,
         scale,
         sizes,
         False,
+        0,
+        L,
+        None,
         cut,
-        L - cut,
-        layer_out,
-        True,
     )
     waited = (mid_1,)
     high[0], high[1], *got = together(*high[:2], *[array for sums in waited for array in sums.got()])
@@ -512,17 +498,16 @@
         count = len(sums.got())
         sums.replace(got[:count])
         got = got[count:]
-    streams = [(keep, [swap(send, 0, "high_core")], 0) for send, keep in zip(high[:2], high[2:])]
-    edge_high = Halving(streams, "high", False)
-    edge_high.move(edge_high.add(L - cut))
+    edge_high = edge_sums(high, "high")
+    edge_high.move(edge_high.add(L))
     done_0, done_1 = mid_0.run(lead), mid_1.run(lead)
     grad_up_second, grad_down_first = finish([[done_0[0], done_1[0]], [done_0[1], done_1[1]]])
-    done_first, done_low = edge_first.run(lead), edge_low.run(cut)
+    done_first = edge_first.run(L)
     got = together(*edge_high.got(), grad_up_second, grad_down_first)
     edge_high.replace(got[:-2])
-    done_high = edge_high.run(L - cut)
-    (grad_up_first,) = finish([done_first])
-    (grad_down_second,) = finish([done_low + [tuple(done_high)]])
+    done_high = edge_high.run(L)
+    (grad_up_first,) = finish([[tuple(done_first)]])
+    (grad_down_second,) = finish([[tuple(done_high)]])
     return (
         layer_out,
         grad_tokens,

time: 219 us -> 216 us (0.986)
  waiting for transfers between devices: 78.9 us -> 81.9 us
  starting transfers between devices: 46.6 us -> 43.8 us
  Pallas kernels: 86 us -> 83.6 us
    pallas_call x4 -> x2, Pallas kernels: 14.9 us -> 11.9 us  [leave(): pl.pallas_call(kernel, name='leave_back' if backward else 'leave_out', gr...]
    ppermute x30 -> x24, waiting for transfers between devices: 24.3 us -> 27.3 us  [swap(): return lax.ppermute(value, 'dp', [(s, s ^ 1 << bit) for s in range(count)])]
    ppermute x30 -> x24, starting transfers between devices: 22.3 us -> 19.7 us  [swap(): return lax.ppermute(value, 'dp', [(s, s ^ 1 << bit) for s in range(count)])]
    unnamed x36 -> x32, local copies, waits for them, and re-layouts: 6.06 us -> 5.34 us
    pallas_call x8 -> x6, Pallas kernels: 5.84 us -> 6.47 us  [split_small(): pl.pallas_call(kernel, name='small', in_specs=[pl.BlockSpec(memory_space=...]
  transfers between devices with their start and end apart: 35 -> 29, of which waited for: 15 -> 17; matrix products, arithmetic and copies ran while one was open for 0% -> 0% of each run, Pallas kernels for 36% -> 35%
where the time goes in v5:
time: 216 us
  Pallas kernels  83.6 us (39%)
  waiting for transfers between devices  81.9 us (38%)
  starting transfers between devices  43.8 us (20%)
  local copies, waits for them, and re-layouts  5.34 us (2%)
    all_to_all x5, waiting for transfers between devices, regroup(): lax.all_to_all(pieces, 'tensor', split_axis=0, concat_axis=0, tiled=True)  54.6 us
    pallas_call x2, Pallas kernels, middle(): pl.pallas_call(kernel, name='middle', grid_spec=pltpu.PrefetchScalarGridS...  38.2 us
    ppermute x24, waiting for transfers between devices, swap(): return lax.ppermute(value, 'dp', [(s, s ^ 1 << bit) for s in range(count)])  27.3 us
    all_to_all x5, starting transfers between devices, regroup(): lax.all_to_all(pieces, 'tensor', split_axis=0, concat_axis=0, tiled=True)  24.1 us
    ppermute x24, starting transfers between devices, swap(): return lax.ppermute(value, 'dp', [(s, s ^ 1 << bit) for s in range(count)])  19.7 us
    pallas_call x2, Pallas kernels, split(): pl.pallas_call(kernel, name='split', grid_spec=pltpu.PrefetchScalarGridSp...  12.8 us
    pallas_call x2, Pallas kernels, leave(): pl.pallas_call(kernel, name='leave_back' if backward else 'leave_out', gr...  11.9 us
    pallas_call x6, Pallas kernels, split_small(): pl.pallas_call(kernel, name='small', in_specs=[pl.BlockSpec(memory_space=...  6.47 us
  transfers between devices with their start and end apart: 29, of which 17 were waited for; matrix products, arithmetic and copies ran while one was open for 0% of the time, Pallas kernels for 35%

profile of v5, /device:TPU:0, one launch (start us, length us, event | category | flops | bytes accessed | tf_op | source)
XLA Modules:
  0.0 215.6 jit_solution(1743095740243801153)
XLA Ops:
  0.6 6.3 %enter.1 = (bf16[4,2,2,4,32,384]{5,4,3,2,1,0:T(8,128)(2,1)}, bf16[4,2,2,4,32,384]{5,4,3,2,1,0:T(8,128)(2,1)}) custom-call(bf16[384,2048]{1,0:T(8,128)(2,1)} %refs_4_.1, bf16[4,512,512]{2,1,0:T(8,128)(2,1)} %refs_2_.5, bf16[384,2048]{1,0:T(8,128)(2,1)} %refs_5_.1, bf16[4,512,512]{2,1,0:T(8,128)(2,1)} %refs_3_.3), custom_call_target="tpu_custom_call" | custom-call | tf_op jit(solution)/shard_map/enter/pallas_call | solution.py:59
  7.0 6.3 %all-to-all-start = ((bf16[4,2,2,4,32,384]{5,4,3,2,1,0:T(8,128)(2,1)}), bf16[4,2,2,4,32,384]{5,4,3,2,1,0:T(8,128)(2,1)S(1)}, u32[]{:S(2)}, u32[]{:S(2)}) async-start(bf16[4,2,2,4,32,384]{5,4,3,2,1,0:T(8,128)(2,1)} %get-tuple-element.89), calls=%async_computation | async-start | bytes 3145728 | tf_op jit(solution)/shard_map/z1/all_to_all | solution.py:249
  13.3 3.8 %turn.1.refs_4_ = bf16[4,4,2,64,384]{4,3,2,1,0:T(8,128)(2,1)} custom-call(bf16[384,2048]{1,0:T(8,128)(2,1)} %refs_4_.1), custom_call_target="tpu_custom_call" | custom-call | tf_op jit(solution)/shard_map/turn/pallas_call | solution.py:79
  17.1 33.1 %all-to-all-done.refs_0_ = bf16[4,2,2,4,32,384]{5,4,3,2,1,0:T(8,128)(2,1)S(1)} async-done(((bf16[4,2,2,4,32,384]{5,4,3,2,1,0:T(8,128)(2,1)}), bf16[4,2,2,4,32,384]{5,4,3,2,1,0:T(8,128)(2,1)S(1)}, u32[]{:S(2)}, u32[]{:S(2)}) %all-to-all-start) | async-done | bytes 1572896 | tf_op jit(solution)/shard_map/z1/all_to_all | solution.py:249
  50.3 4.3 %all-to-all-start.1 = ((bf16[4,2,2,4,32,384]{5,4,3,2,1,0:T(8,128)(2,1)}), bf16[4,2,2,4,32,384]{5,4,3,2,1,0:T(8,128)(2,1)}, u32[]{:S(2)}, u32[]{:S(2)}) async-start(bf16[4,2,2,4,32,384]{5,4,3,2,1,0:T(8,128)(2,1)} %get-tuple-element.91), calls=%async_computation.1 | async-start | bytes 3145728 | tf_op jit(solution)/shard_map/z2/all_to_all | solution.py:249
  54.6 19.0 %middle.2 = (bf16[4,2,8,32,384]{4,3,2,1,0:T(8,128)(2,1)}, bf16[2,4,64,2048]{3,2,1,0:T(8,128)(2,1)}, bf16[2,4,64,2048]{3,2,1,0:T(8,128)(2,1)}, bf16[2,4,256,512]{3,2,1,0:T(8,128)(2,1)}, bf16[2,4,256,512]{3,2,1,0:T(8,128)(2,1)}) custom-call(s32[1]{0:T(128)} %bitcast.where_ref, bf16[4,2,2,4,32,384]{5,4,3,2,1,0:T(8,128)(2,1)} %copy-done.15, ...), custom_call_target="tpu_custom_call" | custom-call | tf_op jit(solution)/shard_map/middle/pallas_call | solution.py:140
  74.2 6.1 %collective-permute-done.refs_1_.refs_3_ = bf16[2,4,64,2048]{3,2,1,0:T(8,128)(2,1)S(1)} collective-permute-done((bf16[2,4,64,2048]{3,2,1,0:T(8,128)(2,1)}, bf16[2,4,64,2048]{3,2,1,0:T(8,128)(2,1)S(1)}, u32[]{:S(2)}, u32[]{:S(2)}) %collective-permute-start) | collective-permute-done | bytes 2097184 | tf_op jit(solution)/shard_map/mid0_core/ppermute | solution.py:255
  81.7 6.4 %split.2 = (bf16[2,2,64,2048]{3,2,1,0:T(8,128)(2,1)}, bf16[2,2,64,2048]{3,2,1,0:T(8,128)(2,1)}, bf16[2,2,256,512]{3,2,1,0:T(8,128)(2,1)}, bf16[2,2,256,512]{3,2,1,0:T(8,128)(2,1)}) custom-call(s32[2]{0:T(128)S(1)} %pad_add_fusion.which_ref, bf16[2,4,64,2048]{3,2,1,0:T(8,128)(2,1)} %get-tuple-element.94.refs_0_.refs_2_, bf16[2,4,64,2048]{3,2,1,0:T(8,128)(2,1)} %copy-done.14, ...), custom_call_target="tpu_custom_call" | custom-call | tf_op jit(solution)/shard_map/split/pallas_call | solution.py:283
  88.1 1.6 collective-permute-start.2
  89.7 1.5 collective-permute-start.3
  91.2 5.0 %all-to-all-start.2 = ((bf16[4,2,8,32,384]{4,3,2,1,0:T(8,128)(2,1)}), bf16[4,2,8,32,384]{4,3,2,1,0:T(8,128)(2,1)}, u32[]{:S(2)}, u32[]{:S(2)}) async-start(bf16[4,2,8,32,384]{4,3,2,1,0:T(8,128)(2,1)} %get-tuple-element.100), calls=%async_computation.2 | async-start | bytes 3145728 | tf_op jit(solution)/shard_map/z3/all_to_all | solution.py:249
  96.2 19.2 %middle.3 = (bf16[4,2,5,32,384]{4,3,2,1,0:T(8,128)(2,1)}, bf16[4,2,3,32,384]{4,3,2,1,0:T(8,128)(2,1)}, bf16[2,4,64,2048]{3,2,1,0:T(8,128)(2,1)}, bf16[2,4,64,204...) custom-call(s32[1]{0:T(128)} %bitcast.where_ref, ...), custom_call_target="tpu_custom_call" | custom-call | tf_op jit(solution)/shard_map/middle/pallas_call | solution.py:140
  118.6 14.4 %all-to-all-done.2.refs_0_ = bf16[4,2,8,32,384]{4,3,2,1,0:T(8,128)(2,1)} async-done(((bf16[4,2,8,32,384]{4,3,2,1,0:T(8,128)(2,1)}), bf16[4,2,8,32,384]{4,3,2,1,0:T(8,128)(2,1)}, u32[]{:S(2)}, u32[]{:S(2)}) %all-to-all-start.2) | async-done | bytes 1572896 | tf_op jit(solution)/shard_map/z3/all_to_all | solution.py:249
  133.0 4.2 %all-to-all-start.3 = ((bf16[4,2,5,32,384]{4,3,2,1,0:T(8,128)(2,1)}), bf16[4,2,5,32,384]{4,3,2,1,0:T(8,128)(2,1)}, u32[]{:S(2)}, u32[]{:S(2)}) async-start(bf16[4,2,5,32,384]{4,3,2,1,0:T(8,128)(2,1)} %get-tuple-element.112), calls=%async_computation.3 | async-start | bytes 1966080 | tf_op jit(solution)/shard_map/z4/all_to_all | solution.py:249
  137.8 1.5 collective-permute-start.5
  139.3 6.4 %split.3 = (bf16[2,2,64,2048]{3,2,1,0:T(8,128)(2,1)}, bf16[2,2,64,2048]{3,2,1,0:T(8,128)(2,1)}, bf16[2,2,256,512]{3,2,1,0:T(8,128)(2,1)}, bf16[2,2,256,512]{3,2,1,0:T(8,128)(2,1)}) custom-call(s32[2]{0:T(128)S(1)} %pad_add_fusion.which_ref, bf16[2,4,64,2048]{3,2,1,0:T(8,128)(2,1)} %get-tuple-element.114.refs_0_.refs_2_, ...), custom_call_target="tpu_custom_call" | custom-call | tf_op jit(solution)/shard_map/split/pallas_call | solution.py:283
  145.7 4.7 %collective-permute-done.4.refs_1_ = bf16[2,1,64,2048]{3,2,1,0:T(8,128)(2,1)S(1)} collective-permute-done((bf16[2,1,64,2048]{3,2,1,0:T(8,128)(2,1)}, bf16[2,1,64,2048]{3,2,1,0:T(8,128)(2,1)S(1)}, u32[]{:S(2)}, u32[]{:S(2)}) %collective-permute-start.4) | collective-permute-done | bytes 524320 | tf_op jit(solution)/shard_map/mid0_bit1/ppermute | solution.py:255
  154.0 7.1 %all-to-all-done.3.refs_1_ = bf16[4,2,5,32,384]{4,3,2,1,0:T(8,128)(2,1)} async-done(((bf16[4,2,5,32,384]{4,3,2,1,0:T(8,128)(2,1)}), bf16[4,2,5,32,384]{4,3,2,1,0:T(8,128)(2,1)}, u32[]{:S(2)}, u32[]{:S(2)}) %all-to-all-start.3) | async-done | bytes 983072 | tf_op jit(solution)/shard_map/z4/all_to_all | solution.py:249
  161.1 4.2 %all-to-all-start.4 = ((bf16[4,2,3,32,384]{4,3,2,1,0:T(8,128)(2,1)}), bf16[4,2,3,32,384]{4,3,2,1,0:T(8,128)(2,1)}, u32[]{:S(2)}, u32[]{:S(2)}) async-start(bf16[4,2,3,32,384]{4,3,2,1,0:T(8,128)(2,1)} %get-tuple-element.123), calls=%async_computation.4 | async-start | bytes 1179648 | tf_op jit(solution)/shard_map/z5/all_to_all | solution.py:249
  165.3 5.9 %leave_back.1 = (bf16[384,2048]{1,0:T(8,128)(2,1)}, bf16[4,4,32,512]{3,2,1,0:T(8,128)(2,1)S(1)}, bf16[4,4,32,512]{3,2,1,0:T(8,128)(2,1)S(1)}, bf16[4,4,32,512]{3...) custom-call(s32[1]{0:T(128)} %bitcast.where_ref, bf16[4,2,8,32,384]{4,3,2,1,0:T(8,128)(2,1)} %all-to-all-done.2.refs_0_, ...), custom_call_target="tpu_custom_call" | custom-call | tf_op jit(solution)/shard_map/leave_back/pallas_call | solution.py:219
  171.7 3.8 %collective-permute-done.10.refs_1_ = bf16[2,2,64,2048]{3,2,1,0:T(8,128)(2,1)S(1)} collective-permute-done((bf16[2,2,64,2048]{3,2,1,0:T(8,128)(2,1)}, bf16[2,2,64,2048]{3,2,1,0:T(8,128)(2,1)S(1)}, u32[]{:S(2)}, u32[]{:S(2)}) %collective-permute-start.10) | collective-permute-done | bytes 1048608 | tf_op jit(solution)/shard_map/mid1_bit0/ppermute | solution.py:255
  175.9 1.9 small.8
  182.9 6.0 %leave_out.1 = (bf16[384,2048]{1,0:T(8,128)(2,1)}, bf16[4,4,32,512]{3,2,1,0:T(8,128)(2,1)S(1)}, bf16[4,4,32,512]{3,2,1,0:T(8,128)(2,1)S(1)}, bf16[4,4,32,512]{3,...) custom-call(s32[1]{0:T(128)} %bitcast.where_ref, bf16[4,2,8,32,384]{4,3,2,1,0:T(8,128)(2,1)} %all-to-all-done.2.refs_0_, ...), custom_call_target="tpu_custom_call" | custom-call | tf_op jit(solution)/shard_map/leave_out/pallas_call | solution.py:219
  188.9 1.6 collective-permute-done.16.refs_3_
  192.7 1.5 collective-permute-start.13
  195.7 1.5 collective-permute-start.21
  197.2 4.3 %collective-permute-done.12.refs_1_ = bf16[4,2,32,512]{3,2,1,0:T(8,128)(2,1)S(1)} collective-permute-done((bf16[4,2,32,512]{3,2,1,0:T(8,128)(2,1)}, bf16[4,2,32,512]{3,2,1,0:T(8,128)(2,1)S(1)}, u32[]{:S(2)}, u32[]{:S(2)}) %collective-permute-start.12) | collective-permute-done | bytes 262176 | tf_op jit(solution)/shard_map/first_bit0/ppermute | solution.py:255
  202.6 1.6 collective-permute-start.14
  204.7 2.3 %finish.4 = (f32[4,64,2048]{2,1,0:T(8,128)}, f32[4,256,512]{2,1,0:T(8,128)}) custom-call(bf16[2,1,64,2048]{3,2,1,0:T(8,128)(2,1)S(1)} %get-tuple-element.152.refs_0_, bf16[2,1,64,2048]{3,2,1,0:T(8,128)(2,1)S(1)} %copy-done.5, bf16[2,1,64,2048]{3,2,1,0:T(8,128)(2,1)S(1)} %copy-done.9, bf16[2,1,64,2048]{3,2,1,0:T(8,128)(2,1)S(1)} %collective-permute-done.16.refs_3_, ...), custom_call_target="tpu_custom_call" | custom-call | tf_op jit(solution)/shard_map/finish/pallas_call | solution.py:363
  208.2 1.6 collective-permute-start.22
  211.2 2.1 collective-permute-done.22.refs_1_
  213.2 1.5 collective-permute-done.23.refs_3_
  (77 shorter events, 24.0 us)
Async XLA Ops:
  7.0 43.3 %all-to-all-start = ((bf16[4,2,2,4,32,384]{5,4,3,2,1,0:T(8,128)(2,1)}), bf16[4,2,2,4,32,384]{5,4,3,2,1,0:T(8,128)(2,1)S(1)}, u32[]{:S(2)}, u32[]{:S(2)}) async-start(bf16[4,2,2,4,32,384]{5,4,3,2,1,0:T(8,128)(2,1)} %get-tuple-element.89), calls=%async_computation | async-start | bytes 3145728 | tf_op jit(solution)/shard_map/z1/all_to_all | solution.py:249
  50.3 40.9 %all-to-all-start.1 = ((bf16[4,2,2,4,32,384]{5,4,3,2,1,0:T(8,128)(2,1)}), bf16[4,2,2,4,32,384]{5,4,3,2,1,0:T(8,128)(2,1)}, u32[]{:S(2)}, u32[]{:S(2)}) async-start(bf16[4,2,2,4,32,384]{5,4,3,2,1,0:T(8,128)(2,1)} %get-tuple-element.91), calls=%async_computation.1 | async-start | bytes 3145728 | tf_op jit(solution)/shard_map/z2/all_to_all | solution.py:249
  73.6 6.7 %collective-permute-start = (bf16[2,4,64,2048]{3,2,1,0:T(8,128)(2,1)}, bf16[2,4,64,2048]{3,2,1,0:T(8,128)(2,1)S(1)}, u32[]{:S(2)}, u32[]{:S(2)}) collective-permute-start(bf16[2,4,64,2048]{3,2,1,0:T(8,128)(2,1)} %get-tuple-element.95), channel_id=1, source_target_pairs={{0,4},{4,0},{8,12},{12,8},{16,20},{20,16},{24,28},{28,24},{1,5},{5... | collective-permute-start | bytes 6291464 | tf_op jit(solution)/shard_map/mid0_core/ppermute | solution.py:255
  73.6 7.5 %collective-permute-start.1 = (bf16[2,4,256,512]{3,2,1,0:T(8,128)(2,1)}, bf16[2,4,256,512]{3,2,1,0:T(8,128)(2,1)}, u32[]{:S(2)}, u32[]{:S(2)}) collective-permute-start(bf16[2,4,256,512]{3,2,1,0:T(8,128)(2,1)} %get-tuple-element.97), channel_id=1, source_target_pairs={{0,4},{4,0},{8,12},{12,8},{16,20},{20,16},{24,28},{28,24},{1,5},{5... | collective-permute-start | bytes 6291464 | tf_op jit(solution)/shard_map/mid0_core/ppermute | solution.py:255
  88.1 27.3 %collective-permute-start.2 = (bf16[2,2,64,2048]{3,2,1,0:T(8,128)(2,1)}, bf16[2,2,64,2048]{3,2,1,0:T(8,128)(2,1)S(1)}, u32[]{:S(2)}, u32[]{:S(2)}) collective-permute-start(bf16[2,2,64,2048]{3,2,1,0:T(8,128)(2,1)} %get-tuple-element.98), channel_id=1, source_target_pairs={{0,8},{4,12},{8,0},{12,4},{16,24},{20,28},{24,16},{28,20},{1,9},{5... | collective-permute-start | bytes 3145736 | tf_op jit(solution)/shard_map/mid0_bit0/ppermute | solution.py:255
  89.7 25.7 %collective-permute-start.3 = (bf16[2,2,256,512]{3,2,1,0:T(8,128)(2,1)}, bf16[2,2,256,512]{3,2,1,0:T(8,128)(2,1)S(1)}, u32[]{:S(2)}, u32[]{:S(2)}) collective-permute-start(bf16[2,2,256,512]{3,2,1,0:T(8,128)(2,1)} %get-tuple-element.99), channel_id=1, source_target_pairs={{0,16},{4,20},{8,24},{12,28},{16,0},{20,4},{24,8},{28,12},{1,17},{... | collective-permute-start | bytes 3145736 | tf_op jit(solution)/shard_map/mid0_bit1/ppermute | solution.py:255
  91.2 41.8 %all-to-all-start.2 = ((bf16[4,2,8,32,384]{4,3,2,1,0:T(8,128)(2,1)}), bf16[4,2,8,32,384]{4,3,2,1,0:T(8,128)(2,1)}, u32[]{:S(2)}, u32[]{:S(2)}) async-start(bf16[4,2,8,32,384]{4,3,2,1,0:T(8,128)(2,1)} %get-tuple-element.100), calls=%async_computation.2 | async-start | bytes 3145728 | tf_op jit(solution)/shard_map/z3/all_to_all | solution.py:249
  96.2 19.8 %copy-start.2 = (bf16[2,2,64,2048]{3,2,1,0:T(8,128)(2,1)S(1)}, bf16[2,2,64,2048]{3,2,1,0:T(8,128)(2,1)}, u32[]{:S(2)}) copy-start(bf16[2,2,64,2048]{3,2,1,0:T(8,128)(2,1)} %get-tuple-element.103.refs_0_) | copy-start | bytes 3145732
  96.2 19.8 %copy-start.3 = (bf16[2,2,256,512]{3,2,1,0:T(8,128)(2,1)S(1)}, bf16[2,2,256,512]{3,2,1,0:T(8,128)(2,1)}, u32[]{:S(2)}) copy-start(bf16[2,2,256,512]{3,2,1,0:T(8,128)(2,1)} %get-tuple-element.107.refs_2_) | copy-start | bytes 3145732
  115.4 23.9 %collective-permute-start.6 = (bf16[2,4,64,2048]{3,2,1,0:T(8,128)(2,1)}, bf16[2,4,64,2048]{3,2,1,0:T(8,128)(2,1)}, u32[]{:S(2)}, u32[]{:S(2)}) collective-permute-start(bf16[2,4,64,2048]{3,2,1,0:T(8,128)(2,1)} %get-tuple-element.115), channel_id=1, source_target_pairs={{0,4},{4,0},{8,12},{12,8},{16,20},{20,16},{24,28},{28,24},{1,5},{5... | collective-permute-start | bytes 6291464 | tf_op jit(solution)/shard_map/mid1_core/ppermute | solution.py:255
  115.5 23.9 %collective-permute-start.7 = (bf16[2,4,256,512]{3,2,1,0:T(8,128)(2,1)}, bf16[2,4,256,512]{3,2,1,0:T(8,128)(2,1)}, u32[]{:S(2)}, u32[]{:S(2)}) collective-permute-start(bf16[2,4,256,512]{3,2,1,0:T(8,128)(2,1)} %get-tuple-element.117), channel_id=1, source_target_pairs={{0,4},{4,0},{8,12},{12,8},{16,20},{20,16},{24,28},{28,24},{1,5},{5... | collective-permute-start | bytes 6291464 | tf_op jit(solution)/shard_map/mid1_core/ppermute | solution.py:255
  133.0 28.1 %all-to-all-start.3 = ((bf16[4,2,5,32,384]{4,3,2,1,0:T(8,128)(2,1)}), bf16[4,2,5,32,384]{4,3,2,1,0:T(8,128)(2,1)}, u32[]{:S(2)}, u32[]{:S(2)}) async-start(bf16[4,2,5,32,384]{4,3,2,1,0:T(8,128)(2,1)} %get-tuple-element.112), calls=%async_computation.3 | async-start | bytes 1966080 | tf_op jit(solution)/shard_map/z4/all_to_all | solution.py:249
  137.2 13.2 %collective-permute-start.4 = (bf16[2,1,64,2048]{3,2,1,0:T(8,128)(2,1)}, bf16[2,1,64,2048]{3,2,1,0:T(8,128)(2,1)S(1)}, u32[]{:S(2)}, u32[]{:S(2)}) collective-permute-start(bf16[2,1,64,2048]{3,2,1,0:T(8,128)(2,1)} %copy-done.13), channel_id=1, source_target_pairs={{0,16},{4,20},{8,24},{12,28},{16,0},{20,4},{24,8},{28,12},{1,17},{... | collective-permute-start | bytes 1572872 | tf_op jit(solution)/shard_map/mid0_bit1/ppermute | solution.py:255
  137.8 13.4 %collective-permute-start.5 = (bf16[2,1,256,512]{3,2,1,0:T(8,128)(2,1)}, bf16[2,1,256,512]{3,2,1,0:T(8,128)(2,1)S(1)}, u32[]{:S(2)}, u32[]{:S(2)}) collective-permute-start(bf16[2,1,256,512]{3,2,1,0:T(8,128)(2,1)} %copy-done.12), channel_id=1, source_target_pairs={{0,8},{4,12},{8,0},{12,4},{16,24},{20,28},{24,16},{28,20},{1,9},{5... | collective-permute-start | bytes 1572872 | tf_op jit(solution)/shard_map/mid0_bit0/ppermute | solution.py:255
  152.0 23.5 %collective-permute-start.10 = (bf16[2,2,64,2048]{3,2,1,0:T(8,128)(2,1)}, bf16[2,2,64,2048]{3,2,1,0:T(8,128)(2,1)S(1)}, u32[]{:S(2)}, u32[]{:S(2)}) collective-permute-start(bf16[2,2,64,2048]{3,2,1,0:T(8,128)(2,1)} %get-tuple-element.120), channel_id=1, source_target_pairs={{0,8},{4,12},{8,0},{12,4},{16,24},{20,28},{24,16},{28,20},{1,9},{5... | collective-permute-start | bytes 3145736 | tf_op jit(solution)/shard_map/mid1_bit0/ppermute | solution.py:255
  152.9 22.9 %collective-permute-start.11 = (bf16[2,2,256,512]{3,2,1,0:T(8,128)(2,1)}, bf16[2,2,256,512]{3,2,1,0:T(8,128)(2,1)S(1)}, u32[]{:S(2)}, u32[]{:S(2)}) collective-permute-start(bf16[2,2,256,512]{3,2,1,0:T(8,128)(2,1)} %get-tuple-element.121), channel_id=1, source_target_pairs={{0,16},{4,20},{8,24},{12,28},{16,0},{20,4},{24,8},{28,12},{1,17},{... | collective-permute-start | bytes 3145736 | tf_op jit(solution)/shard_map/mid1_bit1/ppermute | solution.py:255
  161.1 21.7 %all-to-all-start.4 = ((bf16[4,2,3,32,384]{4,3,2,1,0:T(8,128)(2,1)}), bf16[4,2,3,32,384]{4,3,2,1,0:T(8,128)(2,1)}, u32[]{:S(2)}, u32[]{:S(2)}) async-start(bf16[4,2,3,32,384]{4,3,2,1,0:T(8,128)(2,1)} %get-tuple-element.123), calls=%async_computation.4 | async-start | bytes 1179648 | tf_op jit(solution)/shard_map/z5/all_to_all | solution.py:249
  171.2 10.2 %collective-permute-start.8 = (bf16[4,4,32,512]{3,2,1,0:T(8,128)(2,1)S(1)}, bf16[4,4,32,512]{3,2,1,0:T(8,128)(2,1)S(1)}, u32[]{:S(2)}, u32[]{:S(2)}) collective-permute-start(bf16[4,4,32,512]{3,2,1,0:T(8,128)(2,1)S(1)} %get-tuple-element.126), channel_id=1, source_target_pairs={{0,4},{4,0},{8,12},{12,8},{16,20},{20,16},{24,28},{28,24},{1,5},{5... | collective-permute-start | bytes 1572872 | tf_op jit(solution)/shard_map/first_core/ppermute | solution.py:255
  171.2 10.2 %collective-permute-start.9 = (bf16[4,4,32,512]{3,2,1,0:T(8,128)(2,1)S(1)}, bf16[4,4,32,512]{3,2,1,0:T(8,128)(2,1)S(1)}, u32[]{:S(2)}, u32[]{:S(2)}) collective-permute-start(bf16[4,4,32,512]{3,2,1,0:T(8,128)(2,1)S(1)} %get-tuple-element.128), channel_id=1, source_target_pairs={{0,4},{4,0},{8,12},{12,8},{16,20},{20,16},{24,28},{28,24},{1,5},{5... | collective-permute-start | bytes 1572872 | tf_op jit(solution)/shard_map/first_core/ppermute | solution.py:255
  179.4 11.1 %collective-permute-start.16 = (bf16[2,1,64,2048]{3,2,1,0:T(8,128)(2,1)}, bf16[2,1,64,2048]{3,2,1,0:T(8,128)(2,1)S(1)}, u32[]{:S(2)}, u32[]{:S(2)}) collective-permute-start(bf16[2,1,64,2048]{3,2,1,0:T(8,128)(2,1)} %get-tuple-element.133), channel_id=1, source_target_pairs={{0,16},{4,20},{8,24},{12,28},{16,0},{20,4},{24,8},{28,12},{1,17},{... | collective-permute-start | bytes 1572872 | tf_op jit(solution)/shard_map/mid1_bit1/ppermute | solution.py:255
  180.7 10.9 %collective-permute-start.17 = (bf16[2,1,256,512]{3,2,1,0:T(8,128)(2,1)}, bf16[2,1,256,512]{3,2,1,0:T(8,128)(2,1)S(1)}, u32[]{:S(2)}, u32[]{:S(2)}) collective-permute-start(bf16[2,1,256,512]{3,2,1,0:T(8,128)(2,1)} %get-tuple-element.134), channel_id=1, source_target_pairs={{0,8},{4,12},{8,0},{12,4},{16,24},{20,28},{24,16},{28,20},{1,9},{5... | collective-permute-start | bytes 1572872 | tf_op jit(solution)/shard_map/mid1_bit0/ppermute | solution.py:255
  188.9 15.8 %copy-start.7 = (bf16[2,1,256,512]{3,2,1,0:T(8,128)(2,1)S(1)}, bf16[2,1,256,512]{3,2,1,0:T(8,128)(2,1)}, u32[]{:S(2)}) copy-start(bf16[2,1,256,512]{3,2,1,0:T(8,128)(2,1)} %copy-done.6) | copy-start | bytes 1572868
  191.6 2.6 %collective-permute-start.18 = (bf16[4,4,32,512]{3,2,1,0:T(8,128)(2,1)S(1)}, bf16[4,4,32,512]{3,2,1,0:T(8,128)(2,1)S(1)}, u32[]{:S(2)}, u32[]{:S(2)}) collective-permute-start(bf16[4,4,32,512]{3,2,1,0:T(8,128)(2,1)S(1)} %get-tuple-element.147), channel_id=1, source_target_pairs={{0,4},{4,0},{8,12},{12,8},{16,20},{20,16},{24,28},{28,24},{1,5},{5... | collective-permute-start | bytes 1572872 | tf_op jit(solution)/shard_map/high_core/ppermute | solution.py:255
  191.6 2.7 %collective-permute-start.19 = (bf16[4,4,32,512]{3,2,1,0:T(8,128)(2,1)S(1)}, bf16[4,4,32,512]{3,2,1,0:T(8,128)(2,1)S(1)}, u32[]{:S(2)}, u32[]{:S(2)}) collective-permute-start(bf16[4,4,32,512]{3,2,1,0:T(8,128)(2,1)S(1)} %get-tuple-element.149), channel_id=1, source_target_pairs={{0,4},{4,0},{8,12},{12,8},{16,20},{20,16},{24,28},{28,24},{1,5},{5... | collective-permute-start | bytes 1572872 | tf_op jit(solution)/shard_map/high_core/ppermute | solution.py:255
  192.1 9.4 %collective-permute-start.12 = (bf16[4,2,32,512]{3,2,1,0:T(8,128)(2,1)}, bf16[4,2,32,512]{3,2,1,0:T(8,128)(2,1)S(1)}, u32[]{:S(2)}, u32[]{:S(2)}) collective-permute-start(bf16[4,2,32,512]{3,2,1,0:T(8,128)(2,1)} %get-tuple-element.129), channel_id=1, source_target_pairs={{0,8},{4,12},{8,0},{12,4},{16,24},{20,28},{24,16},{28,20},{1,9},{5... | collective-permute-start | bytes 786440 | tf_op jit(solution)/shard_map/first_bit0/ppermute | solution.py:255
  192.7 9.2 %collective-permute-start.13 = (bf16[4,2,32,512]{3,2,1,0:T(8,128)(2,1)S(1)}, bf16[4,2,32,512]{3,2,1,0:T(8,128)(2,1)S(1)}, u32[]{:S(2)}, u32[]{:S(2)}) collective-permute-start(bf16[4,2,32,512]{3,2,1,0:T(8,128)(2,1)S(1)} %get-tuple-element.130), channel_id=1, source_target_pairs={{0,16},{4,20},{8,24},{12,28},{16,0},{20,4},{24,8},{28,12},{1,17},{... | collective-permute-start | bytes 786440 | tf_op jit(solution)/shard_map/first_bit1/ppermute | solution.py:255
  195.1 12.1 %collective-permute-start.20 = (bf16[4,2,32,512]{3,2,1,0:T(8,128)(2,1)S(1)}, bf16[4,2,32,512]{3,2,1,0:T(8,128)(2,1)S(1)}, u32[]{:S(2)}, u32[]{:S(2)}) collective-permute-start(bf16[4,2,32,512]{3,2,1,0:T(8,128)(2,1)S(1)} %get-tuple-element.150), channel_id=1, source_target_pairs={{0,8},{4,12},{8,0},{12,4},{16,24},{20,28},{24,16},{28,20},{1,9},{5... | collective-permute-start | bytes 786440 | tf_op jit(solution)/shard_map/high_bit0/ppermute | solution.py:255
  195.7 11.8 %collective-permute-start.21 = (bf16[4,2,32,512]{3,2,1,0:T(8,128)(2,1)S(1)}, bf16[4,2,32,512]{3,2,1,0:T(8,128)(2,1)S(1)}, u32[]{:S(2)}, u32[]{:S(2)}) collective-permute-start(bf16[4,2,32,512]{3,2,1,0:T(8,128)(2,1)S(1)} %get-tuple-element.151), channel_id=1, source_target_pairs={{0,16},{4,20},{8,24},{12,28},{16,0},{20,4},{24,8},{28,12},{1,17},{... | collective-permute-start | bytes 786440 | tf_op jit(solution)/shard_map/high_bit1/ppermute | solution.py:255
  202.6 7.7 %collective-permute-start.14 = (bf16[4,1,32,512]{3,2,1,0:T(8,128)(2,1)S(1)}, bf16[4,1,32,512]{3,2,1,0:T(8,128)(2,1)S(1)}, u32[]{:S(2)}, u32[]{:S(2)}) collective-permute-start(bf16[4,1,32,512]{3,2,1,0:T(8,128)(2,1)S(1)} %get-tuple-element.141), channel_id=1, source_target_pairs={{0,16},{4,20},{8,24},{12,28},{16,0},{20,4},{24,8},{28,12},{1,17},{... | collective-permute-start | bytes 393224 | tf_op jit(solution)/shard_map/first_bit1/ppermute | solution.py:255
  204.1 6.2 %collective-permute-start.15 = (bf16[4,1,32,512]{3,2,1,0:T(8,128)(2,1)S(1)}, bf16[4,1,32,512]{3,2,1,0:T(8,128)(2,1)S(1)}, u32[]{:S(2)}, u32[]{:S(2)}) collective-permute-start(bf16[4,1,32,512]{3,2,1,0:T(8,128)(2,1)S(1)} %get-tuple-element.143), channel_id=1, source_target_pairs={{0,8},{4,12},{8,0},{12,4},{16,24},{20,28},{24,16},{28,20},{1,9},{5... | collective-permute-start | bytes 393224 | tf_op jit(solution)/shard_map/first_bit0/ppermute | solution.py:255
  208.2 5.0 %collective-permute-start.22 = (bf16[4,1,32,512]{3,2,1,0:T(8,128)(2,1)S(1)}, bf16[4,1,32,512]{3,2,1,0:T(8,128)(2,1)S(1)}, u32[]{:S(2)}, u32[]{:S(2)}) collective-permute-start(bf16[4,1,32,512]{3,2,1,0:T(8,128)(2,1)S(1)} %get-tuple-element.169), channel_id=1, source_target_pairs={{0,16},{4,20},{8,24},{12,28},{16,0},{20,4},{24,8},{28,12},{1,17},{... | collective-permute-start | bytes 393224 | tf_op jit(solution)/shard_map/high_bit1/ppermute | solution.py:255
  209.8 5.0 %collective-permute-start.23 = (bf16[4,1,32,512]{3,2,1,0:T(8,128)(2,1)S(1)}, bf16[4,1,32,512]{3,2,1,0:T(8,128)(2,1)S(1)}, u32[]{:S(2)}, u32[]{:S(2)}) collective-permute-start(bf16[4,1,32,512]{3,2,1,0:T(8,128)(2,1)S(1)} %get-tuple-element.171), channel_id=1, source_target_pairs={{0,8},{4,12},{8,0},{12,4},{16,24},{20,28},{24,16},{28,20},{1,9},{5... | collective-permute-start | bytes 393224 | tf_op jit(solution)/shard_map/high_bit0/ppermute | solution.py:255
  (13 other events, 79.1 us)

commit v6 on v5

--- a/solution.py
+++ b/solution.py
@@ -454,13 +454,11 @@
     (most_1, rest_1), *parts = middle(where, in_1, up_second, down_first, 1, scale, sizes, False)
     mid_1 = middle_sums(parts, "mid1", mid_0)
     leaving_0 = mid_0.add(lead)
-    both_0, most_1, *_ = together(both_0, most_1, *leaving_0)
+    mid_0.move(leaving_0)
+    both_0, most_1, *got = together(both_0, most_1, *mid_0.got())
+    mid_0.replace(got)
     most_1 = regroup(most_1, "z4")
-    mid_0.move(leaving_0)
     leaving_1 = mid_1.add(lead)
-    got = together(*mid_0.got(), *leaving_1)
-    mid_0.replace(got[:2])
-    leaving_1 = got[2:]
     mid_1.move(leaving_1)
     most_1, rest_1, *_ = together(most_1, rest_1, *leaving_1)
     rest_1 = regroup(rest_1, "z5")

time: 216 us -> 215 us (level)
    all_to_all x5, waiting for transfers between devices: 54.6 us -> 50.5 us  [regroup(): lax.all_to_all(pieces, 'tensor', split_axis=0, concat_axis=0, tiled=True)]
    ppermute x24, waiting for transfers between devices: 27.3 us -> 30.8 us  [swap(): return lax.ppermute(value, 'dp', [(s, s ^ 1 << bit) for s in range(count)])]
    unnamed x32 -> x28, local copies, waits for them, and re-layouts: 5.34 us -> 3.76 us
  transfers between devices with their start and end apart: 29 -> 29, of which waited for: 17 -> 15; matrix products, arithmetic and copies ran while one was open for 0% -> 0% of each run, Pallas kernels for 35% -> 36%
where the time goes in v6:
time: 215 us; the launch traced here: 214 us
  Pallas kernels  83.4 us (39%)
  waiting for transfers between devices  81.3 us (38%)
  starting transfers between devices  44.8 us (21%)
  local copies, waits for them, and re-layouts  3.76 us (2%)
    all_to_all x5, waiting for transfers between devices, regroup(): lax.all_to_all(pieces, 'tensor', split_axis=0, concat_axis=0, tiled=True)  50.5 us
    pallas_call x2, Pallas kernels, middle(): pl.pallas_call(kernel, name='middle', grid_spec=pltpu.PrefetchScalarGridS...  38.1 us
    ppermute x24, waiting for transfers between devices, swap(): return lax.ppermute(value, 'dp', [(s, s ^ 1 << bit) for s in range(count)])  30.8 us
    all_to_all x5, starting transfers between devices, regroup(): lax.all_to_all(pieces, 'tensor', split_axis=0, concat_axis=0, tiled=True)  24.5 us
    ppermute x24, starting transfers between devices, swap(): return lax.ppermute(value, 'dp', [(s, s ^ 1 << bit) for s in range(count)])  20.3 us
    pallas_call x2, Pallas kernels, split(): pl.pallas_call(kernel, name='split', grid_spec=pltpu.PrefetchScalarGridSp...  12.8 us
    pallas_call x2, Pallas kernels, leave(): pl.pallas_call(kernel, name='leave_back' if backward else 'leave_out', gr...  11.8 us
    pallas_call x6, Pallas kernels, split_small(): pl.pallas_call(kernel, name='small', in_specs=[pl.BlockSpec(memory_space=...  6.47 us
  transfers between devices with their start and end apart: 29, of which 15 were waited for; matrix products, arithmetic and copies ran while one was open for 0% of the time, Pallas kernels for 36%

profile of v6, /device:TPU:0, one launch (start us, length us, event | category | flops | bytes accessed | tf_op | source)
XLA Modules:
  0.0 214.1 jit_solution(9641122819342090626)
XLA Ops:
  0.6 6.3 %enter.1 = (bf16[4,2,2,4,32,384]{5,4,3,2,1,0:T(8,128)(2,1)}, bf16[4,2,2,4,32,384]{5,4,3,2,1,0:T(8,128)(2,1)}) custom-call(bf16[384,2048]{1,0:T(8,128)(2,1)} %refs_4_.1, bf16[4,512,512]{2,1,0:T(8,128)(2,1)} %refs_2_.5, bf16[384,2048]{1,0:T(8,128)(2,1)} %refs_5_.1, bf16[4,512,512]{2,1,0:T(8,128)(2,1)} %refs_3_.3), custom_call_target="tpu_custom_call" | custom-call | tf_op jit(solution)/shard_map/enter/pallas_call | solution.py:59
  7.0 6.3 %all-to-all-start = ((bf16[4,2,2,4,32,384]{5,4,3,2,1,0:T(8,128)(2,1)}), bf16[4,2,2,4,32,384]{5,4,3,2,1,0:T(8,128)(2,1)S(1)}, u32[]{:S(2)}, u32[]{:S(2)}) async-start(bf16[4,2,2,4,32,384]{5,4,3,2,1,0:T(8,128)(2,1)} %get-tuple-element.87), calls=%async_computation | async-start | bytes 3145728 | tf_op jit(solution)/shard_map/z1/all_to_all | solution.py:249
  13.3 3.8 %turn.1.refs_4_ = bf16[4,4,2,64,384]{4,3,2,1,0:T(8,128)(2,1)} custom-call(bf16[384,2048]{1,0:T(8,128)(2,1)} %refs_4_.1), custom_call_target="tpu_custom_call" | custom-call | tf_op jit(solution)/shard_map/turn/pallas_call | solution.py:79
  17.1 33.1 %all-to-all-done.refs_0_ = bf16[4,2,2,4,32,384]{5,4,3,2,1,0:T(8,128)(2,1)S(1)} async-done(((bf16[4,2,2,4,32,384]{5,4,3,2,1,0:T(8,128)(2,1)}), bf16[4,2,2,4,32,384]{5,4,3,2,1,0:T(8,128)(2,1)S(1)}, u32[]{:S(2)}, u32[]{:S(2)}) %all-to-all-start) | async-done | bytes 1572896 | tf_op jit(solution)/shard_map/z1/all_to_all | solution.py:249
  50.3 4.4 %all-to-all-start.1 = ((bf16[4,2,2,4,32,384]{5,4,3,2,1,0:T(8,128)(2,1)}), bf16[4,2,2,4,32,384]{5,4,3,2,1,0:T(8,128)(2,1)}, u32[]{:S(2)}, u32[]{:S(2)}) async-start(bf16[4,2,2,4,32,384]{5,4,3,2,1,0:T(8,128)(2,1)} %get-tuple-element.89), calls=%async_computation.1 | async-start | bytes 3145728 | tf_op jit(solution)/shard_map/z2/all_to_all | solution.py:249
  54.6 19.0 %middle.2 = (bf16[4,2,8,32,384]{4,3,2,1,0:T(8,128)(2,1)}, bf16[2,4,64,2048]{3,2,1,0:T(8,128)(2,1)}, bf16[2,4,64,2048]{3,2,1,0:T(8,128)(2,1)}, bf16[2,4,256,512]{3,2,1,0:T(8,128)(2,1)}, bf16[2,4,256,512]{3,2,1,0:T(8,128)(2,1)}) custom-call(s32[1]{0:T(128)} %bitcast.where_ref, bf16[4,2,2,4,32,384]{5,4,3,2,1,0:T(8,128)(2,1)} %copy-done.13, ...), custom_call_target="tpu_custom_call" | custom-call | tf_op jit(solution)/shard_map/middle/pallas_call | solution.py:140
  74.2 6.1 %collective-permute-done.refs_1_.refs_3_ = bf16[2,4,64,2048]{3,2,1,0:T(8,128)(2,1)S(1)} collective-permute-done((bf16[2,4,64,2048]{3,2,1,0:T(8,128)(2,1)}, bf16[2,4,64,2048]{3,2,1,0:T(8,128)(2,1)S(1)}, u32[]{:S(2)}, u32[]{:S(2)}) %collective-permute-start) | collective-permute-done | bytes 2097184 | tf_op jit(solution)/shard_map/mid0_core/ppermute | solution.py:255
  81.7 6.4 %split.2 = (bf16[2,2,64,2048]{3,2,1,0:T(8,128)(2,1)}, bf16[2,2,64,2048]{3,2,1,0:T(8,128)(2,1)}, bf16[2,2,256,512]{3,2,1,0:T(8,128)(2,1)}, bf16[2,2,256,512]{3,2,1,0:T(8,128)(2,1)}) custom-call(s32[2]{0:T(128)S(1)} %pad_add_fusion.which_ref, bf16[2,4,64,2048]{3,2,1,0:T(8,128)(2,1)} %get-tuple-element.92.refs_0_.refs_2_, bf16[2,4,64,2048]{3,2,1,0:T(8,128)(2,1)} %copy-done.12, ...), custom_call_target="tpu_custom_call" | custom-call | tf_op jit(solution)/shard_map/split/pallas_call | solution.py:283
  88.1 1.6 collective-permute-start.2
  89.6 1.5 collective-permute-start.3
  91.2 5.0 %all-to-all-start.2 = ((bf16[4,2,8,32,384]{4,3,2,1,0:T(8,128)(2,1)}), bf16[4,2,8,32,384]{4,3,2,1,0:T(8,128)(2,1)}, u32[]{:S(2)}, u32[]{:S(2)}) async-start(bf16[4,2,8,32,384]{4,3,2,1,0:T(8,128)(2,1)} %get-tuple-element.98), calls=%async_computation.2 | async-start | bytes 3145728 | tf_op jit(solution)/shard_map/z3/all_to_all | solution.py:249
  96.2 19.1 %middle.3 = (bf16[4,2,5,32,384]{4,3,2,1,0:T(8,128)(2,1)}, bf16[4,2,3,32,384]{4,3,2,1,0:T(8,128)(2,1)}, bf16[2,4,64,2048]{3,2,1,0:T(8,128)(2,1)}, bf16[2,4,64,204...) custom-call(s32[1]{0:T(128)} %bitcast.where_ref, ...), custom_call_target="tpu_custom_call" | custom-call | tf_op jit(solution)/shard_map/middle/pallas_call | solution.py:140
  118.1 1.5 collective-permute-start.5
  119.6 11.3 %collective-permute-done.4.refs_1_ = bf16[2,1,64,2048]{3,2,1,0:T(8,128)(2,1)S(1)} collective-permute-done((bf16[2,1,64,2048]{3,2,1,0:T(8,128)(2,1)S(1)}, bf16[2,1,64,2048]{3,2,1,0:T(8,128)(2,1)S(1)}, u32[]{:S(2)}, u32[]{:S(2)}) %collective-permute-start.4) | collective-permute-done | bytes 524320 | tf_op jit(solution)/shard_map/mid0_bit1/ppermute | solution.py:255
  133.0 4.7 %all-to-all-start.3 = ((bf16[4,2,5,32,384]{4,3,2,1,0:T(8,128)(2,1)}), bf16[4,2,5,32,384]{4,3,2,1,0:T(8,128)(2,1)}, u32[]{:S(2)}, u32[]{:S(2)}) async-start(bf16[4,2,5,32,384]{4,3,2,1,0:T(8,128)(2,1)} %get-tuple-element.110), calls=%async_computation.3 | async-start | bytes 1966080 | tf_op jit(solution)/shard_map/z4/all_to_all | solution.py:249
  137.6 6.4 %split.3 = (bf16[2,2,64,2048]{3,2,1,0:T(8,128)(2,1)}, bf16[2,2,64,2048]{3,2,1,0:T(8,128)(2,1)}, bf16[2,2,256,512]{3,2,1,0:T(8,128)(2,1)}, bf16[2,2,256,512]{3,2,1,0:T(8,128)(2,1)}) custom-call(s32[2]{0:T(128)S(1)} %pad_add_fusion.which_ref, bf16[2,4,64,2048]{3,2,1,0:T(8,128)(2,1)} %get-tuple-element.112.refs_0_.refs_2_, ...), custom_call_target="tpu_custom_call" | custom-call | tf_op jit(solution)/shard_map/split/pallas_call | solution.py:283
  144.1 1.3 collective-permute-start.10
  146.4 15.1 %all-to-all-done.3.refs_1_ = bf16[4,2,5,32,384]{4,3,2,1,0:T(8,128)(2,1)} async-done(((bf16[4,2,5,32,384]{4,3,2,1,0:T(8,128)(2,1)}), bf16[4,2,5,32,384]{4,3,2,1,0:T(8,128)(2,1)}, u32[]{:S(2)}, u32[]{:S(2)}) %all-to-all-start.3) | async-done | bytes 983072 | tf_op jit(solution)/shard_map/z4/all_to_all | solution.py:249
  161.6 4.2 %all-to-all-start.4 = ((bf16[4,2,3,32,384]{4,3,2,1,0:T(8,128)(2,1)}), bf16[4,2,3,32,384]{4,3,2,1,0:T(8,128)(2,1)}, u32[]{:S(2)}, u32[]{:S(2)}) async-start(bf16[4,2,3,32,384]{4,3,2,1,0:T(8,128)(2,1)} %get-tuple-element.119), calls=%async_computation.4 | async-start | bytes 1179648 | tf_op jit(solution)/shard_map/z5/all_to_all | solution.py:249
  165.8 5.8 %leave_back.1 = (bf16[384,2048]{1,0:T(8,128)(2,1)}, bf16[4,4,32,512]{3,2,1,0:T(8,128)(2,1)S(1)}, bf16[4,4,32,512]{3,2,1,0:T(8,128)(2,1)S(1)}, bf16[4,4,32,512]{3...) custom-call(s32[1]{0:T(128)} %bitcast.where_ref, bf16[4,2,8,32,384]{4,3,2,1,0:T(8,128)(2,1)} %all-to-all-done.2.refs_0_, ...), custom_call_target="tpu_custom_call" | custom-call | tf_op jit(solution)/shard_map/leave_back/pallas_call | solution.py:219
  172.1 1.9 small.8
  176.4 1.5 collective-permute-start.17
  178.0 1.4 small.7
  179.4 1.8 all-to-all-done.4.refs_2_
  181.2 6.0 %leave_out.1 = (bf16[384,2048]{1,0:T(8,128)(2,1)}, bf16[4,4,32,512]{3,2,1,0:T(8,128)(2,1)S(1)}, bf16[4,4,32,512]{3,2,1,0:T(8,128)(2,1)S(1)}, bf16[4,4,32,512]{3,...) custom-call(s32[1]{0:T(128)} %bitcast.where_ref, bf16[4,2,8,32,384]{4,3,2,1,0:T(8,128)(2,1)} %all-to-all-done.2.refs_0_, ...), custom_call_target="tpu_custom_call" | custom-call | tf_op jit(solution)/shard_map/leave_out/pallas_call | solution.py:219
  187.2 2.5 %collective-permute-done.16.refs_3_ = bf16[2,1,64,2048]{3,2,1,0:T(8,128)(2,1)S(1)} collective-permute-done((bf16[2,1,64,2048]{3,2,1,0:T(8,128)(2,1)}, bf16[2,1,64,2048]{3,2,1,0:T(8,128)(2,1)S(1)}, u32[]{:S(2)}, u32[]{:S(2)}) %collective-permute-start.16) | collective-permute-done | bytes 524320 | tf_op jit(solution)/shard_map/mid1_bit1/ppermute | solution.py:255
  190.7 1.5 collective-permute-start.12
  193.7 1.6 collective-permute-start.20
  195.8 4.3 %collective-permute-done.12.refs_1_ = bf16[4,2,32,512]{3,2,1,0:T(8,128)(2,1)S(1)} collective-permute-done((bf16[4,2,32,512]{3,2,1,0:T(8,128)(2,1)}, bf16[4,2,32,512]{3,2,1,0:T(8,128)(2,1)S(1)}, u32[]{:S(2)}, u32[]{:S(2)}) %collective-permute-start.12) | collective-permute-done | bytes 262176 | tf_op jit(solution)/shard_map/first_bit0/ppermute | solution.py:255
  200.1 1.3 collective-permute-done.13.refs_3_
  203.9 2.4 %finish.4 = (f32[4,64,2048]{2,1,0:T(8,128)}, f32[4,256,512]{2,1,0:T(8,128)}) custom-call(bf16[2,1,64,2048]{3,2,1,0:T(8,128)(2,1)S(1)} %get-tuple-element.148.refs_0_, bf16[2,1,64,2048]{3,2,1,0:T(8,128)(2,1)S(1)} %copy-done.5, bf16[2,1,64,2048]{3,2,1,0:T(8,128)(2,1)S(1)} %copy-done.9, bf16[2,1,64,2048]{3,2,1,0:T(8,128)(2,1)S(1)} %collective-permute-done.16.refs_3_, ...), custom_call_target="tpu_custom_call" | custom-call | tf_op jit(solution)/shard_map/finish/pallas_call | solution.py:363
  210.4 2.4 %collective-permute-done.22.refs_1_ = bf16[4,1,32,512]{3,2,1,0:T(8,128)(2,1)S(1)} collective-permute-done((bf16[4,1,32,512]{3,2,1,0:T(8,128)(2,1)S(1)}, bf16[4,1,32,512]{3,2,1,0:T(8,128)(2,1)S(1)}, u32[]{:S(2)}, u32[]{:S(2)}) %collective-permute-start.22) | collective-permute-done | bytes 131104 | tf_op jit(solution)/shard_map/high_bit1/ppermute | solution.py:255
  (73 shorter events, 21.7 us)
Async XLA Ops:
  7.0 43.3 %all-to-all-start = ((bf16[4,2,2,4,32,384]{5,4,3,2,1,0:T(8,128)(2,1)}), bf16[4,2,2,4,32,384]{5,4,3,2,1,0:T(8,128)(2,1)S(1)}, u32[]{:S(2)}, u32[]{:S(2)}) async-start(bf16[4,2,2,4,32,384]{5,4,3,2,1,0:T(8,128)(2,1)} %get-tuple-element.87), calls=%async_computation | async-start | bytes 3145728 | tf_op jit(solution)/shard_map/z1/all_to_all | solution.py:249
  50.3 40.9 %all-to-all-start.1 = ((bf16[4,2,2,4,32,384]{5,4,3,2,1,0:T(8,128)(2,1)}), bf16[4,2,2,4,32,384]{5,4,3,2,1,0:T(8,128)(2,1)}, u32[]{:S(2)}, u32[]{:S(2)}) async-start(bf16[4,2,2,4,32,384]{5,4,3,2,1,0:T(8,128)(2,1)} %get-tuple-element.89), calls=%async_computation.1 | async-start | bytes 3145728 | tf_op jit(solution)/shard_map/z2/all_to_all | solution.py:249
  73.6 6.7 %collective-permute-start = (bf16[2,4,64,2048]{3,2,1,0:T(8,128)(2,1)}, bf16[2,4,64,2048]{3,2,1,0:T(8,128)(2,1)S(1)}, u32[]{:S(2)}, u32[]{:S(2)}) collective-permute-start(bf16[2,4,64,2048]{3,2,1,0:T(8,128)(2,1)} %get-tuple-element.93), channel_id=1, source_target_pairs={{0,4},{4,0},{8,12},{12,8},{16,20},{20,16},{24,28},{28,24},{1,5},{5... | collective-permute-start | bytes 6291464 | tf_op jit(solution)/shard_map/mid0_core/ppermute | solution.py:255
  73.6 7.5 %collective-permute-start.1 = (bf16[2,4,256,512]{3,2,1,0:T(8,128)(2,1)}, bf16[2,4,256,512]{3,2,1,0:T(8,128)(2,1)}, u32[]{:S(2)}, u32[]{:S(2)}) collective-permute-start(bf16[2,4,256,512]{3,2,1,0:T(8,128)(2,1)} %get-tuple-element.95), channel_id=1, source_target_pairs={{0,4},{4,0},{8,12},{12,8},{16,20},{20,16},{24,28},{28,24},{1,5},{5... | collective-permute-start | bytes 6291464 | tf_op jit(solution)/shard_map/mid0_core/ppermute | solution.py:255
  88.1 27.2 %collective-permute-start.2 = (bf16[2,2,64,2048]{3,2,1,0:T(8,128)(2,1)}, bf16[2,2,64,2048]{3,2,1,0:T(8,128)(2,1)S(1)}, u32[]{:S(2)}, u32[]{:S(2)}) collective-permute-start(bf16[2,2,64,2048]{3,2,1,0:T(8,128)(2,1)} %get-tuple-element.96), channel_id=1, source_target_pairs={{0,8},{4,12},{8,0},{12,4},{16,24},{20,28},{24,16},{28,20},{1,9},{5... | collective-permute-start | bytes 3145736 | tf_op jit(solution)/shard_map/mid0_bit0/ppermute | solution.py:255
  89.6 25.7 %collective-permute-start.3 = (bf16[2,2,256,512]{3,2,1,0:T(8,128)(2,1)}, bf16[2,2,256,512]{3,2,1,0:T(8,128)(2,1)S(1)}, u32[]{:S(2)}, u32[]{:S(2)}) collective-permute-start(bf16[2,2,256,512]{3,2,1,0:T(8,128)(2,1)} %get-tuple-element.97), channel_id=1, source_target_pairs={{0,16},{4,20},{8,24},{12,28},{16,0},{20,4},{24,8},{28,12},{1,17},{... | collective-permute-start | bytes 3145736 | tf_op jit(solution)/shard_map/mid0_bit1/ppermute | solution.py:255
  91.2 41.8 %all-to-all-start.2 = ((bf16[4,2,8,32,384]{4,3,2,1,0:T(8,128)(2,1)}), bf16[4,2,8,32,384]{4,3,2,1,0:T(8,128)(2,1)}, u32[]{:S(2)}, u32[]{:S(2)}) async-start(bf16[4,2,8,32,384]{4,3,2,1,0:T(8,128)(2,1)} %get-tuple-element.98), calls=%async_computation.2 | async-start | bytes 3145728 | tf_op jit(solution)/shard_map/z3/all_to_all | solution.py:249
  96.2 19.8 %copy-start = (bf16[2,2,64,2048]{3,2,1,0:T(8,128)(2,1)S(1)}, bf16[2,2,64,2048]{3,2,1,0:T(8,128)(2,1)}, u32[]{:S(2)}) copy-start(bf16[2,2,64,2048]{3,2,1,0:T(8,128)(2,1)} %get-tuple-element.101.refs_0_) | copy-start | bytes 3145732
  96.2 19.8 %copy-start.1 = (bf16[2,2,256,512]{3,2,1,0:T(8,128)(2,1)S(1)}, bf16[2,2,256,512]{3,2,1,0:T(8,128)(2,1)}, u32[]{:S(2)}) copy-start(bf16[2,2,256,512]{3,2,1,0:T(8,128)(2,1)} %get-tuple-element.105.refs_2_) | copy-start | bytes 3145732
  115.3 22.4 %collective-permute-start.6 = (bf16[2,4,64,2048]{3,2,1,0:T(8,128)(2,1)}, bf16[2,4,64,2048]{3,2,1,0:T(8,128)(2,1)}, u32[]{:S(2)}, u32[]{:S(2)}) collective-permute-start(bf16[2,4,64,2048]{3,2,1,0:T(8,128)(2,1)} %get-tuple-element.113), channel_id=1, source_target_pairs={{0,4},{4,0},{8,12},{12,8},{16,20},{20,16},{24,28},{28,24},{1,5},{5... | collective-permute-start | bytes 6291464 | tf_op jit(solution)/shard_map/mid1_core/ppermute | solution.py:255
  115.4 22.3 %collective-permute-start.7 = (bf16[2,4,256,512]{3,2,1,0:T(8,128)(2,1)}, bf16[2,4,256,512]{3,2,1,0:T(8,128)(2,1)}, u32[]{:S(2)}, u32[]{:S(2)}) collective-permute-start(bf16[2,4,256,512]{3,2,1,0:T(8,128)(2,1)} %get-tuple-element.115), channel_id=1, source_target_pairs={{0,4},{4,0},{8,12},{12,8},{16,20},{20,16},{24,28},{28,24},{1,5},{5... | collective-permute-start | bytes 6291464 | tf_op jit(solution)/shard_map/mid1_core/ppermute | solution.py:255
  117.0 14.0 %collective-permute-start.4 = (bf16[2,1,64,2048]{3,2,1,0:T(8,128)(2,1)S(1)}, bf16[2,1,64,2048]{3,2,1,0:T(8,128)(2,1)S(1)}, u32[]{:S(2)}, u32[]{:S(2)}) collective-permute-start(bf16[2,1,64,2048]{3,2,1,0:T(8,128)(2,1)S(1)} %get-tuple-element.107), channel_id=1, source_target_pairs={{0,16},{4,20},{8,24},{12,28},{16,0},{20,4},{24,8},{28,12},{1,17},{... | collective-permute-start | bytes 1572872 | tf_op jit(solution)/shard_map/mid0_bit1/ppermute | solution.py:255
  118.1 13.6 %collective-permute-start.5 = (bf16[2,1,256,512]{3,2,1,0:T(8,128)(2,1)S(1)}, bf16[2,1,256,512]{3,2,1,0:T(8,128)(2,1)S(1)}, u32[]{:S(2)}, u32[]{:S(2)}) collective-permute-start(bf16[2,1,256,512]{3,2,1,0:T(8,128)(2,1)S(1)} %get-tuple-element.108), channel_id=1, source_target_pairs={{0,8},{4,12},{8,0},{12,4},{16,24},{20,28},{24,16},{28,20},{1,9},{5... | collective-permute-start | bytes 1572872 | tf_op jit(solution)/shard_map/mid0_bit0/ppermute | solution.py:255
  133.0 28.6 %all-to-all-start.3 = ((bf16[4,2,5,32,384]{4,3,2,1,0:T(8,128)(2,1)}), bf16[4,2,5,32,384]{4,3,2,1,0:T(8,128)(2,1)}, u32[]{:S(2)}, u32[]{:S(2)}) async-start(bf16[4,2,5,32,384]{4,3,2,1,0:T(8,128)(2,1)} %get-tuple-element.110), calls=%async_computation.3 | async-start | bytes 1966080 | tf_op jit(solution)/shard_map/z4/all_to_all | solution.py:249
  144.1 28.0 %collective-permute-start.10 = (bf16[2,2,64,2048]{3,2,1,0:T(8,128)(2,1)}, bf16[2,2,64,2048]{3,2,1,0:T(8,128)(2,1)S(1)}, u32[]{:S(2)}, u32[]{:S(2)}) collective-permute-start(bf16[2,2,64,2048]{3,2,1,0:T(8,128)(2,1)} %get-tuple-element.116), channel_id=1, source_target_pairs={{0,8},{4,12},{8,0},{12,4},{16,24},{20,28},{24,16},{28,20},{1,9},{5... | collective-permute-start | bytes 3145736 | tf_op jit(solution)/shard_map/mid1_bit0/ppermute | solution.py:255
  145.4 26.7 %collective-permute-start.11 = (bf16[2,2,256,512]{3,2,1,0:T(8,128)(2,1)}, bf16[2,2,256,512]{3,2,1,0:T(8,128)(2,1)S(1)}, u32[]{:S(2)}, u32[]{:S(2)}) collective-permute-start(bf16[2,2,256,512]{3,2,1,0:T(8,128)(2,1)} %get-tuple-element.117), channel_id=1, source_target_pairs={{0,16},{4,20},{8,24},{12,28},{16,0},{20,4},{24,8},{28,12},{1,17},{... | collective-permute-start | bytes 3145736 | tf_op jit(solution)/shard_map/mid1_bit1/ppermute | solution.py:255
  161.6 19.6 %all-to-all-start.4 = ((bf16[4,2,3,32,384]{4,3,2,1,0:T(8,128)(2,1)}), bf16[4,2,3,32,384]{4,3,2,1,0:T(8,128)(2,1)}, u32[]{:S(2)}, u32[]{:S(2)}) async-start(bf16[4,2,3,32,384]{4,3,2,1,0:T(8,128)(2,1)} %get-tuple-element.119), calls=%async_computation.4 | async-start | bytes 1179648 | tf_op jit(solution)/shard_map/z5/all_to_all | solution.py:249
  171.6 6.4 %collective-permute-start.8 = (bf16[4,4,32,512]{3,2,1,0:T(8,128)(2,1)S(1)}, bf16[4,4,32,512]{3,2,1,0:T(8,128)(2,1)S(1)}, u32[]{:S(2)}, u32[]{:S(2)}) collective-permute-start(bf16[4,4,32,512]{3,2,1,0:T(8,128)(2,1)S(1)} %get-tuple-element.122), channel_id=1, source_target_pairs={{0,4},{4,0},{8,12},{12,8},{16,20},{20,16},{24,28},{28,24},{1,5},{5... | collective-permute-start | bytes 1572872 | tf_op jit(solution)/shard_map/first_core/ppermute | solution.py:255
  171.6 6.4 %collective-permute-start.9 = (bf16[4,4,32,512]{3,2,1,0:T(8,128)(2,1)S(1)}, bf16[4,4,32,512]{3,2,1,0:T(8,128)(2,1)S(1)}, u32[]{:S(2)}, u32[]{:S(2)}) collective-permute-start(bf16[4,4,32,512]{3,2,1,0:T(8,128)(2,1)S(1)} %get-tuple-element.124), channel_id=1, source_target_pairs={{0,4},{4,0},{8,12},{12,8},{16,20},{20,16},{24,28},{28,24},{1,5},{5... | collective-permute-start | bytes 1572872 | tf_op jit(solution)/shard_map/first_core/ppermute | solution.py:255
  175.6 14.0 %collective-permute-start.16 = (bf16[2,1,64,2048]{3,2,1,0:T(8,128)(2,1)}, bf16[2,1,64,2048]{3,2,1,0:T(8,128)(2,1)S(1)}, u32[]{:S(2)}, u32[]{:S(2)}) collective-permute-start(bf16[2,1,64,2048]{3,2,1,0:T(8,128)(2,1)} %get-tuple-element.129), channel_id=1, source_target_pairs={{0,16},{4,20},{8,24},{12,28},{16,0},{20,4},{24,8},{28,12},{1,17},{... | collective-permute-start | bytes 1572872 | tf_op jit(solution)/shard_map/mid1_bit1/ppermute | solution.py:255
  176.4 13.8 %collective-permute-start.17 = (bf16[2,1,256,512]{3,2,1,0:T(8,128)(2,1)}, bf16[2,1,256,512]{3,2,1,0:T(8,128)(2,1)S(1)}, u32[]{:S(2)}, u32[]{:S(2)}) collective-permute-start(bf16[2,1,256,512]{3,2,1,0:T(8,128)(2,1)} %get-tuple-element.130), channel_id=1, source_target_pairs={{0,8},{4,12},{8,0},{12,4},{16,24},{20,28},{24,16},{28,20},{1,9},{5... | collective-permute-start | bytes 1572872 | tf_op jit(solution)/shard_map/mid1_bit0/ppermute | solution.py:255
  187.2 16.8 %copy-start.7 = (bf16[2,1,256,512]{3,2,1,0:T(8,128)(2,1)S(1)}, bf16[2,1,256,512]{3,2,1,0:T(8,128)(2,1)}, u32[]{:S(2)}) copy-start(bf16[2,1,256,512]{3,2,1,0:T(8,128)(2,1)} %copy-done.6) | copy-start | bytes 1572868
  190.2 2.5 %collective-permute-start.18 = (bf16[4,4,32,512]{3,2,1,0:T(8,128)(2,1)S(1)}, bf16[4,4,32,512]{3,2,1,0:T(8,128)(2,1)S(1)}, u32[]{:S(2)}, u32[]{:S(2)}) collective-permute-start(bf16[4,4,32,512]{3,2,1,0:T(8,128)(2,1)S(1)} %get-tuple-element.143), channel_id=1, source_target_pairs={{0,4},{4,0},{8,12},{12,8},{16,20},{20,16},{24,28},{28,24},{1,5},{5... | collective-permute-start | bytes 1572872 | tf_op jit(solution)/shard_map/high_core/ppermute | solution.py:255
  190.2 2.7 %collective-permute-start.19 = (bf16[4,4,32,512]{3,2,1,0:T(8,128)(2,1)S(1)}, bf16[4,4,32,512]{3,2,1,0:T(8,128)(2,1)S(1)}, u32[]{:S(2)}, u32[]{:S(2)}) collective-permute-start(bf16[4,4,32,512]{3,2,1,0:T(8,128)(2,1)S(1)} %get-tuple-element.145), channel_id=1, source_target_pairs={{0,4},{4,0},{8,12},{12,8},{16,20},{20,16},{24,28},{28,24},{1,5},{5... | collective-permute-start | bytes 1572872 | tf_op jit(solution)/shard_map/high_core/ppermute | solution.py:255
  190.7 9.4 %collective-permute-start.12 = (bf16[4,2,32,512]{3,2,1,0:T(8,128)(2,1)}, bf16[4,2,32,512]{3,2,1,0:T(8,128)(2,1)S(1)}, u32[]{:S(2)}, u32[]{:S(2)}) collective-permute-start(bf16[4,2,32,512]{3,2,1,0:T(8,128)(2,1)} %get-tuple-element.125), channel_id=1, source_target_pairs={{0,8},{4,12},{8,0},{12,4},{16,24},{20,28},{24,16},{28,20},{1,9},{5... | collective-permute-start | bytes 786440 | tf_op jit(solution)/shard_map/first_bit0/ppermute | solution.py:255
  192.2 9.2 %collective-permute-start.13 = (bf16[4,2,32,512]{3,2,1,0:T(8,128)(2,1)S(1)}, bf16[4,2,32,512]{3,2,1,0:T(8,128)(2,1)S(1)}, u32[]{:S(2)}, u32[]{:S(2)}) collective-permute-start(bf16[4,2,32,512]{3,2,1,0:T(8,128)(2,1)S(1)} %get-tuple-element.126), channel_id=1, source_target_pairs={{0,16},{4,20},{8,24},{12,28},{16,0},{20,4},{24,8},{28,12},{1,17},{... | collective-permute-start | bytes 786440 | tf_op jit(solution)/shard_map/first_bit1/ppermute | solution.py:255
  193.7 12.6 %collective-permute-start.20 = (bf16[4,2,32,512]{3,2,1,0:T(8,128)(2,1)S(1)}, bf16[4,2,32,512]{3,2,1,0:T(8,128)(2,1)S(1)}, u32[]{:S(2)}, u32[]{:S(2)}) collective-permute-start(bf16[4,2,32,512]{3,2,1,0:T(8,128)(2,1)S(1)} %get-tuple-element.146), channel_id=1, source_target_pairs={{0,8},{4,12},{8,0},{12,4},{16,24},{20,28},{24,16},{28,20},{1,9},{5... | collective-permute-start | bytes 786440 | tf_op jit(solution)/shard_map/high_bit0/ppermute | solution.py:255
  195.2 11.8 %collective-permute-start.21 = (bf16[4,2,32,512]{3,2,1,0:T(8,128)(2,1)S(1)}, bf16[4,2,32,512]{3,2,1,0:T(8,128)(2,1)S(1)}, u32[]{:S(2)}, u32[]{:S(2)}) collective-permute-start(bf16[4,2,32,512]{3,2,1,0:T(8,128)(2,1)S(1)} %get-tuple-element.147), channel_id=1, source_target_pairs={{0,16},{4,20},{8,24},{12,28},{16,0},{20,4},{24,8},{28,12},{1,17},{... | collective-permute-start | bytes 786440 | tf_op jit(solution)/shard_map/high_bit1/ppermute | solution.py:255
  202.1 7.4 %collective-permute-start.14 = (bf16[4,1,32,512]{3,2,1,0:T(8,128)(2,1)S(1)}, bf16[4,1,32,512]{3,2,1,0:T(8,128)(2,1)S(1)}, u32[]{:S(2)}, u32[]{:S(2)}) collective-permute-start(bf16[4,1,32,512]{3,2,1,0:T(8,128)(2,1)S(1)} %get-tuple-element.137), channel_id=1, source_target_pairs={{0,16},{4,20},{8,24},{12,28},{16,0},{20,4},{24,8},{28,12},{1,17},{... | collective-permute-start | bytes 393224 | tf_op jit(solution)/shard_map/first_bit1/ppermute | solution.py:255
  202.7 6.8 %collective-permute-start.15 = (bf16[4,1,32,512]{3,2,1,0:T(8,128)(2,1)S(1)}, bf16[4,1,32,512]{3,2,1,0:T(8,128)(2,1)S(1)}, u32[]{:S(2)}, u32[]{:S(2)}) collective-permute-start(bf16[4,1,32,512]{3,2,1,0:T(8,128)(2,1)S(1)} %get-tuple-element.139), channel_id=1, source_target_pairs={{0,8},{4,12},{8,0},{12,4},{16,24},{20,28},{24,16},{28,20},{1,9},{5... | collective-permute-start | bytes 393224 | tf_op jit(solution)/shard_map/first_bit0/ppermute | solution.py:255
  207.7 5.0 %collective-permute-start.22 = (bf16[4,1,32,512]{3,2,1,0:T(8,128)(2,1)S(1)}, bf16[4,1,32,512]{3,2,1,0:T(8,128)(2,1)S(1)}, u32[]{:S(2)}, u32[]{:S(2)}) collective-permute-start(bf16[4,1,32,512]{3,2,1,0:T(8,128)(2,1)S(1)} %get-tuple-element.165), channel_id=1, source_target_pairs={{0,16},{4,20},{8,24},{12,28},{16,0},{20,4},{24,8},{28,12},{1,17},{... | collective-permute-start | bytes 393224 | tf_op jit(solution)/shard_map/high_bit1/ppermute | solution.py:255
  208.3 5.0 %collective-permute-start.23 = (bf16[4,1,32,512]{3,2,1,0:T(8,128)(2,1)S(1)}, bf16[4,1,32,512]{3,2,1,0:T(8,128)(2,1)S(1)}, u32[]{:S(2)}, u32[]{:S(2)}) collective-permute-start(bf16[4,1,32,512]{3,2,1,0:T(8,128)(2,1)S(1)} %get-tuple-element.167), channel_id=1, source_target_pairs={{0,8},{4,12},{8,0},{12,4},{16,24},{20,28},{24,16},{28,20},{1,9},{5... | collective-permute-start | bytes 393224 | tf_op jit(solution)/shard_map/high_bit0/ppermute | solution.py:255
  (11 other events, 71.9 us)

commit v7 on v6

--- a/solution.py
+++ b/solution.py
@@ -490,7 +490,7 @@
         None,
         cut,
     )
-    waited = (mid_1,)
+    waited = (edge_first, mid_1)
     high[0], high[1], *got = together(*high[:2], *[array for sums in waited for array in sums.got()])
     for sums in waited:
         count = len(sums.got())

time: 215 us -> 217 us (level)
  waiting for transfers between devices: 81.3 us -> 84.3 us
    ppermute x24, waiting for transfers between devices: 30.8 us -> 34.8 us  [swap(): return lax.ppermute(value, 'dp', [(s, s ^ 1 << bit) for s in range(count)])]
  transfers between devices with their start and end apart: 29 -> 29, of which waited for: 15 -> 16; matrix products, arithmetic and copies ran while one was open for 0% -> 0% of each run, Pallas kernels for 36% -> 35%
where the time goes in v7:
time: 217 us; the launch traced here: 216 us
  waiting for transfers between devices  84.3 us (39%)
  Pallas kernels  83.4 us (38%)
  starting transfers between devices  44.7 us (21%)
  local copies, waits for them, and re-layouts  2.97 us (1%)
    all_to_all x5, waiting for transfers between devices, regroup(): lax.all_to_all(pieces, 'tensor', split_axis=0, concat_axis=0, tiled=True)  49.5 us
    pallas_call x2, Pallas kernels, middle(): pl.pallas_call(kernel, name='middle', grid_spec=pltpu.PrefetchScalarGridS...  38.1 us
    ppermute x24, waiting for transfers between devices, swap(): return lax.ppermute(value, 'dp', [(s, s ^ 1 << bit) for s in range(count)])  34.8 us
    all_to_all x5, starting transfers between devices, regroup(): lax.all_to_all(pieces, 'tensor', split_axis=0, concat_axis=0, tiled=True)  24.5 us
    ppermute x24, starting transfers between devices, swap(): return lax.ppermute(value, 'dp', [(s, s ^ 1 << bit) for s in range(count)])  20.2 us
    pallas_call x2, Pallas kernels, split(): pl.pallas_call(kernel, name='split', grid_spec=pltpu.PrefetchScalarGridSp...  12.8 us
    pallas_call x2, Pallas kernels, leave(): pl.pallas_call(kernel, name='leave_back' if backward else 'leave_out', gr...  11.8 us
    pallas_call x6, Pallas kernels, split_small(): pl.pallas_call(kernel, name='small', in_specs=[pl.BlockSpec(memory_space=...  6.47 us
  transfers between devices with their start and end apart: 29, of which 16 were waited for; matrix products, arithmetic and copies ran while one was open for 0% of the time, Pallas kernels for 35%

profile of v7, /device:TPU:0, one launch (start us, length us, event | category | flops | bytes accessed | tf_op | source)
XLA Modules:
  0.0 216.3 jit_solution(15162592457718776317)
XLA Ops:
  0.6 6.3 %enter.1 = (bf16[4,2,2,4,32,384]{5,4,3,2,1,0:T(8,128)(2,1)}, bf16[4,2,2,4,32,384]{5,4,3,2,1,0:T(8,128)(2,1)}) custom-call(bf16[384,2048]{1,0:T(8,128)(2,1)} %refs_4_.1, bf16[4,512,512]{2,1,0:T(8,128)(2,1)} %refs_2_.5, bf16[384,2048]{1,0:T(8,128)(2,1)} %refs_5_.1, bf16[4,512,512]{2,1,0:T(8,128)(2,1)} %refs_3_.3), custom_call_target="tpu_custom_call" | custom-call | tf_op jit(solution)/shard_map/enter/pallas_call | solution.py:59
  7.0 6.3 %all-to-all-start = ((bf16[4,2,2,4,32,384]{5,4,3,2,1,0:T(8,128)(2,1)}), bf16[4,2,2,4,32,384]{5,4,3,2,1,0:T(8,128)(2,1)S(1)}, u32[]{:S(2)}, u32[]{:S(2)}) async-start(bf16[4,2,2,4,32,384]{5,4,3,2,1,0:T(8,128)(2,1)} %get-tuple-element.89), calls=%async_computation | async-start | bytes 3145728 | tf_op jit(solution)/shard_map/z1/all_to_all | solution.py:249
  13.3 3.8 %turn.1.refs_4_ = bf16[4,4,2,64,384]{4,3,2,1,0:T(8,128)(2,1)} custom-call(bf16[384,2048]{1,0:T(8,128)(2,1)} %refs_4_.1), custom_call_target="tpu_custom_call" | custom-call | tf_op jit(solution)/shard_map/turn/pallas_call | solution.py:79
  17.1 33.1 %all-to-all-done.refs_0_ = bf16[4,2,2,4,32,384]{5,4,3,2,1,0:T(8,128)(2,1)S(1)} async-done(((bf16[4,2,2,4,32,384]{5,4,3,2,1,0:T(8,128)(2,1)}), bf16[4,2,2,4,32,384]{5,4,3,2,1,0:T(8,128)(2,1)S(1)}, u32[]{:S(2)}, u32[]{:S(2)}) %all-to-all-start) | async-done | bytes 1572896 | tf_op jit(solution)/shard_map/z1/all_to_all | solution.py:249
  50.3 4.4 %all-to-all-start.1 = ((bf16[4,2,2,4,32,384]{5,4,3,2,1,0:T(8,128)(2,1)}), bf16[4,2,2,4,32,384]{5,4,3,2,1,0:T(8,128)(2,1)}, u32[]{:S(2)}, u32[]{:S(2)}) async-start(bf16[4,2,2,4,32,384]{5,4,3,2,1,0:T(8,128)(2,1)} %get-tuple-element.91), calls=%async_computation.1 | async-start | bytes 3145728 | tf_op jit(solution)/shard_map/z2/all_to_all | solution.py:249
  54.6 19.0 %middle.2 = (bf16[4,2,8,32,384]{4,3,2,1,0:T(8,128)(2,1)}, bf16[2,4,64,2048]{3,2,1,0:T(8,128)(2,1)}, bf16[2,4,64,2048]{3,2,1,0:T(8,128)(2,1)}, bf16[2,4,256,512]{3,2,1,0:T(8,128)(2,1)}, bf16[2,4,256,512]{3,2,1,0:T(8,128)(2,1)}) custom-call(s32[1]{0:T(128)} %bitcast.where_ref, bf16[4,2,2,4,32,384]{5,4,3,2,1,0:T(8,128)(2,1)} %copy-done.13, ...), custom_call_target="tpu_custom_call" | custom-call | tf_op jit(solution)/shard_map/middle/pallas_call | solution.py:140
  74.2 6.1 %collective-permute-done.refs_1_.refs_3_ = bf16[2,4,64,2048]{3,2,1,0:T(8,128)(2,1)S(1)} collective-permute-done((bf16[2,4,64,2048]{3,2,1,0:T(8,128)(2,1)}, bf16[2,4,64,2048]{3,2,1,0:T(8,128)(2,1)S(1)}, u32[]{:S(2)}, u32[]{:S(2)}) %collective-permute-start) | collective-permute-done | bytes 2097184 | tf_op jit(solution)/shard_map/mid0_core/ppermute | solution.py:255
  81.7 6.4 %split.2 = (bf16[2,2,64,2048]{3,2,1,0:T(8,128)(2,1)}, bf16[2,2,64,2048]{3,2,1,0:T(8,128)(2,1)}, bf16[2,2,256,512]{3,2,1,0:T(8,128)(2,1)}, bf16[2,2,256,512]{3,2,1,0:T(8,128)(2,1)}) custom-call(s32[2]{0:T(128)S(1)} %pad_add_fusion.which_ref, bf16[2,4,64,2048]{3,2,1,0:T(8,128)(2,1)} %get-tuple-element.94.refs_0_.refs_2_, bf16[2,4,64,2048]{3,2,1,0:T(8,128)(2,1)} %copy-done.12, ...), custom_call_target="tpu_custom_call" | custom-call | tf_op jit(solution)/shard_map/split/pallas_call | solution.py:283
  88.1 1.6 collective-permute-start.2
  89.6 1.5 collective-permute-start.3
  91.2 5.0 %all-to-all-start.2 = ((bf16[4,2,8,32,384]{4,3,2,1,0:T(8,128)(2,1)}), bf16[4,2,8,32,384]{4,3,2,1,0:T(8,128)(2,1)}, u32[]{:S(2)}, u32[]{:S(2)}) async-start(bf16[4,2,8,32,384]{4,3,2,1,0:T(8,128)(2,1)} %get-tuple-element.100), calls=%async_computation.2 | async-start | bytes 3145728 | tf_op jit(solution)/shard_map/z3/all_to_all | solution.py:249
  96.2 19.1 %middle.3 = (bf16[4,2,5,32,384]{4,3,2,1,0:T(8,128)(2,1)}, bf16[4,2,3,32,384]{4,3,2,1,0:T(8,128)(2,1)}, bf16[2,4,64,2048]{3,2,1,0:T(8,128)(2,1)}, bf16[2,4,64,204...) custom-call(s32[1]{0:T(128)} %bitcast.where_ref, ...), custom_call_target="tpu_custom_call" | custom-call | tf_op jit(solution)/shard_map/middle/pallas_call | solution.py:140
  118.1 1.5 collective-permute-start.5
  119.6 11.3 %collective-permute-done.4.refs_1_ = bf16[2,1,64,2048]{3,2,1,0:T(8,128)(2,1)S(1)} collective-permute-done((bf16[2,1,64,2048]{3,2,1,0:T(8,128)(2,1)S(1)}, bf16[2,1,64,2048]{3,2,1,0:T(8,128)(2,1)S(1)}, u32[]{:S(2)}, u32[]{:S(2)}) %collective-permute-start.4) | collective-permute-done | bytes 524320 | tf_op jit(solution)/shard_map/mid0_bit1/ppermute | solution.py:255
  133.0 4.7 %all-to-all-start.3 = ((bf16[4,2,5,32,384]{4,3,2,1,0:T(8,128)(2,1)}), bf16[4,2,5,32,384]{4,3,2,1,0:T(8,128)(2,1)}, u32[]{:S(2)}, u32[]{:S(2)}) async-start(bf16[4,2,5,32,384]{4,3,2,1,0:T(8,128)(2,1)} %get-tuple-element.112), calls=%async_computation.3 | async-start | bytes 1966080 | tf_op jit(solution)/shard_map/z4/all_to_all | solution.py:249
  137.6 6.4 %split.3 = (bf16[2,2,64,2048]{3,2,1,0:T(8,128)(2,1)}, bf16[2,2,64,2048]{3,2,1,0:T(8,128)(2,1)}, bf16[2,2,256,512]{3,2,1,0:T(8,128)(2,1)}, bf16[2,2,256,512]{3,2,1,0:T(8,128)(2,1)}) custom-call(s32[2]{0:T(128)S(1)} %pad_add_fusion.which_ref, bf16[2,4,64,2048]{3,2,1,0:T(8,128)(2,1)} %get-tuple-element.114.refs_0_.refs_2_, ...), custom_call_target="tpu_custom_call" | custom-call | tf_op jit(solution)/shard_map/split/pallas_call | solution.py:283
  146.4 15.1 %all-to-all-done.3.refs_1_ = bf16[4,2,5,32,384]{4,3,2,1,0:T(8,128)(2,1)} async-done(((bf16[4,2,5,32,384]{4,3,2,1,0:T(8,128)(2,1)}), bf16[4,2,5,32,384]{4,3,2,1,0:T(8,128)(2,1)}, u32[]{:S(2)}, u32[]{:S(2)}) %all-to-all-start.3) | async-done | bytes 983072 | tf_op jit(solution)/shard_map/z4/all_to_all | solution.py:249
  161.6 4.2 %all-to-all-start.4 = ((bf16[4,2,3,32,384]{4,3,2,1,0:T(8,128)(2,1)}), bf16[4,2,3,32,384]{4,3,2,1,0:T(8,128)(2,1)}, u32[]{:S(2)}, u32[]{:S(2)}) async-start(bf16[4,2,3,32,384]{4,3,2,1,0:T(8,128)(2,1)} %get-tuple-element.121), calls=%async_computation.4 | async-start | bytes 1179648 | tf_op jit(solution)/shard_map/z5/all_to_all | solution.py:249
  165.8 5.8 %leave_back.1 = (bf16[384,2048]{1,0:T(8,128)(2,1)}, bf16[4,4,32,512]{3,2,1,0:T(8,128)(2,1)S(1)}, bf16[4,4,32,512]{3,2,1,0:T(8,128)(2,1)S(1)}, bf16[4,4,32,512]{3...) custom-call(s32[1]{0:T(128)} %bitcast.where_ref, bf16[4,2,8,32,384]{4,3,2,1,0:T(8,128)(2,1)} %all-to-all-done.2.refs_0_, ...), custom_call_target="tpu_custom_call" | custom-call | tf_op jit(solution)/shard_map/leave_back/pallas_call | solution.py:219
  172.1 1.9 small.8
  175.7 1.5 collective-permute-start.15
  177.2 1.4 small.7
  181.2 6.0 %leave_out.1 = (bf16[384,2048]{1,0:T(8,128)(2,1)}, bf16[4,4,32,512]{3,2,1,0:T(8,128)(2,1)S(1)}, bf16[4,4,32,512]{3,2,1,0:T(8,128)(2,1)S(1)}, bf16[4,4,32,512]{3,...) custom-call(s32[1]{0:T(128)} %bitcast.where_ref, bf16[4,2,8,32,384]{4,3,2,1,0:T(8,128)(2,1)} %all-to-all-done.2.refs_0_, ...), custom_call_target="tpu_custom_call" | custom-call | tf_op jit(solution)/shard_map/leave_out/pallas_call | solution.py:219
  187.2 2.7 %collective-permute-done.14.refs_3_ = bf16[2,1,64,2048]{3,2,1,0:T(8,128)(2,1)S(1)} collective-permute-done((bf16[2,1,64,2048]{3,2,1,0:T(8,128)(2,1)}, bf16[2,1,64,2048]{3,2,1,0:T(8,128)(2,1)S(1)}, u32[]{:S(2)}, u32[]{:S(2)}) %collective-permute-start.14) | collective-permute-done | bytes 524320 | tf_op jit(solution)/shard_map/mid1_bit1/ppermute | solution.py:255
  190.7 4.3 %collective-permute-done.12.refs_1_ = bf16[4,2,32,512]{3,2,1,0:T(8,128)(2,1)S(1)} collective-permute-done((bf16[4,2,32,512]{3,2,1,0:T(8,128)(2,1)}, bf16[4,2,32,512]{3,2,1,0:T(8,128)(2,1)S(1)}, u32[]{:S(2)}, u32[]{:S(2)}) %collective-permute-start.12) | collective-permute-done | bytes 262176 | tf_op jit(solution)/shard_map/first_bit0/ppermute | solution.py:255
  195.6 1.4 collective-permute-done.18.refs_1_
  198.5 1.6 collective-permute-start.20
  201.3 1.6 collective-permute-start.16
  203.4 2.4 %finish.4 = (f32[4,64,2048]{2,1,0:T(8,128)}, f32[4,256,512]{2,1,0:T(8,128)}) custom-call(bf16[2,1,64,2048]{3,2,1,0:T(8,128)(2,1)S(1)} %get-tuple-element.152.refs_0_, bf16[2,1,64,2048]{3,2,1,0:T(8,128)(2,1)S(1)} %copy-done.5, bf16[2,1,64,2048]{3,2,1,0:T(8,128)(2,1)S(1)} %copy-done.9, bf16[2,1,64,2048]{3,2,1,0:T(8,128)(2,1)S(1)} %collective-permute-done.14.refs_3_, ...), custom_call_target="tpu_custom_call" | custom-call | tf_op jit(solution)/shard_map/finish/pallas_call | solution.py:363
  205.7 2.0 collective-permute-done.20.refs_1_
  207.7 1.6 collective-permute-done.21.refs_3_
  212.6 2.4 %collective-permute-done.22.refs_1_ = bf16[4,1,32,512]{3,2,1,0:T(8,128)(2,1)S(1)} collective-permute-done((bf16[4,1,32,512]{3,2,1,0:T(8,128)(2,1)S(1)}, bf16[4,1,32,512]{3,2,1,0:T(8,128)(2,1)S(1)}, u32[]{:S(2)}, u32[]{:S(2)}) %collective-permute-start.22) | collective-permute-done | bytes 131104 | tf_op jit(solution)/shard_map/high_bit1/ppermute | solution.py:255
  (73 shorter events, 23.2 us)
Async XLA Ops:
  7.0 43.3 %all-to-all-start = ((bf16[4,2,2,4,32,384]{5,4,3,2,1,0:T(8,128)(2,1)}), bf16[4,2,2,4,32,384]{5,4,3,2,1,0:T(8,128)(2,1)S(1)}, u32[]{:S(2)}, u32[]{:S(2)}) async-start(bf16[4,2,2,4,32,384]{5,4,3,2,1,0:T(8,128)(2,1)} %get-tuple-element.89), calls=%async_computation | async-start | bytes 3145728 | tf_op jit(solution)/shard_map/z1/all_to_all | solution.py:249
  50.3 40.9 %all-to-all-start.1 = ((bf16[4,2,2,4,32,384]{5,4,3,2,1,0:T(8,128)(2,1)}), bf16[4,2,2,4,32,384]{5,4,3,2,1,0:T(8,128)(2,1)}, u32[]{:S(2)}, u32[]{:S(2)}) async-start(bf16[4,2,2,4,32,384]{5,4,3,2,1,0:T(8,128)(2,1)} %get-tuple-element.91), calls=%async_computation.1 | async-start | bytes 3145728 | tf_op jit(solution)/shard_map/z2/all_to_all | solution.py:249
  73.6 6.7 %collective-permute-start = (bf16[2,4,64,2048]{3,2,1,0:T(8,128)(2,1)}, bf16[2,4,64,2048]{3,2,1,0:T(8,128)(2,1)S(1)}, u32[]{:S(2)}, u32[]{:S(2)}) collective-permute-start(bf16[2,4,64,2048]{3,2,1,0:T(8,128)(2,1)} %get-tuple-element.95), channel_id=1, source_target_pairs={{0,4},{4,0},{8,12},{12,8},{16,20},{20,16},{24,28},{28,24},{1,5},{5... | collective-permute-start | bytes 6291464 | tf_op jit(solution)/shard_map/mid0_core/ppermute | solution.py:255
  73.6 7.5 %collective-permute-start.1 = (bf16[2,4,256,512]{3,2,1,0:T(8,128)(2,1)}, bf16[2,4,256,512]{3,2,1,0:T(8,128)(2,1)}, u32[]{:S(2)}, u32[]{:S(2)}) collective-permute-start(bf16[2,4,256,512]{3,2,1,0:T(8,128)(2,1)} %get-tuple-element.97), channel_id=1, source_target_pairs={{0,4},{4,0},{8,12},{12,8},{16,20},{20,16},{24,28},{28,24},{1,5},{5... | collective-permute-start | bytes 6291464 | tf_op jit(solution)/shard_map/mid0_core/ppermute | solution.py:255
  88.1 27.2 %collective-permute-start.2 = (bf16[2,2,64,2048]{3,2,1,0:T(8,128)(2,1)}, bf16[2,2,64,2048]{3,2,1,0:T(8,128)(2,1)S(1)}, u32[]{:S(2)}, u32[]{:S(2)}) collective-permute-start(bf16[2,2,64,2048]{3,2,1,0:T(8,128)(2,1)} %get-tuple-element.98), channel_id=1, source_target_pairs={{0,8},{4,12},{8,0},{12,4},{16,24},{20,28},{24,16},{28,20},{1,9},{5... | collective-permute-start | bytes 3145736 | tf_op jit(solution)/shard_map/mid0_bit0/ppermute | solution.py:255
  89.6 25.7 %collective-permute-start.3 = (bf16[2,2,256,512]{3,2,1,0:T(8,128)(2,1)}, bf16[2,2,256,512]{3,2,1,0:T(8,128)(2,1)S(1)}, u32[]{:S(2)}, u32[]{:S(2)}) collective-permute-start(bf16[2,2,256,512]{3,2,1,0:T(8,128)(2,1)} %get-tuple-element.99), channel_id=1, source_target_pairs={{0,16},{4,20},{8,24},{12,28},{16,0},{20,4},{24,8},{28,12},{1,17},{... | collective-permute-start | bytes 3145736 | tf_op jit(solution)/shard_map/mid0_bit1/ppermute | solution.py:255
  91.2 41.8 %all-to-all-start.2 = ((bf16[4,2,8,32,384]{4,3,2,1,0:T(8,128)(2,1)}), bf16[4,2,8,32,384]{4,3,2,1,0:T(8,128)(2,1)}, u32[]{:S(2)}, u32[]{:S(2)}) async-start(bf16[4,2,8,32,384]{4,3,2,1,0:T(8,128)(2,1)} %get-tuple-element.100), calls=%async_computation.2 | async-start | bytes 3145728 | tf_op jit(solution)/shard_map/z3/all_to_all | solution.py:249
  96.2 19.8 %copy-start = (bf16[2,2,64,2048]{3,2,1,0:T(8,128)(2,1)S(1)}, bf16[2,2,64,2048]{3,2,1,0:T(8,128)(2,1)}, u32[]{:S(2)}) copy-start(bf16[2,2,64,2048]{3,2,1,0:T(8,128)(2,1)} %get-tuple-element.103.refs_0_) | copy-start | bytes 3145732
  96.2 19.8 %copy-start.1 = (bf16[2,2,256,512]{3,2,1,0:T(8,128)(2,1)S(1)}, bf16[2,2,256,512]{3,2,1,0:T(8,128)(2,1)}, u32[]{:S(2)}) copy-start(bf16[2,2,256,512]{3,2,1,0:T(8,128)(2,1)} %get-tuple-element.107.refs_2_) | copy-start | bytes 3145732
  115.3 22.4 %collective-permute-start.6 = (bf16[2,4,64,2048]{3,2,1,0:T(8,128)(2,1)}, bf16[2,4,64,2048]{3,2,1,0:T(8,128)(2,1)}, u32[]{:S(2)}, u32[]{:S(2)}) collective-permute-start(bf16[2,4,64,2048]{3,2,1,0:T(8,128)(2,1)} %get-tuple-element.115), channel_id=1, source_target_pairs={{0,4},{4,0},{8,12},{12,8},{16,20},{20,16},{24,28},{28,24},{1,5},{5... | collective-permute-start | bytes 6291464 | tf_op jit(solution)/shard_map/mid1_core/ppermute | solution.py:255
  115.4 22.3 %collective-permute-start.7 = (bf16[2,4,256,512]{3,2,1,0:T(8,128)(2,1)}, bf16[2,4,256,512]{3,2,1,0:T(8,128)(2,1)}, u32[]{:S(2)}, u32[]{:S(2)}) collective-permute-start(bf16[2,4,256,512]{3,2,1,0:T(8,128)(2,1)} %get-tuple-element.117), channel_id=1, source_target_pairs={{0,4},{4,0},{8,12},{12,8},{16,20},{20,16},{24,28},{28,24},{1,5},{5... | collective-permute-start | bytes 6291464 | tf_op jit(solution)/shard_map/mid1_core/ppermute | solution.py:255
  117.0 14.0 %collective-permute-start.4 = (bf16[2,1,64,2048]{3,2,1,0:T(8,128)(2,1)S(1)}, bf16[2,1,64,2048]{3,2,1,0:T(8,128)(2,1)S(1)}, u32[]{:S(2)}, u32[]{:S(2)}) collective-permute-start(bf16[2,1,64,2048]{3,2,1,0:T(8,128)(2,1)S(1)} %get-tuple-element.109), channel_id=1, source_target_pairs={{0,16},{4,20},{8,24},{12,28},{16,0},{20,4},{24,8},{28,12},{1,17},{... | collective-permute-start | bytes 1572872 | tf_op jit(solution)/shard_map/mid0_bit1/ppermute | solution.py:255
  118.1 13.6 %collective-permute-start.5 = (bf16[2,1,256,512]{3,2,1,0:T(8,128)(2,1)S(1)}, bf16[2,1,256,512]{3,2,1,0:T(8,128)(2,1)S(1)}, u32[]{:S(2)}, u32[]{:S(2)}) collective-permute-start(bf16[2,1,256,512]{3,2,1,0:T(8,128)(2,1)S(1)} %get-tuple-element.110), channel_id=1, source_target_pairs={{0,8},{4,12},{8,0},{12,4},{16,24},{20,28},{24,16},{28,20},{1,9},{5... | collective-permute-start | bytes 1572872 | tf_op jit(solution)/shard_map/mid0_bit0/ppermute | solution.py:255
  133.0 28.6 %all-to-all-start.3 = ((bf16[4,2,5,32,384]{4,3,2,1,0:T(8,128)(2,1)}), bf16[4,2,5,32,384]{4,3,2,1,0:T(8,128)(2,1)}, u32[]{:S(2)}, u32[]{:S(2)}) async-start(bf16[4,2,5,32,384]{4,3,2,1,0:T(8,128)(2,1)} %get-tuple-element.112), calls=%async_computation.3 | async-start | bytes 1966080 | tf_op jit(solution)/shard_map/z4/all_to_all | solution.py:249
  144.1 28.0 %collective-permute-start.10 = (bf16[2,2,64,2048]{3,2,1,0:T(8,128)(2,1)}, bf16[2,2,64,2048]{3,2,1,0:T(8,128)(2,1)S(1)}, u32[]{:S(2)}, u32[]{:S(2)}) collective-permute-start(bf16[2,2,64,2048]{3,2,1,0:T(8,128)(2,1)} %get-tuple-element.118), channel_id=1, source_target_pairs={{0,8},{4,12},{8,0},{12,4},{16,24},{20,28},{24,16},{28,20},{1,9},{5... | collective-permute-start | bytes 3145736 | tf_op jit(solution)/shard_map/mid1_bit0/ppermute | solution.py:255
  145.4 26.7 %collective-permute-start.11 = (bf16[2,2,256,512]{3,2,1,0:T(8,128)(2,1)}, bf16[2,2,256,512]{3,2,1,0:T(8,128)(2,1)S(1)}, u32[]{:S(2)}, u32[]{:S(2)}) collective-permute-start(bf16[2,2,256,512]{3,2,1,0:T(8,128)(2,1)} %get-tuple-element.119), channel_id=1, source_target_pairs={{0,16},{4,20},{8,24},{12,28},{16,0},{20,4},{24,8},{28,12},{1,17},{... | collective-permute-start | bytes 3145736 | tf_op jit(solution)/shard_map/mid1_bit1/ppermute | solution.py:255
  161.6 19.6 %all-to-all-start.4 = ((bf16[4,2,3,32,384]{4,3,2,1,0:T(8,128)(2,1)}), bf16[4,2,3,32,384]{4,3,2,1,0:T(8,128)(2,1)}, u32[]{:S(2)}, u32[]{:S(2)}) async-start(bf16[4,2,3,32,384]{4,3,2,1,0:T(8,128)(2,1)} %get-tuple-element.121), calls=%async_computation.4 | async-start | bytes 1179648 | tf_op jit(solution)/shard_map/z5/all_to_all | solution.py:249
  171.6 5.6 %collective-permute-start.8 = (bf16[4,4,32,512]{3,2,1,0:T(8,128)(2,1)S(1)}, bf16[4,4,32,512]{3,2,1,0:T(8,128)(2,1)S(1)}, u32[]{:S(2)}, u32[]{:S(2)}) collective-permute-start(bf16[4,4,32,512]{3,2,1,0:T(8,128)(2,1)S(1)} %get-tuple-element.124), channel_id=1, source_target_pairs={{0,4},{4,0},{8,12},{12,8},{16,20},{20,16},{24,28},{28,24},{1,5},{5... | collective-permute-start | bytes 1572872 | tf_op jit(solution)/shard_map/first_core/ppermute | solution.py:255
  171.6 5.6 %collective-permute-start.9 = (bf16[4,4,32,512]{3,2,1,0:T(8,128)(2,1)S(1)}, bf16[4,4,32,512]{3,2,1,0:T(8,128)(2,1)S(1)}, u32[]{:S(2)}, u32[]{:S(2)}) collective-permute-start(bf16[4,4,32,512]{3,2,1,0:T(8,128)(2,1)S(1)} %get-tuple-element.126), channel_id=1, source_target_pairs={{0,4},{4,0},{8,12},{12,8},{16,20},{20,16},{24,28},{28,24},{1,5},{5... | collective-permute-start | bytes 1572872 | tf_op jit(solution)/shard_map/first_core/ppermute | solution.py:255
  174.8 15.0 %collective-permute-start.14 = (bf16[2,1,64,2048]{3,2,1,0:T(8,128)(2,1)}, bf16[2,1,64,2048]{3,2,1,0:T(8,128)(2,1)S(1)}, u32[]{:S(2)}, u32[]{:S(2)}) collective-permute-start(bf16[2,1,64,2048]{3,2,1,0:T(8,128)(2,1)} %get-tuple-element.131), channel_id=1, source_target_pairs={{0,16},{4,20},{8,24},{12,28},{16,0},{20,4},{24,8},{28,12},{1,17},{... | collective-permute-start | bytes 1572872 | tf_op jit(solution)/shard_map/mid1_bit1/ppermute | solution.py:255
  175.7 15.0 %collective-permute-start.15 = (bf16[2,1,256,512]{3,2,1,0:T(8,128)(2,1)}, bf16[2,1,256,512]{3,2,1,0:T(8,128)(2,1)S(1)}, u32[]{:S(2)}, u32[]{:S(2)}) collective-permute-start(bf16[2,1,256,512]{3,2,1,0:T(8,128)(2,1)} %get-tuple-element.132), channel_id=1, source_target_pairs={{0,8},{4,12},{8,0},{12,4},{16,24},{20,28},{24,16},{28,20},{1,9},{5... | collective-permute-start | bytes 1572872 | tf_op jit(solution)/shard_map/mid1_bit0/ppermute | solution.py:255
  178.6 16.4 %collective-permute-start.12 = (bf16[4,2,32,512]{3,2,1,0:T(8,128)(2,1)}, bf16[4,2,32,512]{3,2,1,0:T(8,128)(2,1)S(1)}, u32[]{:S(2)}, u32[]{:S(2)}) collective-permute-start(bf16[4,2,32,512]{3,2,1,0:T(8,128)(2,1)} %get-tuple-element.127), channel_id=1, source_target_pairs={{0,8},{4,12},{8,0},{12,4},{16,24},{20,28},{24,16},{28,20},{1,9},{5... | collective-permute-start | bytes 786440 | tf_op jit(solution)/shard_map/first_bit0/ppermute | solution.py:255
  179.1 15.9 %collective-permute-start.13 = (bf16[4,2,32,512]{3,2,1,0:T(8,128)(2,1)S(1)}, bf16[4,2,32,512]{3,2,1,0:T(8,128)(2,1)S(1)}, u32[]{:S(2)}, u32[]{:S(2)}) collective-permute-start(bf16[4,2,32,512]{3,2,1,0:T(8,128)(2,1)S(1)} %get-tuple-element.128), channel_id=1, source_target_pairs={{0,16},{4,20},{8,24},{12,28},{16,0},{20,4},{24,8},{28,12},{1,17},{... | collective-permute-start | bytes 786440 | tf_op jit(solution)/shard_map/first_bit1/ppermute | solution.py:255
  187.2 16.2 %copy-start.7 = (bf16[2,1,256,512]{3,2,1,0:T(8,128)(2,1)S(1)}, bf16[2,1,256,512]{3,2,1,0:T(8,128)(2,1)}, u32[]{:S(2)}) copy-start(bf16[2,1,256,512]{3,2,1,0:T(8,128)(2,1)} %copy-done.6) | copy-start | bytes 1572868
  195.0 1.9 collective-permute-start.18
  195.0 2.7 %collective-permute-start.19 = (bf16[4,4,32,512]{3,2,1,0:T(8,128)(2,1)S(1)}, bf16[4,4,32,512]{3,2,1,0:T(8,128)(2,1)S(1)}, u32[]{:S(2)}, u32[]{:S(2)}) collective-permute-start(bf16[4,4,32,512]{3,2,1,0:T(8,128)(2,1)S(1)} %get-tuple-element.149), channel_id=1, source_target_pairs={{0,4},{4,0},{8,12},{12,8},{16,20},{20,16},{24,28},{28,24},{1,5},{5... | collective-permute-start | bytes 1572872 | tf_op jit(solution)/shard_map/high_core/ppermute | solution.py:255
  198.5 9.2 %collective-permute-start.20 = (bf16[4,2,32,512]{3,2,1,0:T(8,128)(2,1)S(1)}, bf16[4,2,32,512]{3,2,1,0:T(8,128)(2,1)S(1)}, u32[]{:S(2)}, u32[]{:S(2)}) collective-permute-start(bf16[4,2,32,512]{3,2,1,0:T(8,128)(2,1)S(1)} %get-tuple-element.150), channel_id=1, source_target_pairs={{0,8},{4,12},{8,0},{12,4},{16,24},{20,28},{24,16},{28,20},{1,9},{5... | collective-permute-start | bytes 786440 | tf_op jit(solution)/shard_map/high_bit0/ppermute | solution.py:255
  200.1 9.2 %collective-permute-start.21 = (bf16[4,2,32,512]{3,2,1,0:T(8,128)(2,1)S(1)}, bf16[4,2,32,512]{3,2,1,0:T(8,128)(2,1)S(1)}, u32[]{:S(2)}, u32[]{:S(2)}) collective-permute-start(bf16[4,2,32,512]{3,2,1,0:T(8,128)(2,1)S(1)} %get-tuple-element.151), channel_id=1, source_target_pairs={{0,16},{4,20},{8,24},{12,28},{16,0},{20,4},{24,8},{28,12},{1,17},{... | collective-permute-start | bytes 786440 | tf_op jit(solution)/shard_map/high_bit1/ppermute | solution.py:255
  201.3 10.5 %collective-permute-start.16 = (bf16[4,1,32,512]{3,2,1,0:T(8,128)(2,1)S(1)}, bf16[4,1,32,512]{3,2,1,0:T(8,128)(2,1)S(1)}, u32[]{:S(2)}, u32[]{:S(2)}) collective-permute-start(bf16[4,1,32,512]{3,2,1,0:T(8,128)(2,1)S(1)} %get-tuple-element.143), channel_id=1, source_target_pairs={{0,16},{4,20},{8,24},{12,28},{16,0},{20,4},{24,8},{28,12},{1,17},{... | collective-permute-start | bytes 393224 | tf_op jit(solution)/shard_map/first_bit1/ppermute | solution.py:255
  202.8 8.9 %collective-permute-start.17 = (bf16[4,1,32,512]{3,2,1,0:T(8,128)(2,1)S(1)}, bf16[4,1,32,512]{3,2,1,0:T(8,128)(2,1)S(1)}, u32[]{:S(2)}, u32[]{:S(2)}) collective-permute-start(bf16[4,1,32,512]{3,2,1,0:T(8,128)(2,1)S(1)} %get-tuple-element.145), channel_id=1, source_target_pairs={{0,8},{4,12},{8,0},{12,4},{16,24},{20,28},{24,16},{28,20},{1,9},{5... | collective-permute-start | bytes 393224 | tf_op jit(solution)/shard_map/first_bit0/ppermute | solution.py:255
  209.9 5.0 %collective-permute-start.22 = (bf16[4,1,32,512]{3,2,1,0:T(8,128)(2,1)S(1)}, bf16[4,1,32,512]{3,2,1,0:T(8,128)(2,1)S(1)}, u32[]{:S(2)}, u32[]{:S(2)}) collective-permute-start(bf16[4,1,32,512]{3,2,1,0:T(8,128)(2,1)S(1)} %get-tuple-element.169), channel_id=1, source_target_pairs={{0,16},{4,20},{8,24},{12,28},{16,0},{20,4},{24,8},{28,12},{1,17},{... | collective-permute-start | bytes 393224 | tf_op jit(solution)/shard_map/high_bit1/ppermute | solution.py:255
  210.5 5.0 %collective-permute-start.23 = (bf16[4,1,32,512]{3,2,1,0:T(8,128)(2,1)S(1)}, bf16[4,1,32,512]{3,2,1,0:T(8,128)(2,1)S(1)}, u32[]{:S(2)}, u32[]{:S(2)}) collective-permute-start(bf16[4,1,32,512]{3,2,1,0:T(8,128)(2,1)S(1)} %get-tuple-element.171), channel_id=1, source_target_pairs={{0,8},{4,12},{8,0},{12,4},{16,24},{20,28},{24,16},{28,20},{1,9},{5... | collective-permute-start | bytes 393224 | tf_op jit(solution)/shard_map/high_bit0/ppermute | solution.py:255
  (11 other events, 73.2 us)
